TPU v7x, 128 devices: a whole 4x4x4 slice. The times are simulated.
128 devices in a mesh: wide: 8 (over y, z_hi), narrow: 16 (over z_lo, x, core).
Axes of the slice: x: 4, y: 4, z: 4 (z_hi: 2, z_lo: 2; z = z_hi * 2 + z_lo), core: 2. Of those that a mesh axis runs over, the one named last changes fastest.
Arguments:
- hidden_pre: bfloat16 [32, 256, 256, 256], P(None, 'wide', 'narrow'), may hold values from -6 to 6
- cotangent: bfloat16 [32, 256, 256, 256], P(None, 'wide', 'narrow'), may hold values from -6 to 6
- mode_weight: bfloat16 [32, 32, 32, 1024], P('narrow', 'wide'), may hold values from -6 to 6
- skip_weight: bfloat16 [32, 32], replicated, may hold values from -1 to 1
Outputs:
- grad_hidden: bfloat16 [32, 256, 256, 256], P(None, 'wide', 'narrow')
- grad_modes: float32 [32, 32, 32, 1024], P('narrow', 'wide')
- grad_skip: float32 [32, 32], replicated
All inputs are finite; a program needn't handle non-finite values.
Results may differ from a plain program's by a relative error of at most 0.0087.
Values may be sent and summed in bfloat16 or wider, within the bound.
A program may use at most 128 MiB of HBM per device.

v0:
```python
import math

import jax
import jax.numpy as jnp
from jax import lax
from jax.experimental import pallas as pl
from jax.experimental.pallas import tpu as pltpu
from jax.sharding import PartitionSpec as P

NX = 256
NY = 256
NZ = 256
XB = 8


def basis_table(mode_count, length):
    mode_index = jnp.arange(mode_count, dtype=jnp.int32)
    halfway = mode_count // 2
    frequency = jnp.where(mode_index < halfway, mode_index, mode_index - halfway + 1)
    points = jnp.arange(length, dtype=jnp.int32)
    phases = frequency[:, None] * points[None, :] % length
    angles = phases.astype(jnp.float32) * (2.0 * math.pi / length)
    values_table = jnp.where((mode_index < halfway)[:, None], jnp.cos(angles), jnp.sin(angles))
    return (values_table * (1.0 / math.sqrt(length))).astype(jnp.bfloat16)


def _nt(a, b):
    return lax.dot_general(a, b, (((1,), (1,)), ((), ())), preferred_element_type=jnp.float32)


def analysis_kernel(h_ref, g_ref, tz_ref, zc_ref, gram_ref, acc_ref):
    step = pl.program_id(0)
    channels, xb, ny, nz = h_ref.shape

    @pl.when(step == 0)
    def _():
        acc_ref[...] = jnp.zeros_like(acc_ref)

    tz = tz_ref[...]
    li = jnp.tanh(h_ref[...].astype(jnp.float32)).astype(jnp.bfloat16)
    g = g_ref[...]
    width = xb * ny
    zl = _nt(tz, li.reshape(channels * width, nz))
    zg = _nt(tz, g.reshape(channels * width, nz))
    for c in range(channels):
        zc_ref[c] = zl[:, c * width:(c + 1) * width].astype(jnp.bfloat16)
        zc_ref[channels + c] = zg[:, c * width:(c + 1) * width].astype(jnp.bfloat16)
    for x in range(xb):
        acc_ref[...] += _nt(li[:, x].reshape(channels * ny, nz), g[:, x].reshape(channels * ny, nz))

    @pl.when(step == pl.num_programs(0) - 1)
    def _():
        gram_ref[...] = acc_ref[...]


def analysis(hidden_pre, cotangent, table_z):
    channels, nx, ny, nz = hidden_pre.shape
    modes = table_z.shape[0]
    steps = nx // XB
    field_spec = pl.BlockSpec((channels, XB, ny, nz), lambda i: (0, i, 0, 0))
    return pl.pallas_call(
        analysis_kernel,
        grid=(steps,),
        in_specs=[field_spec, field_spec, pl.BlockSpec((modes, nz), lambda i: (0, 0))],
        out_specs=[
            pl.BlockSpec((2 * channels, modes, XB * ny), lambda i: (0, 0, i)),
            pl.BlockSpec((channels * ny, channels * ny), lambda i: (0, 0)),
        ],
        out_shape=[
            jax.ShapeDtypeStruct((2 * channels, modes, nx * ny), jnp.bfloat16),
            jax.ShapeDtypeStruct((channels * ny, channels * ny), jnp.float32),
        ],
        scratch_shapes=[pltpu.VMEM((channels * ny, channels * ny), jnp.float32)],
        compiler_params=pltpu.CompilerParams(
            dimension_semantics=("arbitrary",), vmem_limit_bytes=60 * 1024 * 1024
        ),
    )(hidden_pre, cotangent, table_z)


def synthesis_kernel(h_ref, g_ref, ys_ref, tz_ref, ks_ref, out_ref):
    channels, xb, ny, nz = h_ref.shape
    tz = tz_ref[...]
    ks = ks_ref[...]
    for x in range(xb):
        spec = jnp.dot(ys_ref[x], tz, preferred_element_type=jnp.float32)
        spec = spec.astype(jnp.bfloat16).astype(jnp.float32)
        skip = jnp.dot(ks, g_ref[:, x].reshape(channels * ny, nz), preferred_element_type=jnp.float32)
        activ = jnp.tanh(h_ref[:, x].astype(jnp.float32)).reshape(channels * ny, nz)
        grad = (spec + skip) * (1.0 - activ * activ)
        out_ref[:, x] = grad.astype(jnp.bfloat16).reshape(channels, ny, nz)


def synthesis(hidden_pre, cotangent, ysynth, table_z, kron_skip):
    channels, nx, ny, nz = hidden_pre.shape
    modes = table_z.shape[0]
    steps = nx // XB
    field_spec = pl.BlockSpec((channels, XB, ny, nz), lambda i: (0, i, 0, 0))
    return pl.pallas_call(
        synthesis_kernel,
        grid=(steps,),
        in_specs=[
            field_spec,
            field_spec,
            pl.BlockSpec((XB, channels * ny, modes), lambda i: (i, 0, 0)),
            pl.BlockSpec((modes, nz), lambda i: (0, 0)),
            pl.BlockSpec((channels * ny, channels * ny), lambda i: (0, 0)),
        ],
        out_specs=field_spec,
        out_shape=jax.ShapeDtypeStruct(hidden_pre.shape, jnp.bfloat16),
        compiler_params=pltpu.CompilerParams(
            dimension_semantics=("arbitrary",), vmem_limit_bytes=60 * 1024 * 1024
        ),
    )(hidden_pre, cotangent, ysynth, table_z, kron_skip)


def per_device(hidden_pre, cotangent, mode_weight, skip_weight):
    highest = lax.Precision.HIGHEST
    channels, nx, ny, nz = hidden_pre.shape
    mode_count = mode_weight.shape[2]
    n_narrow = lax.axis_size("narrow")
    n_wide = lax.axis_size("wide")
    table_x = basis_table(mode_count, NX)
    table_y = basis_table(mode_count, NY)
    table_z = basis_table(mode_count, NZ)

    zc, gram = analysis(hidden_pre, cotangent, table_z)
    zc = zc.reshape(2 * channels, mode_count, nx, ny)
    zc = lax.all_to_all(zc, "narrow", split_axis=1, concat_axis=3, tiled=True)
    ycoeffs = jnp.einsum(
        "cmxy,ny->mcnx", zc, table_y, preferred_element_type=jnp.float32
    ).astype(jnp.bfloat16)
    ycoeffs = lax.all_to_all(ycoeffs, "wide", split_axis=2, concat_axis=3, tiled=True)
    spectra = jnp.einsum("zcyx,kx->zcyk", ycoeffs, table_x, preferred_element_type=jnp.float32)
    s_modes = jnp.transpose(spectra[:, :channels], (0, 2, 3, 1))
    q_modes = jnp.transpose(spectra[:, channels:], (0, 2, 3, 1))
    z_local, y_local = (s_modes.shape[0], s_modes.shape[1])
    grad_modes = (s_modes[..., :, None] * q_modes[..., None, :]).reshape(
        z_local, y_local, mode_count, channels * channels
    )
    weights_five = mode_weight.reshape(z_local, y_local, mode_count, channels, channels).astype(
        jnp.float32
    )
    back_spec = jnp.einsum("zykco,zyko->zcyk", weights_five, q_modes, precision=highest).astype(
        jnp.bfloat16
    )
    xsynth = jnp.einsum(
        "zcyk,kx->zcyx", back_spec, table_x, preferred_element_type=jnp.float32
    ).astype(jnp.bfloat16)
    xsynth = lax.all_to_all(xsynth, "wide", split_axis=3, concat_axis=2, tiled=True)
    ysynth = jnp.einsum(
        "zcnx,ny->xcyz", xsynth, table_y, preferred_element_type=jnp.float32
    ).astype(jnp.bfloat16)
    ysynth = lax.all_to_all(ysynth, "narrow", split_axis=2, concat_axis=3, tiled=True)
    ysynth = ysynth.reshape(nx, channels * ny, mode_count)
    kron_skip = jnp.kron(skip_weight, jnp.eye(ny, dtype=skip_weight.dtype))
    grad_hidden = synthesis(hidden_pre, cotangent, ysynth, table_z, kron_skip)

    diag = jnp.eye(ny, dtype=jnp.float32)
    local_terms = (gram.reshape(channels, ny, channels, ny) * diag[None, :, None, :]).sum((1, 3))
    grad_skip = lax.psum(local_terms, ("wide", "narrow")) * (1.0 / math.sqrt(NX * NY * NZ))
    del n_narrow, n_wide
    return (grad_hidden, grad_modes, grad_skip)


def solution(mesh):
    in_specs = (
        P(None, "wide", "narrow", None),
        P(None, "wide", "narrow", None),
        P("narrow", "wide", None, None),
        P(),
    )
    out_specs = (P(None, "wide", "narrow", None), P("narrow", "wide", None, None), P())
    return jax.shard_map(
        per_device, mesh=mesh, in_specs=in_specs, out_specs=out_specs, check_vma=False
    )
```

profile of v0, /device:TPU:1, one launch (start us, length us, event | category | flops | bytes accessed | tf_op | source)
XLA Modules:
  0.0 250.1 jit_solution(17866723393587144640)
XLA Ops:
  0.7 0.8 multiply_convert_fusion.tz_ref
  1.5 13.7 %shard_map.67 = (bf16[64,32,512]{2,1,0:T(8,128)(2,1)}, f32[512,512]{1,0:T(8,128)}) custom-call(bf16[32,32,16,256]{3,2,1,0:T(8,128)(2,1)} %h_ref.3, bf16[32,32,16,256]{3,2,1,0:T(8,128)(2,1)} %g_ref.3, bf16[32,256]{1,0:T(8,128)(2,1)} %multiply_convert_fusion.tz_ref), custom_call_target="tpu_custom_call" | custom-call | tf_op jit(solution)/shard_map/pallas_call | solution.py:61
  15.2 5.2 %copy.33 = bf16[64,32,512]{0,2,1:T(8,128)(2,1)} copy(bf16[64,32,512]{2,1,0:T(8,128)(2,1)} %get-tuple-element.5) | data formatting | bytes 4194304 | tf_op jit(solution)/shard_map/pallas_call | solution.py:61
  20.3 6.3 %reshape.62 = bf16[16,2,32768]{2,1,0:T(2,128)(2,1)S(1)} reshape(bf16[32,32,16,64]{3,2,1,0:T(8,128)(2,1)} %bitcast.70) | data formatting | bytes 4194304
  26.7 33.8 %all_to_all.69 = bf16[16,2,32768]{2,1,0:T(2,128)(2,1)} all-to-all(bf16[16,2,32768]{2,1,0:T(2,128)(2,1)S(1)} %reshape.62), channel_id=1, replica_groups=mesh['wide'=8,'narrow'=16] {'narrow'}, dimensions={0} | all-to-all | bytes 4194304 | tf_op jit(solution)/shard_map/all_to_all | solution.py:128
  60.5 7.4 %reshape.63 = bf16[32,32,16,64]{3,2,1,0:T(8,128)(2,1)} reshape(bf16[16,2,32768]{2,1,0:T(2,128)(2,1)} %all_to_all.69) | data formatting | bytes 4194304
  67.9 3.4 %copy.34 = bf16[64,16,2,32,16]{0,4,1,3,2:T(8,128)(2,1)S(1)} copy(bf16[64,16,2,32,16]{0,4,3,2,1:T(8,128)(2,1)} %bitcast.73) | data formatting | bytes 4194304 | tf_op jit(solution)/shard_map/all_to_all | solution.py:128
  71.3 0.0 copy-start.1
  71.3 1.0 fusion.1
  72.3 0.2 copy.58
  72.5 1.1 reshape.64
  73.6 7.2 %all-to-all-start.1 = ((bf16[8,2,8192]{2,1,0:T(2,128)(2,1)}), bf16[8,2,8192]{2,1,0:T(2,128)(2,1)S(1)}, u32[]{:S(2)}, u32[]{:S(2)}) async-start(bf16[8,2,8192]{2,1,0:T(2,128)(2,1)} %reshape.64), calls=%async_computation.1 | async-start | bytes 524288 | tf_op jit(solution)/shard_map/all_to_all | solution.py:132
  80.8 0.0 copy-done.1
  80.8 1.6 reshape.56
  82.4 0.0 copy-start.2
  82.4 5.7 %all-to-all-done.1 = bf16[8,2,8192]{2,1,0:T(2,128)(2,1)S(1)} async-done(((bf16[8,2,8192]{2,1,0:T(2,128)(2,1)}), bf16[8,2,8192]{2,1,0:T(2,128)(2,1)S(1)}, u32[]{:S(2)}, u32[]{:S(2)}) %all-to-all-start.1) | async-done | bytes 262176 | tf_op jit(solution)/shard_map/all_to_all | solution.py:132
  88.1 0.3 reshape.65
  88.5 0.3 fusion.13
  88.8 0.1 slice_bitcast_fusion
  88.9 3.4 %fusion.38 = bf16[2,4,32,1,32]{4,3,2,1,0:T(2,128)(2,1)S(1)} fusion(f32[2,4,32,32,1]{3,4,2,1,0:T(1,128)S(1)} %bitcast.81, bf16[2,4,32,32,32]{4,3,2,1,0:T(8,128)(2,1)S(1)} %reshape.56), kind=kOutput, calls=%fused_computation.55 | convolution fusion | flops 3145728 | bytes 573440 | tf_op jit(solution)/shard_map/zykco,zyko->zcyk/dot_general | solution.py:143
  92.3 0.1 copy.51
  92.4 0.4 convolution_convert_fusion.2
  92.8 0.3 copy.39
  93.1 1.2 reshape.66
  94.3 3.5 %all-to-all-start.2 = ((bf16[8,2,4096]{2,1,0:T(2,128)(2,1)}), bf16[8,2,4096]{2,1,0:T(2,128)(2,1)S(1)}, u32[]{:S(2)}, u32[]{:S(2)}) async-start(bf16[8,2,4096]{2,1,0:T(2,128)(2,1)} %reshape.66), calls=%async_computation.2 | async-start | bytes 262144 | tf_op jit(solution)/shard_map/all_to_all | solution.py:149
  97.8 0.0 copy-done.2
  97.8 0.0 copy-start
  97.8 2.4 broadcast_multiply_fusion.1
  100.2 8.4 %mul.150.ks_ref = bf16[512,512]{1,0:T(8,128)(2,1)} reshape(bf16[32,16,32,16]{3,2,1,0:T(8,128)(2,1)} %broadcast_multiply_fusion.1) | data formatting | bytes 1048576 | tf_op jit(solution)/shard_map/jit(kron)/mul | solution.py:155
  108.6 0.0 copy-done
  108.6 4.8 %reshape.58 = f32[32,16,32,16]{3,2,1,0:T(8,128)} reshape(f32[512,512]{1,0:T(8,128)S(1)} %copy-done) | data formatting | bytes 2097152 | tf_op jit(solution)/shard_map/reshape | solution.py:159
  113.4 0.0 all-to-all-done.2
  113.4 0.3 reshape.67
  113.7 0.4 copy.53
  114.1 0.6 fusion
  114.7 6.5 %copy.43 = bf16[32,32,256,2]{0,1,3,2:T(8,128)(2,1)} copy(bf16[32,32,256,2]{2,0,1,3:T(8,128)(2,1)S(1)} %fusion) | data formatting | bytes 2097152 | tf_op jit(solution)/shard_map/convert_element_type | solution.py:152
  121.2 7.4 %reshape.68 = bf16[16,2,16384]{2,1,0:T(2,128)(2,1)} reshape(bf16[256,2,32,32]{3,2,1,0:T(8,128)(2,1)} %bitcast.69) | data formatting | bytes 2097152
  128.6 5.9 %all-to-all-start.3 = ((bf16[16,2,16384]{2,1,0:T(2,128)(2,1)}), bf16[16,2,16384]{2,1,0:T(2,128)(2,1)S(1)}, u32[]{:S(2)}, u32[]{:S(2)}) async-start(bf16[16,2,16384]{2,1,0:T(2,128)(2,1)} %reshape.68), calls=%async_computation.3 | async-start | bytes 2097152 | tf_op jit(solution)/shard_map/all_to_all | solution.py:153
  134.6 4.3 %multiply_reduce_fusion = f32[32,32]{1,0:T(8,128)S(1)} fusion(f32[32,16,32,16]{3,2,1,0:T(8,128)} %reshape.58, f32[16,16]{1,0:T(8,128)S(1)} %fusion.16), kind=kLoop, calls=%fused_computation | loop fusion | flops 523264 | bytes 1053696 | tf_op jit(solution)/shard_map/reduce_sum | solution.py:159
  138.9 67.7 %psum.7 = f32[32,32]{1,0:T(8,128)S(1)} all-reduce(f32[32,32]{1,0:T(8,128)S(1)} %multiply_reduce_fusion), channel_id=1, replica_groups=mesh['wide'=8,'narrow'=16] {'wide','narrow'}, use_global_device_ids=true, to_apply=%region_1.2 | all-reduce | flops 1024 | bytes 8192 | tf_op jit(solution)/shard_map/psum | solution.py:160
  206.6 0.6 broadcast_multiply_fusion.2
  207.2 3.0 %broadcast_multiply_fusion = f32[2,4,32,32,32]{4,3,2,1,0:T(8,128)} fusion(f32[2,4,32,32]{3,2,1,0:T(8,128)S(1)} %get-tuple-element.8, f32[2,4,32,32]{3,2,1,0:T(8,128)S(1)} %get-tuple-element.7), kind=kLoop, calls=%fused_computation.1 | loop fusion | flops 262144 | bytes 1114112 | tf_op jit(solution)/shard_map/mul | solution.py:137
  210.2 4.6 %mul.154 = f32[2,4,32,1024]{3,2,1,0:T(8,128)} reshape(f32[2,4,32,32,32]{4,3,2,1,0:T(8,128)} %broadcast_multiply_fusion) | data formatting | bytes 2097152 | tf_op jit(solution)/shard_map/mul | solution.py:137
  214.8 0.0 all-to-all-done.3
  214.8 3.5 %reshape.69 = bf16[256,2,32,32]{3,2,1,0:T(8,128)(2,1)} reshape(bf16[16,2,16384]{2,1,0:T(2,128)(2,1)S(1)} %all-to-all-done.3) | data formatting | bytes 2097152
  218.3 10.8 %copy.45 = bf16[32,32,16,16,2]{0,2,1,4,3:T(8,128)(2,1)} copy(bf16[32,32,16,16,2]{0,1,4,2,3:T(8,128)(2,1)} %bitcast.72) | data formatting | bytes 2097152 | tf_op jit(solution)/shard_map/all_to_all | solution.py:153
  229.0 7.1 %copy.46.ys_ref = bf16[32,512,32]{2,1,0:T(8,128)(2,1)} copy(bf16[32,512,32]{0,1,2:T(8,128)(2,1)} %bitcast.74) | data formatting | bytes 2097152 | tf_op jit(solution)/shard_map/reshape | solution.py:154
  236.1 14.0 %shard_map.68 = bf16[32,32,16,256]{3,2,1,0:T(8,128)(2,1)} custom-call(bf16[32,32,16,256]{3,2,1,0:T(8,128)(2,1)} %h_ref.3, bf16[32,32,16,256]{3,2,1,0:T(8,128)(2,1)} %g_ref.3, bf16[32,512,32]{2,1,0:T(8,128)(2,1)} %copy.46.ys_ref, bf16[32,256]{1,0:T(8,128)(2,1)} %multiply_convert_fusion.tz_ref, bf16[512,512]{1,0:T(8,128)(2,1)} %mul.150.ks_ref), custom_call_target="tpu_custom_call" | custom-call | tf_op jit(solution)/shard_map/pallas_call | solution.py:98
  (5 shorter events, 0.1 us)
Async XLA Ops:
  71.3 9.5 %copy-start.1 = (bf16[2,4,32,1024]{3,2,1,0:T(8,128)(2,1)S(1)}, bf16[2,4,32,1024]{3,2,1,0:T(8,128)(2,1)}, u32[]{:S(2)}) copy-start(bf16[2,4,32,1024]{3,2,1,0:T(8,128)(2,1)} %param.6) | copy-start | bytes 1572868
  73.6 14.5 %all-to-all-start.1 = ((bf16[8,2,8192]{2,1,0:T(2,128)(2,1)}), bf16[8,2,8192]{2,1,0:T(2,128)(2,1)S(1)}, u32[]{:S(2)}, u32[]{:S(2)}) async-start(bf16[8,2,8192]{2,1,0:T(2,128)(2,1)} %reshape.64), calls=%async_computation.1 | async-start | bytes 524288 | tf_op jit(solution)/shard_map/all_to_all | solution.py:132
  82.4 15.4 %copy-start.2 = (bf16[32,32]{1,0:T(8,128)(2,1)S(1)}, bf16[32,32]{1,0:T(8,128)(2,1)}, u32[]{:S(2)}) copy-start(bf16[32,32]{1,0:T(8,128)(2,1)} %param.7) | copy-start | bytes 6148
  94.3 19.2 %all-to-all-start.2 = ((bf16[8,2,4096]{2,1,0:T(2,128)(2,1)}), bf16[8,2,4096]{2,1,0:T(2,128)(2,1)S(1)}, u32[]{:S(2)}, u32[]{:S(2)}) async-start(bf16[8,2,4096]{2,1,0:T(2,128)(2,1)} %reshape.66), calls=%async_computation.2 | async-start | bytes 262144 | tf_op jit(solution)/shard_map/all_to_all | solution.py:149
  97.8 10.8 %copy-start = (f32[512,512]{1,0:T(8,128)S(1)}, f32[512,512]{1,0:T(8,128)}, u32[]{:S(2)}) copy-start(f32[512,512]{1,0:T(8,128)} %get-tuple-element.6) | copy-start | bytes 3145732
  128.6 86.2 %all-to-all-start.3 = ((bf16[16,2,16384]{2,1,0:T(2,128)(2,1)}), bf16[16,2,16384]{2,1,0:T(2,128)(2,1)S(1)}, u32[]{:S(2)}, u32[]{:S(2)}) async-start(bf16[16,2,16384]{2,1,0:T(2,128)(2,1)} %reshape.68), calls=%async_computation.3 | async-start | bytes 2097152 | tf_op jit(solution)/shard_map/all_to_all | solution.py:153
where the time goes:
time: 251 us; the launch traced here: 250 us
  blocking collectives  101 us (40%)
  local copies, waits for them, and re-layouts  81 us (32%)
  Pallas kernels  27.7 us (11%)
  starting transfers between devices  16.7 us (7%)
  other arithmetic  11.1 us (4%)
  waiting for transfers between devices  5.67 us (2%)
  matrix products  5.65 us (2%)
    psum x1, blocking collectives, per_device(): lax.psum(local_terms, ('wide', 'narrow')) * (1.0 / math.sqrt(NX * NY * NZ))  67.7 us
    all_to_all x1, blocking collectives, per_device(): zc = lax.all_to_all(zc, 'narrow', split_axis=1, concat_axis=3, tiled=True)  33.8 us
    unnamed x14, local copies, waits for them, and re-layouts  27.5 us
    pallas_call x1, Pallas kernels, synthesis(): pl.pallas_call(synthesis_kernel, grid=(steps,), in_specs=[field_spec, fie...  14 us
    pallas_call x1, Pallas kernels, analysis(): pl.pallas_call(analysis_kernel, grid=(steps,), in_specs=[field_spec, fiel...  13.7 us
    all_to_all x1, local copies, waits for them, and re-layouts, per_device(): lax.all_to_all(ysynth, 'narrow', split_axis=2, concat_axis=3, tiled=True)  10.8 us
    mul x1, local copies, waits for them, and re-layouts, per_device(): kron_skip = jnp.kron(skip_weight, jnp.eye(ny, dtype=skip_weight.dtype))  8.4 us
    all_to_all x1, starting transfers between devices, per_device(): lax.all_to_all(ycoeffs, 'wide', split_axis=2, concat_axis=3, tiled=True)  7.21 us
  transfers between devices with their start and end apart: 3, of which 1 were waited for; matrix products, arithmetic and copies ran while one was open for 12% of the time, Pallas kernels for 0%

commit v1 on v0

--- a/solution.py
+++ b/solution.py
@@ -77,8 +77,24 @@
     )(hidden_pre, cotangent, table_z)
 
 
-def synthesis_kernel(h_ref, g_ref, ys_ref, tz_ref, ks_ref, out_ref):
+def synthesis_kernel(h_ref, g_ref, ys_ref, tz_ref, sw_ref, out_ref, ks_ref):
     channels, xb, ny, nz = h_ref.shape
+    rows = channels * ny
+
+    @pl.when(pl.program_id(0) == 0)
+    def _():
+        r = lax.broadcasted_iota(jnp.int32, (rows, channels), 0)
+        k = lax.broadcasted_iota(jnp.int32, (rows, channels), 1)
+        expand = (r // ny == k).astype(jnp.float32)
+        spread = jnp.dot(expand, sw_ref[...].astype(jnp.float32), preferred_element_type=jnp.float32)
+        kr = lax.broadcasted_iota(jnp.int32, (channels, rows), 0)
+        kc = lax.broadcasted_iota(jnp.int32, (channels, rows), 1)
+        expand_t = (kc // ny == kr).astype(jnp.float32)
+        full = jnp.dot(spread, expand_t, preferred_element_type=jnp.float32)
+        ri = lax.broadcasted_iota(jnp.int32, (rows, rows), 0)
+        ci = lax.broadcasted_iota(jnp.int32, (rows, rows), 1)
+        ks_ref[...] = jnp.where(ri % ny == ci % ny, full, 0.0).astype(ks_ref.dtype)
+
     tz = tz_ref[...]
     ks = ks_ref[...]
     for x in range(xb):
@@ -90,7 +106,7 @@
         out_ref[:, x] = grad.astype(jnp.bfloat16).reshape(channels, ny, nz)
 
 
-def synthesis(hidden_pre, cotangent, ysynth, table_z, kron_skip):
+def synthesis(hidden_pre, cotangent, ysynth, table_z, skip_weight):
     channels, nx, ny, nz = hidden_pre.shape
     modes = table_z.shape[0]
     steps = nx // XB
@@ -103,14 +119,15 @@
             field_spec,
             pl.BlockSpec((XB, channels * ny, modes), lambda i: (i, 0, 0)),
             pl.BlockSpec((modes, nz), lambda i: (0, 0)),
-            pl.BlockSpec((channels * ny, channels * ny), lambda i: (0, 0)),
+            pl.BlockSpec((channels, channels), lambda i: (0, 0)),
         ],
         out_specs=field_spec,
         out_shape=jax.ShapeDtypeStruct(hidden_pre.shape, jnp.bfloat16),
+        scratch_shapes=[pltpu.VMEM((channels * ny, channels * ny), jnp.bfloat16)],
         compiler_params=pltpu.CompilerParams(
             dimension_semantics=("arbitrary",), vmem_limit_bytes=60 * 1024 * 1024
         ),
-    )(hidden_pre, cotangent, ysynth, table_z, kron_skip)
+    )(hidden_pre, cotangent, ysynth, table_z, skip_weight)
 
 
 def per_device(hidden_pre, cotangent, mode_weight, skip_weight):
@@ -152,13 +169,15 @@
     ).astype(jnp.bfloat16)
     ysynth = lax.all_to_all(ysynth, "narrow", split_axis=2, concat_axis=3, tiled=True)
     ysynth = ysynth.reshape(nx, channels * ny, mode_count)
-    kron_skip = jnp.kron(skip_weight, jnp.eye(ny, dtype=skip_weight.dtype))
-    grad_hidden = synthesis(hidden_pre, cotangent, ysynth, table_z, kron_skip)
+    grad_hidden = synthesis(hidden_pre, cotangent, ysynth, table_z, skip_weight)
 
     diag = jnp.eye(ny, dtype=jnp.float32)
     local_terms = (gram.reshape(channels, ny, channels, ny) * diag[None, :, None, :]).sum((1, 3))
-    grad_skip = lax.psum(local_terms, ("wide", "narrow")) * (1.0 / math.sqrt(NX * NY * NZ))
-    del n_narrow, n_wide
+    total = local_terms.reshape(1, channels * channels)
+    for axis, count in (("narrow", n_narrow), ("wide", n_wide)):
+        spread = jnp.broadcast_to(total, (count, channels * channels))
+        total = lax.all_to_all(spread, axis, 0, 0, tiled=True).sum(0, keepdims=True)
+    grad_skip = total.reshape(channels, channels) * (1.0 / math.sqrt(NX * NY * NZ))
     return (grad_hidden, grad_modes, grad_skip)
 
 

time: 251 us -> 190 us (0.76)
  blocking collectives: 101 us -> 0 us
  waiting for transfers between devices: 5.67 us -> 36.3 us
  starting transfers between devices: 16.7 us -> 34.1 us
  local copies, waits for them, and re-layouts: 81 us -> 75.4 us
  other arithmetic: 11.1 us -> 8.41 us
    psum x1 -> x0, blocking collectives: 67.7 us -> none  [per_device(): lax.psum(local_terms, ('wide', 'narrow')) * (1.0 / math.sqrt(NX * NY * NZ))]
    all_to_all x1 -> x0, blocking collectives: 33.8 us -> none  [per_device(): zc = lax.all_to_all(zc, 'narrow', split_axis=1, concat_axis=3, tiled=True)]
    all_to_all x0 -> x3, waiting for transfers between devices: none -> 19.2 us  [the longest x1 19.2 us: per_device(): zc = lax.all_to_all(zc, 'narrow', split_axis=1, concat_axis=3, tiled=True)]
    all_to_all x0 -> x3, starting transfers between devices: none -> 16.5 us  [the longest x2 9.21 us: per_device(): total = lax.all_to_all(spread, axis, 0, 0, tiled=True).sum(0, keepdims=True)]
    mul x1, local copies, waits for them, and re-layouts: 8.4 us -> 0.68 us  [per_device(): total.reshape(channels, channels) * (1.0 / math.sqrt(NX * NY * NZ))]
    all_to_all x1, waiting for transfers between devices: 0.01 us -> 7.52 us  [per_device(): lax.all_to_all(ysynth, 'narrow', split_axis=2, concat_axis=3, tiled=True)]
    all_to_all x1, waiting for transfers between devices: 0.01 us -> 6.71 us  [per_device(): lax.all_to_all(xsynth, 'wide', split_axis=3, concat_axis=2, tiled=True)]
    mul x2 -> x1, other arithmetic: 2.96 us -> 0.01 us  [per_device(): total.reshape(channels, channels) * (1.0 / math.sqrt(NX * NY * NZ))]
  transfers between devices with their start and end apart: 3 -> 6, of which waited for: 1 -> 4; matrix products, arithmetic and copies ran while one was open for 12% -> 23% of each run, Pallas kernels for 0% -> 0%
where the time goes in v1:
time: 190 us; the launch traced here: 189 us
  local copies, waits for them, and re-layouts  75.4 us (40%)
  waiting for transfers between devices  36.3 us (19%)
  starting transfers between devices  34.1 us (18%)
  Pallas kernels  27.9 us (15%)
  other arithmetic  8.41 us (4%)
  matrix products  5.63 us (3%)
    unnamed x12, local copies, waits for them, and re-layouts  26.2 us
    all_to_all x1, waiting for transfers between devices, per_device(): zc = lax.all_to_all(zc, 'narrow', split_axis=1, concat_axis=3, tiled=True)  19.2 us
    pallas_call x1, Pallas kernels, synthesis(): pl.pallas_call(synthesis_kernel, grid=(steps,), in_specs=[field_spec, fie...  14.2 us
    pallas_call x1, Pallas kernels, analysis(): pl.pallas_call(analysis_kernel, grid=(steps,), in_specs=[field_spec, fiel...  13.7 us
    all_to_all x1, local copies, waits for them, and re-layouts, per_device(): lax.all_to_all(ysynth, 'narrow', split_axis=2, concat_axis=3, tiled=True)  10.8 us
    all_to_all x2, starting transfers between devices, per_device(): total = lax.all_to_all(spread, axis, 0, 0, tiled=True).sum(0, keepdims=True)  9.21 us
    all_to_all x1, waiting for transfers between devices, per_device(): lax.all_to_all(ysynth, 'narrow', split_axis=2, concat_axis=3, tiled=True)  7.52 us
    all_to_all x1, starting transfers between devices, per_device(): zc = lax.all_to_all(zc, 'narrow', split_axis=1, concat_axis=3, tiled=True)  7.31 us
  transfers between devices with their start and end apart: 6, of which 4 were waited for; matrix products, arithmetic and copies ran while one was open for 23% of the time, Pallas kernels for 0%

profile of v1, /device:TPU:1, one launch (start us, length us, event | category | flops | bytes accessed | tf_op | source)
XLA Modules:
  0.0 188.5 jit_solution(8750308868185278274)
XLA Ops:
  0.7 0.8 multiply_convert_fusion.tz_ref
  1.5 13.7 %shard_map.67 = (bf16[64,32,512]{2,1,0:T(8,128)(2,1)}, f32[512,512]{1,0:T(8,128)}) custom-call(bf16[32,32,16,256]{3,2,1,0:T(8,128)(2,1)} %h_ref.3, bf16[32,32,16,256]{3,2,1,0:T(8,128)(2,1)} %g_ref.3, bf16[32,256]{1,0:T(8,128)(2,1)} %multiply_convert_fusion.tz_ref), custom_call_target="tpu_custom_call" | custom-call | tf_op jit(solution)/shard_map/pallas_call | solution.py:61
  15.2 5.2 %copy.61 = bf16[64,32,512]{0,2,1:T(8,128)(2,1)} copy(bf16[64,32,512]{2,1,0:T(8,128)(2,1)} %get-tuple-element.5) | data formatting | bytes 4194304 | tf_op jit(solution)/shard_map/pallas_call | solution.py:61
  20.3 7.5 %reshape.68 = bf16[16,2,32768]{2,1,0:T(2,128)(2,1)} reshape(bf16[32,32,16,64]{3,2,1,0:T(8,128)(2,1)} %bitcast.68) | data formatting | bytes 4194304
  27.8 0.0 copy-start.1
  27.8 7.3 %all-to-all-start = ((bf16[16,2,32768]{2,1,0:T(2,128)(2,1)}), bf16[16,2,32768]{2,1,0:T(2,128)(2,1)S(1)}, u32[]{:S(2)}, u32[]{:S(2)}) async-start(bf16[16,2,32768]{2,1,0:T(2,128)(2,1)} %reshape.68), calls=%async_computation | async-start | bytes 4194304 | tf_op jit(solution)/shard_map/all_to_all | solution.py:145
  35.1 3.7 %reshape.62 = bf16[2,4,32,32,32]{4,3,2,1,0:T(8,128)(2,1)} reshape(bf16[2,4,32,1024]{3,2,1,0:T(8,128)(2,1)} %param.6) | data formatting | bytes 1048576 | tf_op jit(solution)/shard_map/reshape | solution.py:157
  38.9 0.0 copy-done.1
  38.9 4.8 %reshape.64 = f32[32,16,32,16]{3,2,1,0:T(8,128)} reshape(f32[512,512]{1,0:T(8,128)S(1)} %copy-done.1) | data formatting | bytes 2097152 | tf_op jit(solution)/shard_map/reshape | solution.py:175
  43.7 19.2 %all-to-all-done = bf16[16,2,32768]{2,1,0:T(2,128)(2,1)S(1)} async-done(((bf16[16,2,32768]{2,1,0:T(2,128)(2,1)}), bf16[16,2,32768]{2,1,0:T(2,128)(2,1)S(1)}, u32[]{:S(2)}, u32[]{:S(2)}) %all-to-all-start) | async-done | bytes 2097184 | tf_op jit(solution)/shard_map/all_to_all | solution.py:145
  62.8 5.0 %reshape.69 = bf16[32,32,16,64]{3,2,1,0:T(8,128)(2,1)} reshape(bf16[16,2,32768]{2,1,0:T(2,128)(2,1)S(1)} %all-to-all-done) | data formatting | bytes 4194304
  67.8 3.4 %copy.62 = bf16[64,16,2,32,16]{0,4,1,3,2:T(8,128)(2,1)S(1)} copy(bf16[64,16,2,32,16]{0,4,3,2,1:T(8,128)(2,1)} %bitcast.71) | data formatting | bytes 4194304 | tf_op jit(solution)/shard_map/all_to_all | solution.py:145
  71.2 1.0 fusion.1
  72.2 0.2 copy.90
  72.4 1.1 reshape.70
  73.5 7.2 %all-to-all-start.1 = ((bf16[8,2,8192]{2,1,0:T(2,128)(2,1)}), bf16[8,2,8192]{2,1,0:T(2,128)(2,1)S(1)}, u32[]{:S(2)}, u32[]{:S(2)}) async-start(bf16[8,2,8192]{2,1,0:T(2,128)(2,1)} %reshape.70), calls=%async_computation.1 | async-start | bytes 524288 | tf_op jit(solution)/shard_map/all_to_all | solution.py:149
  80.7 0.0 copy-start
  80.7 4.5 %multiply_reduce_fusion = f32[32,32]{1,0:T(8,128)S(1)} fusion(f32[32,16,32,16]{3,2,1,0:T(8,128)} %reshape.64, f32[16,16]{1,0:T(8,128)S(1)} %fusion.16), kind=kLoop, calls=%fused_computation | loop fusion | flops 523264 | bytes 1053696 | tf_op jit(solution)/shard_map/reduce_sum | solution.py:175
  85.2 0.1 broadcast_in_dim.50
  85.2 2.9 %all-to-all-done.1 = bf16[8,2,8192]{2,1,0:T(2,128)(2,1)S(1)} async-done(((bf16[8,2,8192]{2,1,0:T(2,128)(2,1)}), bf16[8,2,8192]{2,1,0:T(2,128)(2,1)S(1)}, u32[]{:S(2)}, u32[]{:S(2)}) %all-to-all-start.1) | async-done | bytes 262176 | tf_op jit(solution)/shard_map/all_to_all | solution.py:149
  88.2 0.7 broadcast_in_dim.51
  88.8 5.9 %all-to-all-start.4 = ((f32[16,1,1024]{2,1,0:T(1,128)}), f32[16,1,1024]{2,1,0:T(1,128)S(1)}, u32[]{:S(2)}, u32[]{:S(2)}) async-start(f32[16,1,1024]{2,1,0:T(1,128)} %broadcast_in_dim.51), calls=%async_computation.4 | async-start | bytes 131072 | tf_op jit(solution)/shard_map/all_to_all | solution.py:179
  94.7 0.3 reshape.71
  95.1 0.3 fusion.13
  95.4 0.1 slice_bitcast_fusion
  95.5 0.0 copy-done
  95.5 3.4 %fusion.37 = bf16[2,4,32,1,32]{4,3,2,1,0:T(2,128)(2,1)S(1)} fusion(f32[2,4,32,32,1]{3,4,2,1,0:T(1,128)S(1)} %bitcast.79, bf16[2,4,32,32,32]{4,3,2,1,0:T(8,128)(2,1)S(1)} %copy-done), kind=kOutput, calls=%fused_computation.53 | convolution fusion | flops 3145728 | bytes 573440 | tf_op jit(solution)/shard_map/zykco,zyko->zcyk/dot_general | solution.py:160
  98.9 0.1 copy.81
  99.0 0.4 convolution_convert_fusion.2
  99.4 0.3 copy.67
  99.7 1.2 reshape.72
  100.9 0.0 all-to-all-done.4
  100.9 3.4 %all-to-all-start.2 = ((bf16[8,2,4096]{2,1,0:T(2,128)(2,1)}), bf16[8,2,4096]{2,1,0:T(2,128)(2,1)S(1)}, u32[]{:S(2)}, u32[]{:S(2)}) async-start(bf16[8,2,4096]{2,1,0:T(2,128)(2,1)} %reshape.72), calls=%async_computation.2 | async-start | bytes 262144 | tf_op jit(solution)/shard_map/all_to_all | solution.py:166
  104.3 0.1 reduce_sum.28
  104.3 6.7 %all-to-all-done.2 = bf16[8,2,4096]{2,1,0:T(2,128)(2,1)S(1)} async-done(((bf16[8,2,4096]{2,1,0:T(2,128)(2,1)}), bf16[8,2,4096]{2,1,0:T(2,128)(2,1)S(1)}, u32[]{:S(2)}, u32[]{:S(2)}) %all-to-all-start.2) | async-done | bytes 131104 | tf_op jit(solution)/shard_map/all_to_all | solution.py:166
  111.0 0.6 broadcast_in_dim.52
  111.7 3.3 %all-to-all-start.5 = ((f32[8,1,1024]{2,1,0:T(1,128)}), f32[8,1,1024]{2,1,0:T(1,128)S(1)}, u32[]{:S(2)}, u32[]{:S(2)}) async-start(f32[8,1,1024]{2,1,0:T(1,128)} %broadcast_in_dim.52), calls=%async_computation.5 | async-start | bytes 65536 | tf_op jit(solution)/shard_map/all_to_all | solution.py:179
  115.0 0.3 reshape.73
  115.3 0.4 copy.83
  115.7 0.6 fusion
  116.3 6.4 %copy.71 = bf16[32,32,256,2]{0,1,3,2:T(8,128)(2,1)} copy(bf16[32,32,256,2]{2,0,1,3:T(8,128)(2,1)S(1)} %fusion) | data formatting | bytes 2097152 | tf_op jit(solution)/shard_map/convert_element_type | solution.py:169
  122.8 7.4 %reshape.74 = bf16[16,2,16384]{2,1,0:T(2,128)(2,1)} reshape(bf16[256,2,32,32]{3,2,1,0:T(8,128)(2,1)} %bitcast.67) | data formatting | bytes 2097152
  130.2 0.0 all-to-all-done.5
  130.2 7.0 %all-to-all-start.3 = ((bf16[16,2,16384]{2,1,0:T(2,128)(2,1)}), bf16[16,2,16384]{2,1,0:T(2,128)(2,1)S(1)}, u32[]{:S(2)}, u32[]{:S(2)}) async-start(bf16[16,2,16384]{2,1,0:T(2,128)(2,1)} %reshape.74), calls=%async_computation.3 | async-start | bytes 2097152 | tf_op jit(solution)/shard_map/all_to_all | solution.py:170
  137.2 0.7 mul.134
  137.9 3.0 %broadcast_multiply_fusion = f32[2,4,32,32,32]{4,3,2,1,0:T(8,128)} fusion(f32[2,4,32,32]{3,2,1,0:T(8,128)S(1)} %get-tuple-element.8, f32[2,4,32,32]{3,2,1,0:T(8,128)S(1)} %get-tuple-element.7), kind=kLoop, calls=%fused_computation.1 | loop fusion | flops 262144 | bytes 1114112 | tf_op jit(solution)/shard_map/mul | solution.py:154
  140.9 4.6 %mul.129 = f32[2,4,32,1024]{3,2,1,0:T(8,128)} reshape(f32[2,4,32,32,32]{4,3,2,1,0:T(8,128)} %broadcast_multiply_fusion) | data formatting | bytes 2097152 | tf_op jit(solution)/shard_map/mul | solution.py:154
  145.5 7.5 %all-to-all-done.3 = bf16[16,2,16384]{2,1,0:T(2,128)(2,1)S(1)} async-done(((bf16[16,2,16384]{2,1,0:T(2,128)(2,1)}), bf16[16,2,16384]{2,1,0:T(2,128)(2,1)S(1)}, u32[]{:S(2)}, u32[]{:S(2)}) %all-to-all-start.3) | async-done | bytes 1048608 | tf_op jit(solution)/shard_map/all_to_all | solution.py:170
  153.0 3.5 %reshape.75 = bf16[256,2,32,32]{3,2,1,0:T(8,128)(2,1)} reshape(bf16[16,2,16384]{2,1,0:T(2,128)(2,1)S(1)} %all-to-all-done.3) | data formatting | bytes 2097152
  156.5 10.8 %copy.73 = bf16[32,32,16,16,2]{0,2,1,4,3:T(8,128)(2,1)} copy(bf16[32,32,16,16,2]{0,1,4,2,3:T(8,128)(2,1)} %bitcast.70) | data formatting | bytes 2097152 | tf_op jit(solution)/shard_map/all_to_all | solution.py:170
  167.2 7.1 %copy.74.ys_ref = bf16[32,512,32]{2,1,0:T(8,128)(2,1)} copy(bf16[32,512,32]{0,1,2:T(8,128)(2,1)} %bitcast.72) | data formatting | bytes 2097152 | tf_op jit(solution)/shard_map/reshape | solution.py:171
  174.3 14.2 %shard_map.68 = bf16[32,32,16,256]{3,2,1,0:T(8,128)(2,1)} custom-call(bf16[32,32,16,256]{3,2,1,0:T(8,128)(2,1)} %h_ref.3, bf16[32,32,16,256]{3,2,1,0:T(8,128)(2,1)} %g_ref.3, bf16[32,512,32]{2,1,0:T(8,128)(2,1)} %copy.74.ys_ref, bf16[32,256]{1,0:T(8,128)(2,1)} %multiply_convert_fusion.tz_ref, bf16[32,32]{1,0:T(8,128)(2,1)} %sw_ref.1), custom_call_target="tpu_custom_call" | custom-call | tf_op jit(solution)/shard_map/pallas_call | solution.py:114
  (6 shorter events, 0.1 us)
Async XLA Ops:
  27.8 11.0 %copy-start.1 = (f32[512,512]{1,0:T(8,128)S(1)}, f32[512,512]{1,0:T(8,128)}, u32[]{:S(2)}) copy-start(f32[512,512]{1,0:T(8,128)} %get-tuple-element.6) | copy-start | bytes 3145732
  27.8 35.0 %all-to-all-start = ((bf16[16,2,32768]{2,1,0:T(2,128)(2,1)}), bf16[16,2,32768]{2,1,0:T(2,128)(2,1)S(1)}, u32[]{:S(2)}, u32[]{:S(2)}) async-start(bf16[16,2,32768]{2,1,0:T(2,128)(2,1)} %reshape.68), calls=%async_computation | async-start | bytes 4194304 | tf_op jit(solution)/shard_map/all_to_all | solution.py:145
  73.5 14.7 %all-to-all-start.1 = ((bf16[8,2,8192]{2,1,0:T(2,128)(2,1)}), bf16[8,2,8192]{2,1,0:T(2,128)(2,1)S(1)}, u32[]{:S(2)}, u32[]{:S(2)}) async-start(bf16[8,2,8192]{2,1,0:T(2,128)(2,1)} %reshape.70), calls=%async_computation.1 | async-start | bytes 524288 | tf_op jit(solution)/shard_map/all_to_all | solution.py:149
  80.7 14.8 %copy-start = (bf16[2,4,32,32,32]{4,3,2,1,0:T(8,128)(2,1)S(1)}, bf16[2,4,32,32,32]{4,3,2,1,0:T(8,128)(2,1)}, u32[]{:S(2)}) copy-start(bf16[2,4,32,32,32]{4,3,2,1,0:T(8,128)(2,1)} %reshape.62) | copy-start | bytes 1572868
  88.8 12.1 %all-to-all-start.4 = ((f32[16,1,1024]{2,1,0:T(1,128)}), f32[16,1,1024]{2,1,0:T(1,128)S(1)}, u32[]{:S(2)}, u32[]{:S(2)}) async-start(f32[16,1,1024]{2,1,0:T(1,128)} %broadcast_in_dim.51), calls=%async_computation.4 | async-start | bytes 131072 | tf_op jit(solution)/shard_map/all_to_all | solution.py:179
  100.9 10.2 %all-to-all-start.2 = ((bf16[8,2,4096]{2,1,0:T(2,128)(2,1)}), bf16[8,2,4096]{2,1,0:T(2,128)(2,1)S(1)}, u32[]{:S(2)}, u32[]{:S(2)}) async-start(bf16[8,2,4096]{2,1,0:T(2,128)(2,1)} %reshape.72), calls=%async_computation.2 | async-start | bytes 262144 | tf_op jit(solution)/shard_map/all_to_all | solution.py:166
  111.7 18.5 %all-to-all-start.5 = ((f32[8,1,1024]{2,1,0:T(1,128)}), f32[8,1,1024]{2,1,0:T(1,128)S(1)}, u32[]{:S(2)}, u32[]{:S(2)}) async-start(f32[8,1,1024]{2,1,0:T(1,128)} %broadcast_in_dim.52), calls=%async_computation.5 | async-start | bytes 65536 | tf_op jit(solution)/shard_map/all_to_all | solution.py:179
  130.2 22.8 %all-to-all-start.3 = ((bf16[16,2,16384]{2,1,0:T(2,128)(2,1)}), bf16[16,2,16384]{2,1,0:T(2,128)(2,1)S(1)}, u32[]{:S(2)}, u32[]{:S(2)}) async-start(bf16[16,2,16384]{2,1,0:T(2,128)(2,1)} %reshape.74), calls=%async_computation.3 | async-start | bytes 2097152 | tf_op jit(solution)/shard_map/all_to_all | solution.py:170

commit v2 on v1

--- a/solution.py
+++ b/solution.py
@@ -50,7 +50,17 @@
 
     @pl.when(step == pl.num_programs(0) - 1)
     def _():
-        gram_ref[...] = acc_ref[...]
+        rows = channels * ny
+        ri = lax.broadcasted_iota(jnp.int32, (rows, rows), 0)
+        ci = lax.broadcasted_iota(jnp.int32, (rows, rows), 1)
+        diag = jnp.where(ri % ny == ci % ny, acc_ref[...], 0.0)
+        er = lax.broadcasted_iota(jnp.int32, (channels, rows), 0)
+        ec = lax.broadcasted_iota(jnp.int32, (channels, rows), 1)
+        gather = (ec // ny == er).astype(jnp.float32)
+        part = jnp.dot(gather, diag, precision=lax.Precision.HIGHEST, preferred_element_type=jnp.float32)
+        gram_ref[...] = lax.dot_general(
+            part, gather, (((1,), (1,)), ((), ())), precision=lax.Precision.HIGHEST,
+            preferred_element_type=jnp.float32)
 
 
 def analysis(hidden_pre, cotangent, table_z):
@@ -64,11 +74,11 @@
         in_specs=[field_spec, field_spec, pl.BlockSpec((modes, nz), lambda i: (0, 0))],
         out_specs=[
             pl.BlockSpec((2 * channels, modes, XB * ny), lambda i: (0, 0, i)),
-            pl.BlockSpec((channels * ny, channels * ny), lambda i: (0, 0)),
+            pl.BlockSpec((channels, channels), lambda i: (0, 0)),
         ],
         out_shape=[
             jax.ShapeDtypeStruct((2 * channels, modes, nx * ny), jnp.bfloat16),
-            jax.ShapeDtypeStruct((channels * ny, channels * ny), jnp.float32),
+            jax.ShapeDtypeStruct((channels, channels), jnp.float32),
         ],
         scratch_shapes=[pltpu.VMEM((channels * ny, channels * ny), jnp.float32)],
         compiler_params=pltpu.CompilerParams(
@@ -130,6 +140,40 @@
     )(hidden_pre, cotangent, ysynth, table_z, skip_weight)
 
 
+def modes_kernel(sp_ref, w_ref, gm_ref, bs_ref):
+    highest = lax.Precision.HIGHEST
+    channels = sp_ref.shape[1] // 2
+    width = channels * channels
+    sp = sp_ref[...]
+    er = lax.broadcasted_iota(jnp.int32, (channels, width), 0)
+    ec = lax.broadcasted_iota(jnp.int32, (channels, width), 1)
+    spread = (ec // channels == er).astype(jnp.float32)
+    tile = (ec % channels == er).astype(jnp.float32)
+    s_rep = jnp.dot(sp[:, :channels], spread, precision=highest, preferred_element_type=jnp.float32)
+    q_rep = jnp.dot(sp[:, channels:], tile, precision=highest, preferred_element_type=jnp.float32)
+    gm_ref[...] = s_rep * q_rep
+    weighted = w_ref[...].astype(jnp.float32) * q_rep
+    back = lax.dot_general(
+        weighted, spread, (((1,), (1,)), ((), ())), precision=highest,
+        preferred_element_type=jnp.float32)
+    bs_ref[...] = back.astype(bs_ref.dtype)
+
+
+def modes_step(spectra, weights):
+    rows, both = spectra.shape
+    channels = both // 2
+    vmem = pl.BlockSpec(memory_space=pltpu.VMEM)
+    return pl.pallas_call(
+        modes_kernel,
+        in_specs=[vmem, vmem],
+        out_specs=[vmem, vmem],
+        out_shape=[
+            jax.ShapeDtypeStruct((rows, channels * channels), jnp.float32),
+            jax.ShapeDtypeStruct((rows, channels), jnp.bfloat16),
+        ],
+    )(spectra, weights)
+
+
 def per_device(hidden_pre, cotangent, mode_weight, skip_weight):
     highest = lax.Precision.HIGHEST
     channels, nx, ny, nz = hidden_pre.shape
@@ -147,18 +191,15 @@
         "cmxy,ny->mcnx", zc, table_y, preferred_element_type=jnp.float32
     ).astype(jnp.bfloat16)
     ycoeffs = lax.all_to_all(ycoeffs, "wide", split_axis=2, concat_axis=3, tiled=True)
-    spectra = jnp.einsum("zcyx,kx->zcyk", ycoeffs, table_x, preferred_element_type=jnp.float32)
-    s_modes = jnp.transpose(spectra[:, :channels], (0, 2, 3, 1))
-    q_modes = jnp.transpose(spectra[:, channels:], (0, 2, 3, 1))
-    z_local, y_local = (s_modes.shape[0], s_modes.shape[1])
-    grad_modes = (s_modes[..., :, None] * q_modes[..., None, :]).reshape(
-        z_local, y_local, mode_count, channels * channels
-    )
-    weights_five = mode_weight.reshape(z_local, y_local, mode_count, channels, channels).astype(
-        jnp.float32
-    )
-    back_spec = jnp.einsum("zykco,zyko->zcyk", weights_five, q_modes, precision=highest).astype(
-        jnp.bfloat16
+    spectra = jnp.einsum("zcyx,kx->zykc", ycoeffs, table_x, preferred_element_type=jnp.float32)
+    z_local, y_local = (spectra.shape[0], spectra.shape[1])
+    grad_modes, back_spec = modes_step(
+        spectra.reshape(z_local * y_local * mode_count, 2 * channels),
+        mode_weight.reshape(z_local * y_local * mode_count, channels * channels),
+    )
+    grad_modes = grad_modes.reshape(z_local, y_local, mode_count, channels * channels)
+    back_spec = jnp.transpose(
+        back_spec.reshape(z_local, y_local, mode_count, channels), (0, 3, 1, 2)
     )
     xsynth = jnp.einsum(
         "zcyk,kx->zcyx", back_spec, table_x, preferred_element_type=jnp.float32
@@ -171,9 +212,7 @@
     ysynth = ysynth.reshape(nx, channels * ny, mode_count)
     grad_hidden = synthesis(hidden_pre, cotangent, ysynth, table_z, skip_weight)
 
-    diag = jnp.eye(ny, dtype=jnp.float32)
-    local_terms = (gram.reshape(channels, ny, channels, ny) * diag[None, :, None, :]).sum((1, 3))
-    total = local_terms.reshape(1, channels * channels)
+    total = gram.reshape(1, channels * channels)
     for axis, count in (("narrow", n_narrow), ("wide", n_wide)):
         spread = jnp.broadcast_to(total, (count, channels * channels))
         total = lax.all_to_all(spread, axis, 0, 0, tiled=True).sum(0, keepdims=True)

time: 190 us -> 193 us (1.016)
  blocking collectives: 0 us -> 33.8 us
  local copies, waits for them, and re-layouts: 75.4 us -> 64.3 us
  other arithmetic: 8.41 us -> 0.92 us
  waiting for transfers between devices: 36.3 us -> 29 us
  starting transfers between devices: 34.1 us -> 27 us
  Pallas kernels: 27.9 us -> 33.6 us
  matrix products: 5.63 us -> 2.94 us
    all_to_all x0 -> x1, blocking collectives: none -> 33.8 us  [per_device(): zc = lax.all_to_all(zc, 'narrow', split_axis=1, concat_axis=3, tiled=True)]
    all_to_all x1 -> x0, waiting for transfers between devices: 19.2 us -> none  [per_device(): zc = lax.all_to_all(zc, 'narrow', split_axis=1, concat_axis=3, tiled=True)]
    all_to_all x1, waiting for transfers between devices: 7.52 us -> 15.1 us  [per_device(): lax.all_to_all(ysynth, 'narrow', split_axis=2, concat_axis=3, tiled=True)]
    reshape x2 -> x1, local copies, waits for them, and re-layouts: 8.51 us -> 0.93 us  [per_device(): back_spec.reshape(z_local, y_local, mode_count, channels)]
    all_to_all x1 -> x0, starting transfers between devices: 7.31 us -> none  [per_device(): zc = lax.all_to_all(zc, 'narrow', split_axis=1, concat_axis=3, tiled=True)]
    pallas_call x0 -> x1, Pallas kernels: none -> 5.16 us  [modes_step(): pl.pallas_call(modes_kernel, in_specs=[vmem, vmem], out_specs=[vmem, vmem...]
    mul x1 -> x0, local copies, waits for them, and re-layouts: 4.58 us -> none  [per_device(): s_modes[..., :, None] * q_modes[..., None, :]]
    reduce_sum x1 -> x0, other arithmetic: 4.45 us -> none  [per_device(): (gram.reshape(channels, ny, channels, ny) * diag[None, :, None, :]).sum((...]
  transfers between devices with their start and end apart: 6 -> 5, of which waited for: 4 -> 3; matrix products, arithmetic and copies ran while one was open for 23% -> 10% of each run, Pallas kernels for 0% -> 3%
where the time goes in v2:
time: 193 us; the launch traced here: 192 us
  local copies, waits for them, and re-layouts  64.3 us (33%)
  blocking collectives  33.8 us (18%)
  Pallas kernels  33.6 us (17%)
  waiting for transfers between devices  29 us (15%)
  starting transfers between devices  27 us (14%)
  matrix products  2.94 us (2%)
    all_to_all x1, blocking collectives, per_device(): zc = lax.all_to_all(zc, 'narrow', split_axis=1, concat_axis=3, tiled=True)  33.8 us
    unnamed x10, local copies, waits for them, and re-layouts  27.5 us
    all_to_all x1, waiting for transfers between devices, per_device(): lax.all_to_all(ysynth, 'narrow', split_axis=2, concat_axis=3, tiled=True)  15.1 us
    pallas_call x1, Pallas kernels, synthesis(): pl.pallas_call(synthesis_kernel, grid=(steps,), in_specs=[field_spec, fie...  14.2 us
    pallas_call x1, Pallas kernels, analysis(): pl.pallas_call(analysis_kernel, grid=(steps,), in_specs=[field_spec, fiel...  14.2 us
    all_to_all x1, local copies, waits for them, and re-layouts, per_device(): lax.all_to_all(ysynth, 'narrow', split_axis=2, concat_axis=3, tiled=True)  10.8 us
    all_to_all x2, starting transfers between devices, per_device(): total = lax.all_to_all(spread, axis, 0, 0, tiled=True).sum(0, keepdims=True)  9.28 us
    all_to_all x1, waiting for transfers between devices, per_device(): lax.all_to_all(ycoeffs, 'wide', split_axis=2, concat_axis=3, tiled=True)  7.21 us
  transfers between devices with their start and end apart: 5, of which 3 were waited for; matrix products, arithmetic and copies ran while one was open for 10% of the time, Pallas kernels for 3%

profile of v2, /device:TPU:1, one launch (start us, length us, event | category | flops | bytes accessed | tf_op | source)
XLA Modules:
  0.0 192.2 jit_solution(9071240418222392514)
XLA Ops:
  0.7 0.8 multiply_convert_fusion.tz_ref
  1.5 14.2 %shard_map.67 = (bf16[64,32,512]{2,1,0:T(8,128)(2,1)}, f32[32,32]{1,0:T(8,128)}) custom-call(bf16[32,32,16,256]{3,2,1,0:T(8,128)(2,1)} %h_ref.3, bf16[32,32,16,256]{3,2,1,0:T(8,128)(2,1)} %g_ref.3, bf16[32,256]{1,0:T(8,128)(2,1)} %multiply_convert_fusion.tz_ref), custom_call_target="tpu_custom_call" | custom-call | tf_op jit(solution)/shard_map/pallas_call | solution.py:71
  15.7 5.2 %copy.66 = bf16[64,32,512]{0,2,1:T(8,128)(2,1)} copy(bf16[64,32,512]{2,1,0:T(8,128)(2,1)} %get-tuple-element.7) | data formatting | bytes 4194304 | tf_op jit(solution)/shard_map/pallas_call | solution.py:71
  20.8 6.3 %reshape.60 = bf16[16,2,32768]{2,1,0:T(2,128)(2,1)S(1)} reshape(bf16[32,32,16,64]{3,2,1,0:T(8,128)(2,1)} %bitcast.55) | data formatting | bytes 4194304
  27.2 33.8 %all_to_all.81 = bf16[16,2,32768]{2,1,0:T(2,128)(2,1)} all-to-all(bf16[16,2,32768]{2,1,0:T(2,128)(2,1)S(1)} %reshape.60), channel_id=1, replica_groups=mesh['wide'=8,'narrow'=16] {'narrow'}, dimensions={0} | all-to-all | bytes 4194304 | tf_op jit(solution)/shard_map/all_to_all | solution.py:189
  61.0 7.4 %reshape.61 = bf16[32,32,16,64]{3,2,1,0:T(8,128)(2,1)} reshape(bf16[16,2,32768]{2,1,0:T(2,128)(2,1)} %all_to_all.81) | data formatting | bytes 4194304
  68.4 3.4 %copy.67 = bf16[64,16,2,32,16]{0,4,1,3,2:T(8,128)(2,1)S(1)} copy(bf16[64,16,2,32,16]{0,4,3,2,1:T(8,128)(2,1)} %bitcast.58) | data formatting | bytes 4194304 | tf_op jit(solution)/shard_map/all_to_all | solution.py:189
  71.8 0.0 copy-start
  71.8 1.0 fusion.1
  72.8 0.2 copy.94
  73.0 1.1 reshape.62
  74.1 7.2 %all-to-all-start.1 = ((bf16[8,2,8192]{2,1,0:T(2,128)(2,1)}), bf16[8,2,8192]{2,1,0:T(2,128)(2,1)S(1)}, u32[]{:S(2)}, u32[]{:S(2)}) async-start(bf16[8,2,8192]{2,1,0:T(2,128)(2,1)} %reshape.62), calls=%async_computation.1 | async-start | bytes 524288 | tf_op jit(solution)/shard_map/all_to_all | solution.py:193
  81.3 0.0 copy-done
  81.3 0.1 broadcast_in_dim.47
  81.4 7.2 %all-to-all-done.1 = bf16[8,2,8192]{2,1,0:T(2,128)(2,1)S(1)} async-done(((bf16[8,2,8192]{2,1,0:T(2,128)(2,1)}), bf16[8,2,8192]{2,1,0:T(2,128)(2,1)S(1)}, u32[]{:S(2)}, u32[]{:S(2)}) %all-to-all-start.1) | async-done | bytes 262176 | tf_op jit(solution)/shard_map/all_to_all | solution.py:193
  88.6 0.7 broadcast_in_dim.48
  89.2 5.8 %all-to-all-start.4 = ((f32[16,1,1024]{2,1,0:T(1,128)}), f32[16,1,1024]{2,1,0:T(1,128)S(1)}, u32[]{:S(2)}, u32[]{:S(2)}) async-start(f32[16,1,1024]{2,1,0:T(1,128)} %broadcast_in_dim.48), calls=%async_computation.4 | async-start | bytes 131072 | tf_op jit(solution)/shard_map/all_to_all | solution.py:218
  95.0 0.3 reshape.63
  95.4 1.0 fusion.12
  96.4 5.2 %shard_map.68 = (f32[256,1024]{1,0:T(8,128)}, bf16[256,32]{1,0:T(8,128)(2,1)}) custom-call(f32[256,64]{1,0:T(8,128)} %bitcast.66, bf16[256,1024]{1,0:T(8,128)(2,1)} %bitcast.67), custom_call_target="tpu_custom_call" | custom-call | tf_op jit(solution)/shard_map/pallas_call | solution.py:166
  101.6 0.9 copy.72
  102.5 0.4 convolution_convert_fusion.2
  102.9 0.3 copy.73
  103.2 1.2 reshape.64
  104.4 0.0 all-to-all-done.4
  104.4 3.4 %all-to-all-start.2 = ((bf16[8,2,4096]{2,1,0:T(2,128)(2,1)}), bf16[8,2,4096]{2,1,0:T(2,128)(2,1)S(1)}, u32[]{:S(2)}, u32[]{:S(2)}) async-start(bf16[8,2,4096]{2,1,0:T(2,128)(2,1)} %reshape.64), calls=%async_computation.2 | async-start | bytes 262144 | tf_op jit(solution)/shard_map/all_to_all | solution.py:207
  107.7 0.1 reduce_sum.18
  107.8 6.6 %all-to-all-done.2 = bf16[8,2,4096]{2,1,0:T(2,128)(2,1)S(1)} async-done(((bf16[8,2,4096]{2,1,0:T(2,128)(2,1)}), bf16[8,2,4096]{2,1,0:T(2,128)(2,1)S(1)}, u32[]{:S(2)}, u32[]{:S(2)}) %all-to-all-start.2) | async-done | bytes 131104 | tf_op jit(solution)/shard_map/all_to_all | solution.py:207
  114.4 0.6 broadcast_in_dim.49
  115.1 3.5 %all-to-all-start.5 = ((f32[8,1,1024]{2,1,0:T(1,128)}), f32[8,1,1024]{2,1,0:T(1,128)S(1)}, u32[]{:S(2)}, u32[]{:S(2)}) async-start(f32[8,1,1024]{2,1,0:T(1,128)} %broadcast_in_dim.49), calls=%async_computation.5 | async-start | bytes 65536 | tf_op jit(solution)/shard_map/all_to_all | solution.py:218
  118.6 0.3 reshape.65
  118.8 0.4 copy.87
  119.2 0.6 fusion
  119.9 6.4 %copy.77 = bf16[32,32,256,2]{0,1,3,2:T(8,128)(2,1)} copy(bf16[32,32,256,2]{2,0,1,3:T(8,128)(2,1)S(1)} %fusion) | data formatting | bytes 2097152 | tf_op jit(solution)/shard_map/convert_element_type | solution.py:210
  126.3 7.4 %reshape.66 = bf16[16,2,16384]{2,1,0:T(2,128)(2,1)} reshape(bf16[256,2,32,32]{3,2,1,0:T(8,128)(2,1)} %bitcast.54) | data formatting | bytes 2097152
  133.7 0.0 all-to-all-done.5
  133.7 7.1 %all-to-all-start.3 = ((bf16[16,2,16384]{2,1,0:T(2,128)(2,1)}), bf16[16,2,16384]{2,1,0:T(2,128)(2,1)S(1)}, u32[]{:S(2)}, u32[]{:S(2)}) async-start(bf16[16,2,16384]{2,1,0:T(2,128)(2,1)} %reshape.66), calls=%async_computation.3 | async-start | bytes 2097152 | tf_op jit(solution)/shard_map/all_to_all | solution.py:211
  140.9 0.7 mul.103
  141.6 15.1 %all-to-all-done.3 = bf16[16,2,16384]{2,1,0:T(2,128)(2,1)S(1)} async-done(((bf16[16,2,16384]{2,1,0:T(2,128)(2,1)}), bf16[16,2,16384]{2,1,0:T(2,128)(2,1)S(1)}, u32[]{:S(2)}, u32[]{:S(2)}) %all-to-all-start.3) | async-done | bytes 1048608 | tf_op jit(solution)/shard_map/all_to_all | solution.py:211
  156.7 3.5 %reshape.67 = bf16[256,2,32,32]{3,2,1,0:T(8,128)(2,1)} reshape(bf16[16,2,16384]{2,1,0:T(2,128)(2,1)S(1)} %all-to-all-done.3) | data formatting | bytes 2097152
  160.1 10.8 %copy.79 = bf16[32,32,16,16,2]{0,2,1,4,3:T(8,128)(2,1)} copy(bf16[32,32,16,16,2]{0,1,4,2,3:T(8,128)(2,1)} %bitcast.57) | data formatting | bytes 2097152 | tf_op jit(solution)/shard_map/all_to_all | solution.py:211
  170.9 7.1 %copy.80.ys_ref = bf16[32,512,32]{2,1,0:T(8,128)(2,1)} copy(bf16[32,512,32]{0,1,2:T(8,128)(2,1)} %bitcast.59) | data formatting | bytes 2097152 | tf_op jit(solution)/shard_map/reshape | solution.py:212
  178.0 14.2 %shard_map.69 = bf16[32,32,16,256]{3,2,1,0:T(8,128)(2,1)} custom-call(bf16[32,32,16,256]{3,2,1,0:T(8,128)(2,1)} %h_ref.3, bf16[32,32,16,256]{3,2,1,0:T(8,128)(2,1)} %g_ref.3, bf16[32,512,32]{2,1,0:T(8,128)(2,1)} %copy.80.ys_ref, bf16[32,256]{1,0:T(8,128)(2,1)} %multiply_convert_fusion.tz_ref, bf16[32,32]{1,0:T(8,128)(2,1)} %sw_ref.1), custom_call_target="tpu_custom_call" | custom-call | tf_op jit(solution)/shard_map/pallas_call | solution.py:124
  (5 shorter events, 0.1 us)
Async XLA Ops:
  71.8 9.5 %copy-start = (f32[32,32]{1,0:T(8,128)S(1)}, f32[32,32]{1,0:T(8,128)}, u32[]{:S(2)}) copy-start(f32[32,32]{1,0:T(8,128)} %get-tuple-element.10) | copy-start | bytes 12292
  74.1 14.5 %all-to-all-start.1 = ((bf16[8,2,8192]{2,1,0:T(2,128)(2,1)}), bf16[8,2,8192]{2,1,0:T(2,128)(2,1)S(1)}, u32[]{:S(2)}, u32[]{:S(2)}) async-start(bf16[8,2,8192]{2,1,0:T(2,128)(2,1)} %reshape.62), calls=%async_computation.1 | async-start | bytes 524288 | tf_op jit(solution)/shard_map/all_to_all | solution.py:193
  89.2 15.1 %all-to-all-start.4 = ((f32[16,1,1024]{2,1,0:T(1,128)}), f32[16,1,1024]{2,1,0:T(1,128)S(1)}, u32[]{:S(2)}, u32[]{:S(2)}) async-start(f32[16,1,1024]{2,1,0:T(1,128)} %broadcast_in_dim.48), calls=%async_computation.4 | async-start | bytes 131072 | tf_op jit(solution)/shard_map/all_to_all | solution.py:218
  104.4 10.1 %all-to-all-start.2 = ((bf16[8,2,4096]{2,1,0:T(2,128)(2,1)}), bf16[8,2,4096]{2,1,0:T(2,128)(2,1)S(1)}, u32[]{:S(2)}, u32[]{:S(2)}) async-start(bf16[8,2,4096]{2,1,0:T(2,128)(2,1)} %reshape.64), calls=%async_computation.2 | async-start | bytes 262144 | tf_op jit(solution)/shard_map/all_to_all | solution.py:207
  115.1 18.7 %all-to-all-start.5 = ((f32[8,1,1024]{2,1,0:T(1,128)}), f32[8,1,1024]{2,1,0:T(1,128)S(1)}, u32[]{:S(2)}, u32[]{:S(2)}) async-start(f32[8,1,1024]{2,1,0:T(1,128)} %broadcast_in_dim.49), calls=%async_computation.5 | async-start | bytes 65536 | tf_op jit(solution)/shard_map/all_to_all | solution.py:218
  133.7 23.0 %all-to-all-start.3 = ((bf16[16,2,16384]{2,1,0:T(2,128)(2,1)}), bf16[16,2,16384]{2,1,0:T(2,128)(2,1)S(1)}, u32[]{:S(2)}, u32[]{:S(2)}) async-start(bf16[16,2,16384]{2,1,0:T(2,128)(2,1)} %reshape.66), calls=%async_computation.3 | async-start | bytes 2097152 | tf_op jit(solution)/shard_map/all_to_all | solution.py:211

commit v3 on v2

--- a/solution.py
+++ b/solution.py
@@ -205,10 +205,12 @@
         "zcyk,kx->zcyx", back_spec, table_x, preferred_element_type=jnp.float32
     ).astype(jnp.bfloat16)
     xsynth = lax.all_to_all(xsynth, "wide", split_axis=3, concat_axis=2, tiled=True)
+    xsynth = lax.all_gather(xsynth, "narrow", axis=0, tiled=True)
+    me = lax.axis_index("narrow")
+    table_y_local = lax.dynamic_slice_in_dim(table_y, me * ny, ny, axis=1)
     ysynth = jnp.einsum(
-        "zcnx,ny->xcyz", xsynth, table_y, preferred_element_type=jnp.float32
+        "zcnx,ny->xcyz", xsynth, table_y_local, preferred_element_type=jnp.float32
     ).astype(jnp.bfloat16)
-    ysynth = lax.all_to_all(ysynth, "narrow", split_axis=2, concat_axis=3, tiled=True)
     ysynth = ysynth.reshape(nx, channels * ny, mode_count)
     grad_hidden = synthesis(hidden_pre, cotangent, ysynth, table_z, skip_weight)
 

time: 193 us -> 203 us (1.052)
  blocking collectives: 33.8 us -> 69.8 us
  local copies, waits for them, and re-layouts: 64.3 us -> 35.6 us
  starting transfers between devices: 27 us -> 3.54 us
  between operations: 0.77 us -> 14.2 us
  matrix products: 2.94 us -> 9.08 us
  waiting for transfers between devices: 29 us -> 35 us
    all_to_all x0 -> x3, blocking collectives: none -> 36 us  [the longest x1 14.4 us: per_device(): lax.all_to_all(ycoeffs, 'wide', split_axis=2, concat_axis=3, tiled=True)]
    all_to_all x3 -> x0, waiting for transfers between devices: 29 us -> none  [the longest x1 15.1 us: per_device(): lax.all_to_all(ysynth, 'narrow', split_axis=2, concat_axis=3, tiled=True)]
    all_gather x0 -> x1, waiting for transfers between devices: none -> 28.5 us  [per_device(): xsynth = lax.all_gather(xsynth, 'narrow', axis=0, tiled=True)]
    all_to_all x3 -> x0, starting transfers between devices: 17.7 us -> none  [the longest x1 7.2 us: per_device(): lax.all_to_all(ycoeffs, 'wide', split_axis=2, concat_axis=3, tiled=True)]
    unnamed x10, local copies, waits for them, and re-layouts: 27.5 us -> 15.2 us
    all_to_all x1 -> x0, local copies, waits for them, and re-layouts: 10.8 us -> none  [per_device(): lax.all_to_all(ysynth, 'narrow', split_axis=2, concat_axis=3, tiled=True)]
    reshape x1 -> x0, local copies, waits for them, and re-layouts: 7.09 us -> none  [per_device(): ysynth = ysynth.reshape(nx, channels * ny, mode_count)]
    all_to_all x2 -> x1, waiting for transfers between devices: 0.01 us -> 6.49 us  [per_device(): total = lax.all_to_all(spread, axis, 0, 0, tiled=True).sum(0, keepdims=True)]
  transfers between devices with their start and end apart: 5 -> 2, of which waited for: 3 -> 2; matrix products, arithmetic and copies ran while one was open for 10% -> 1% of each run, Pallas kernels for 3% -> 0%
where the time goes in v3:
time: 203 us; the launch traced here: 202 us
  blocking collectives  69.8 us (34%)
  local copies, waits for them, and re-layouts  35.6 us (18%)
  waiting for transfers between devices  35 us (17%)
  Pallas kernels  33.6 us (17%)
  between operations  14.2 us (7%)
  matrix products  9.08 us (4%)
  starting transfers between devices  3.54 us (2%)
    all_to_all x1, blocking collectives, per_device(): zc = lax.all_to_all(zc, 'narrow', split_axis=1, concat_axis=3, tiled=True)  33.8 us
    all_gather x1, waiting for transfers between devices, per_device(): xsynth = lax.all_gather(xsynth, 'narrow', axis=0, tiled=True)  28.5 us
    unnamed x10, local copies, waits for them, and re-layouts  15.2 us
    all_to_all x1, blocking collectives, per_device(): lax.all_to_all(ycoeffs, 'wide', split_axis=2, concat_axis=3, tiled=True)  14.4 us
    pallas_call x1, Pallas kernels, synthesis(): pl.pallas_call(synthesis_kernel, grid=(steps,), in_specs=[field_spec, fie...  14.2 us
    pallas_call x1, Pallas kernels, analysis(): pl.pallas_call(analysis_kernel, grid=(steps,), in_specs=[field_spec, fiel...  14.2 us
    all_to_all x1, blocking collectives, per_device(): total = lax.all_to_all(spread, axis, 0, 0, tiled=True).sum(0, keepdims=True)  12.1 us
    all_to_all x1, blocking collectives, per_device(): lax.all_to_all(xsynth, 'wide', split_axis=3, concat_axis=2, tiled=True)  9.5 us
  transfers between devices with their start and end apart: 2, of which 2 were waited for; matrix products, arithmetic and copies ran while one was open for 1% of the time, Pallas kernels for 0%

profile of v3, /device:TPU:1, one launch (start us, length us, event | category | flops | bytes accessed | tf_op | source)
XLA Modules:
  0.0 201.7 jit_solution(18333631063069153565)
XLA Ops:
  7.2 0.0 all-gather.2.cloned.1.call-start
  7.2 0.8 multiply_convert_fusion.tz_ref
  8.0 14.2 %shard_map.67 = (bf16[64,32,512]{2,1,0:T(8,128)(2,1)}, f32[32,32]{1,0:T(8,128)}) custom-call(bf16[32,32,16,256]{3,2,1,0:T(8,128)(2,1)} %h_ref.3, bf16[32,32,16,256]{3,2,1,0:T(8,128)(2,1)} %g_ref.3, bf16[32,256]{1,0:T(8,128)(2,1)} %multiply_convert_fusion.tz_ref), custom_call_target="tpu_custom_call" | custom-call | tf_op jit(solution)/shard_map/pallas_call | solution.py:71
  22.2 5.2 %copy.44 = bf16[64,32,512]{0,2,1:T(8,128)(2,1)} copy(bf16[64,32,512]{2,1,0:T(8,128)(2,1)} %get-tuple-element.7) | data formatting | bytes 4194304 | tf_op jit(solution)/shard_map/pallas_call | solution.py:71
  27.4 6.3 %reshape.60 = bf16[16,2,32768]{2,1,0:T(2,128)(2,1)S(1)} reshape(bf16[32,32,16,64]{3,2,1,0:T(8,128)(2,1)} %bitcast.50) | data formatting | bytes 4194304
  33.7 33.8 %all_to_all.66 = bf16[16,2,32768]{2,1,0:T(2,128)(2,1)} all-to-all(bf16[16,2,32768]{2,1,0:T(2,128)(2,1)S(1)} %reshape.60), channel_id=1, replica_groups=mesh['wide'=8,'narrow'=16] {'narrow'}, dimensions={0} | all-to-all | bytes 4194304 | tf_op jit(solution)/shard_map/all_to_all | solution.py:189
  67.6 7.4 %reshape.61 = bf16[32,32,16,64]{3,2,1,0:T(8,128)(2,1)} reshape(bf16[16,2,32768]{2,1,0:T(2,128)(2,1)} %all_to_all.66) | data formatting | bytes 4194304
  74.9 3.4 %copy.45 = bf16[64,16,2,32,16]{0,4,1,3,2:T(8,128)(2,1)S(1)} copy(bf16[64,16,2,32,16]{0,4,3,2,1:T(8,128)(2,1)} %bitcast.52) | data formatting | bytes 4194304 | tf_op jit(solution)/shard_map/all_to_all | solution.py:189
  78.4 1.0 fusion
  79.3 0.2 copy.65
  79.6 0.0 copy-start.1
  79.6 0.4 reshape.62
  80.0 0.0 copy-start
  80.0 14.4 %all_to_all.67 = bf16[8,2,8192]{2,1,0:T(2,128)(2,1)S(1)} all-to-all(bf16[8,2,8192]{2,1,0:T(2,128)(2,1)S(1)} %reshape.62), channel_id=1, replica_groups=mesh['wide'=8,'narrow'=16] {'wide'}, dimensions={0} | all-to-all | bytes 524288 | tf_op jit(solution)/shard_map/all_to_all | solution.py:193
  94.4 0.3 reshape.63
  94.8 1.0 fusion.9
  95.8 5.2 %shard_map.68 = (f32[256,1024]{1,0:T(8,128)}, bf16[256,32]{1,0:T(8,128)(2,1)}) custom-call(f32[256,64]{1,0:T(8,128)} %bitcast.60, bf16[256,1024]{1,0:T(8,128)(2,1)} %bitcast.61), custom_call_target="tpu_custom_call" | custom-call | tf_op jit(solution)/shard_map/pallas_call | solution.py:166
  100.9 0.9 copy.50
  101.9 0.4 convolution_convert_fusion.1
  102.2 0.3 copy.51
  102.6 0.5 reshape.64
  103.1 9.5 %all_to_all.68 = bf16[8,2,4096]{2,1,0:T(2,128)(2,1)S(1)} all-to-all(bf16[8,2,4096]{2,1,0:T(2,128)(2,1)S(1)} %reshape.64), channel_id=1, replica_groups=mesh['wide'=8,'narrow'=16] {'wide'}, dimensions={0} | all-to-all | bytes 262144 | tf_op jit(solution)/shard_map/all_to_all | solution.py:207
  112.6 0.3 reshape.65
  112.8 1.7 copy.52
  114.6 0.0 all-gather.2.cloned.1.call-update
  114.6 0.0 copy-done.1
  114.6 0.1 broadcast_in_dim.47
  114.7 12.1 %all_to_all.69 = f32[16,1,1024]{2,1,0:T(1,128)S(1)} all-to-all(f32[16,1,1024]{2,1,0:T(1,128)S(1)} %broadcast_in_dim.48), channel_id=1, replica_groups=mesh['wide'=8,'narrow'=16] {'narrow'}, dimensions={0} | all-to-all | bytes 131072 | tf_op jit(solution)/shard_map/all_to_all | solution.py:220
  126.8 0.1 reduce_sum.18
  126.9 0.6 broadcast_in_dim.49
  127.5 3.5 %all-to-all-start.4 = ((f32[8,1,1024]{2,1,0:T(1,128)}), f32[8,1,1024]{2,1,0:T(1,128)S(1)}, u32[]{:S(2)}, u32[]{:S(2)}) async-start(f32[8,1,1024]{2,1,0:T(1,128)} %broadcast_in_dim.49), calls=%async_computation.4 | async-start | bytes 65536 | tf_op jit(solution)/shard_map/all_to_all | solution.py:220
  131.0 6.5 %all-to-all-done.4 = f32[8,1,1024]{2,1,0:T(1,128)S(1)} async-done(((f32[8,1,1024]{2,1,0:T(1,128)}), f32[8,1,1024]{2,1,0:T(1,128)S(1)}, u32[]{:S(2)}, u32[]{:S(2)}) %all-to-all-start.4) | async-done | bytes 32800 | tf_op jit(solution)/shard_map/all_to_all | solution.py:220
  137.5 0.7 mul.107
  138.2 28.5 %all-gather.2.cloned.1.call-done = bf16[32,32,32,32]{3,2,1,0:T(8,128)(2,1)} async-done(((bf16[2,32,32,32]{3,2,1,0:T(8,128)(2,1)}), bf16[32,32,32,32]{3,2,1,0:T(8,128)(2,1)}) %all-gather.2.cloned.1.call-update) | async-done | bytes 2097168 | tf_op jit(solution)/shard_map/all_gather | solution.py:208
  166.7 0.0 copy-done
  166.7 6.8 %convert_bitcast_fusion = bf16[32,32,16,32]{0,2,1,3:T(8,128)(2,1)} fusion(bf16[32,32,32,32]{3,2,1,0:T(8,128)(2,1)} %all-gather.2.cloned.1.call-done, bf16[32,256]{1,0:T(8,128)(2,1)S(1)} %copy-done, s32[]{:T(128)S(6)} %select_n.63), kind=kOutput, calls=%fused_computation | convolution fusion | flops 34078720 | bytes 3153924 | tf_op jit(solution)/shard_map/zcnx,ny->xcyz/dot_general | solution.py:211
  173.5 7.1 %copy.54 = bf16[32,32,16,32]{3,2,1,0:T(8,128)(2,1)} copy(bf16[32,32,16,32]{0,2,1,3:T(8,128)(2,1)} %convert_bitcast_fusion) | data formatting | bytes 2097152 | tf_op jit(solution)/shard_map/convert_element_type | solution.py:213
  180.6 14.2 %shard_map.69 = bf16[32,32,16,256]{3,2,1,0:T(8,128)(2,1)} custom-call(bf16[32,32,16,256]{3,2,1,0:T(8,128)(2,1)} %h_ref.3, bf16[32,32,16,256]{3,2,1,0:T(8,128)(2,1)} %g_ref.3, bf16[32,512,32]{2,1,0:T(8,128)(2,1)} %bitcast.53, bf16[32,256]{1,0:T(8,128)(2,1)} %multiply_convert_fusion.tz_ref, bf16[32,32]{1,0:T(8,128)(2,1)} %sw_ref.1), custom_call_target="tpu_custom_call" | custom-call | tf_op jit(solution)/shard_map/pallas_call | solution.py:124
  (6 shorter events, 0.1 us)
Async XLA Ops:
  7.2 159.6 %all-gather.2.cloned.1.call-start = ((), (), s32[]{:S(2)}) async-start(), calls=%async_computation.5 | async-start | bytes 8912896 | tf_op jit(solution)/shard_map/all_gather | solution.py:208
  79.6 35.0 %copy-start.1 = (f32[32,32]{1,0:T(8,128)S(1)}, f32[32,32]{1,0:T(8,128)}, u32[]{:S(2)}) copy-start(f32[32,32]{1,0:T(8,128)} %get-tuple-element.10) | copy-start | bytes 12292
  80.0 86.8 %copy-start = (bf16[32,256]{1,0:T(8,128)(2,1)S(1)}, bf16[32,256]{1,0:T(8,128)(2,1)}, u32[]{:S(2)}) copy-start(bf16[32,256]{1,0:T(8,128)(2,1)} %multiply_convert_fusion.tz_ref) | copy-start | bytes 49156
  127.5 10.0 %all-to-all-start.4 = ((f32[8,1,1024]{2,1,0:T(1,128)}), f32[8,1,1024]{2,1,0:T(1,128)S(1)}, u32[]{:S(2)}, u32[]{:S(2)}) async-start(f32[8,1,1024]{2,1,0:T(1,128)} %broadcast_in_dim.49), calls=%async_computation.4 | async-start | bytes 65536 | tf_op jit(solution)/shard_map/all_to_all | solution.py:220
Sparse Core Ops, SparseCore 0:
  114.7 51.9 all-gather.1

commit v4 on v2

--- a/solution.py
+++ b/solution.py
@@ -1,3 +1,4 @@
+import functools
 import math
 
 import jax
@@ -28,7 +29,7 @@
     return lax.dot_general(a, b, (((1,), (1,)), ((), ())), preferred_element_type=jnp.float32)
 
 
-def analysis_kernel(h_ref, g_ref, tz_ref, zc_ref, gram_ref, acc_ref):
+def analysis_kernel(h_ref, g_ref, tz_ref, zc_ref, gram_ref, acc_ref, stage_ref):
     step = pl.program_id(0)
     channels, xb, ny, nz = h_ref.shape
 
@@ -43,8 +44,9 @@
     zl = _nt(tz, li.reshape(channels * width, nz))
     zg = _nt(tz, g.reshape(channels * width, nz))
     for c in range(channels):
-        zc_ref[c] = zl[:, c * width:(c + 1) * width].astype(jnp.bfloat16)
-        zc_ref[channels + c] = zg[:, c * width:(c + 1) * width].astype(jnp.bfloat16)
+        stage_ref[:, c, :] = zl[:, c * width:(c + 1) * width]
+        stage_ref[:, channels + c, :] = zg[:, c * width:(c + 1) * width]
+    zc_ref[...] = stage_ref[...].astype(jnp.bfloat16)
     for x in range(xb):
         acc_ref[...] += _nt(li[:, x].reshape(channels * ny, nz), g[:, x].reshape(channels * ny, nz))
 
@@ -73,18 +75,74 @@
         grid=(steps,),
         in_specs=[field_spec, field_spec, pl.BlockSpec((modes, nz), lambda i: (0, 0))],
         out_specs=[
-            pl.BlockSpec((2 * channels, modes, XB * ny), lambda i: (0, 0, i)),
+            pl.BlockSpec((modes, 2 * channels, XB * ny), lambda i: (0, 0, i)),
             pl.BlockSpec((channels, channels), lambda i: (0, 0)),
         ],
         out_shape=[
-            jax.ShapeDtypeStruct((2 * channels, modes, nx * ny), jnp.bfloat16),
+            jax.ShapeDtypeStruct((modes, 2 * channels, nx * ny), jnp.bfloat16),
             jax.ShapeDtypeStruct((channels, channels), jnp.float32),
         ],
-        scratch_shapes=[pltpu.VMEM((channels * ny, channels * ny), jnp.float32)],
+        scratch_shapes=[
+            pltpu.VMEM((channels * ny, channels * ny), jnp.float32),
+            pltpu.VMEM((modes, 2 * channels, XB * ny), jnp.float32),
+        ],
         compiler_params=pltpu.CompilerParams(
             dimension_semantics=("arbitrary",), vmem_limit_bytes=60 * 1024 * 1024
         ),
     )(hidden_pre, cotangent, table_z)
+
+
+def exchange_kernel(axis, count, src_ref, dst_ref, local_sem, send_sems, recv_sems):
+    mesh_ids = pl.DeviceIdType.MESH
+    me = lax.axis_index(axis)
+    barrier = pltpu.get_barrier_semaphore()
+    for k in range(1, count):
+        peer = lax.rem(me + k, count)
+        pl.semaphore_signal(barrier, inc=1, device_id={axis: peer}, device_id_type=mesh_ids)
+    pl.semaphore_wait(barrier, count - 1)
+    local = pltpu.make_async_copy(src_ref.at[me], dst_ref.at[me], local_sem)
+    local.start()
+    sends = []
+    for k in range(1, count):
+        peer = lax.rem(me + k, count)
+        copy = pltpu.make_async_remote_copy(
+            src_ref=src_ref.at[peer],
+            dst_ref=dst_ref.at[me],
+            send_sem=send_sems.at[k],
+            recv_sem=recv_sems.at[k],
+            device_id={axis: peer},
+            device_id_type=mesh_ids,
+        )
+        copy.start()
+        sends.append(copy)
+    local.wait()
+    for k in range(1, count):
+        sends[k - 1].wait_send()
+        origin = lax.rem(me + count - k, count)
+        incoming = pltpu.make_async_remote_copy(
+            src_ref=src_ref.at[me],
+            dst_ref=dst_ref.at[origin],
+            send_sem=send_sems.at[k],
+            recv_sem=recv_sems.at[k],
+            device_id={axis: origin},
+            device_id_type=mesh_ids,
+        )
+        incoming.wait_recv()
+
+
+def exchange(chunks, axis, count, collective_id):
+    return pl.pallas_call(
+        functools.partial(exchange_kernel, axis, count),
+        in_specs=[pl.BlockSpec(memory_space=pl.ANY)],
+        out_specs=pl.BlockSpec(memory_space=pl.ANY),
+        out_shape=jax.ShapeDtypeStruct(chunks.shape, chunks.dtype),
+        scratch_shapes=[
+            pltpu.SemaphoreType.DMA,
+            pltpu.SemaphoreType.DMA((count,)),
+            pltpu.SemaphoreType.DMA((count,)),
+        ],
+        compiler_params=pltpu.CompilerParams(collective_id=collective_id, has_side_effects=True),
+    )(chunks)
 
 
 def synthesis_kernel(h_ref, g_ref, ys_ref, tz_ref, sw_ref, out_ref, ks_ref):
@@ -185,10 +243,13 @@
     table_z = basis_table(mode_count, NZ)
 
     zc, gram = analysis(hidden_pre, cotangent, table_z)
-    zc = zc.reshape(2 * channels, mode_count, nx, ny)
-    zc = lax.all_to_all(zc, "narrow", split_axis=1, concat_axis=3, tiled=True)
+    mz_local = mode_count // n_narrow
+    zc = zc.reshape(n_narrow, mz_local, 2 * channels, nx * ny)
+    zc = exchange(zc, "narrow", n_narrow, 0)
+    zc = zc.reshape(n_narrow, mz_local, 2 * channels, nx, ny)
     ycoeffs = jnp.einsum(
-        "cmxy,ny->mcnx", zc, table_y, preferred_element_type=jnp.float32
+        "smcxl,nsl->mcnx", zc, table_y.reshape(mode_count, n_narrow, ny),
+        preferred_element_type=jnp.float32,
     ).astype(jnp.bfloat16)
     ycoeffs = lax.all_to_all(ycoeffs, "wide", split_axis=2, concat_axis=3, tiled=True)
     spectra = jnp.einsum("zcyx,kx->zykc", ycoeffs, table_x, preferred_element_type=jnp.float32)

time: 193 us -> 183 us (0.948)
  Pallas kernels: 33.6 us -> 72.9 us
  blocking collectives: 33.8 us -> 0 us
  local copies, waits for them, and re-layouts: 64.3 us -> 48.2 us
  starting transfers between devices: 27 us -> 23.8 us
  matrix products: 2.94 us -> 5.62 us
    pallas_call x0 -> x1, Pallas kernels: none -> 38.3 us  [exchange(): pl.pallas_call(functools.partial(exchange_kernel, axis, count), in_specs=...]
    all_to_all x1 -> x0, blocking collectives: 33.8 us -> none  [per_device(): zc = lax.all_to_all(zc, 'narrow', split_axis=1, concat_axis=3, tiled=True)]
    unnamed x10 -> x8, local copies, waits for them, and re-layouts: 27.5 us -> 13.8 us
    reshape x0 -> x1, local copies, waits for them, and re-layouts: none -> 6.22 us  [per_device(): zc = zc.reshape(n_narrow, mz_local, 2 * channels, nx, ny)]
    pallas_call x1 -> x0, local copies, waits for them, and re-layouts: 5.16 us -> none  [analysis(): pl.pallas_call(analysis_kernel, grid=(steps,), in_specs=[field_spec, fiel...]
    all_to_all x1 -> x0, local copies, waits for them, and re-layouts: 3.41 us -> none  [per_device(): zc = lax.all_to_all(zc, 'narrow', split_axis=1, concat_axis=3, tiled=True)]
    dot_general x1, matrix products: 0.96 us -> 3.64 us  [per_device(): jnp.einsum('smcxl,nsl->mcnx', zc, table_y.reshape(mode_count, n_narrow, n...]
    all_to_all x2, starting transfers between devices: 9.28 us -> 6.9 us  [per_device(): total = lax.all_to_all(spread, axis, 0, 0, tiled=True).sum(0, keepdims=True)]
  transfers between devices with their start and end apart: 5 -> 5, of which waited for: 3 -> 3; matrix products, arithmetic and copies ran while one was open for 10% -> 11% of each run, Pallas kernels for 3% -> 3%
where the time goes in v4:
time: 183 us; the launch traced here: 182 us
  Pallas kernels  72.9 us (40%)
  local copies, waits for them, and re-layouts  48.2 us (26%)
  waiting for transfers between devices  29.8 us (16%)
  starting transfers between devices  23.8 us (13%)
  matrix products  5.62 us (3%)
    pallas_call x1, Pallas kernels, exchange(): pl.pallas_call(functools.partial(exchange_kernel, axis, count), in_specs=...  38.3 us
    pallas_call x1, Pallas kernels, analysis(): pl.pallas_call(analysis_kernel, grid=(steps,), in_specs=[field_spec, fiel...  15.2 us
    all_to_all x1, waiting for transfers between devices, per_device(): lax.all_to_all(ysynth, 'narrow', split_axis=2, concat_axis=3, tiled=True)  15.1 us
    pallas_call x1, Pallas kernels, synthesis(): pl.pallas_call(synthesis_kernel, grid=(steps,), in_specs=[field_spec, fie...  14.2 us
    unnamed x8, local copies, waits for them, and re-layouts  13.8 us
    all_to_all x1, local copies, waits for them, and re-layouts, per_device(): lax.all_to_all(ysynth, 'narrow', split_axis=2, concat_axis=3, tiled=True)  10.8 us
    all_to_all x1, waiting for transfers between devices, per_device(): lax.all_to_all(ycoeffs, 'wide', split_axis=2, concat_axis=3, tiled=True)  7.71 us
    all_to_all x1, starting transfers between devices, per_device(): lax.all_to_all(ycoeffs, 'wide', split_axis=2, concat_axis=3, tiled=True)  7.21 us
  transfers between devices with their start and end apart: 5, of which 3 were waited for; matrix products, arithmetic and copies ran while one was open for 11% of the time, Pallas kernels for 3%

profile of v4, /device:TPU:1, one launch (start us, length us, event | category | flops | bytes accessed | tf_op | source)
XLA Modules:
  0.0 182.0 jit_solution(16318349255944972081)
XLA Ops:
  0.7 0.8 multiply_convert_fusion.1.tz_ref
  1.5 15.2 %shard_map.67 = (bf16[32,64,512]{2,1,0:T(8,128)(2,1)}, f32[32,32]{1,0:T(8,128)}) custom-call(bf16[32,32,16,256]{3,2,1,0:T(8,128)(2,1)} %h_ref.3, bf16[32,32,16,256]{3,2,1,0:T(8,128)(2,1)} %g_ref.3, bf16[32,256]{1,0:T(8,128)(2,1)} %multiply_convert_fusion.1.tz_ref), custom_call_target="tpu_custom_call" | custom-call | tf_op jit(solution)/shard_map/pallas_call | solution.py:73
  16.6 38.3 %shard_map.68 = bf16[16,2,64,512]{3,2,1,0:T(8,128)(2,1)} custom-call(bf16[16,2,64,512]{3,2,1,0:T(8,128)(2,1)} %bitcast.67), custom_call_target="tpu_custom_call" | custom-call | tf_op jit(solution)/shard_map/pallas_call | solution.py:134
  55.0 6.2 %copy.82 = bf16[16,2,64,512]{2,0,3,1:T(8,128)(2,1)} copy(bf16[16,2,64,512]{3,2,1,0:T(8,128)(2,1)} %shard_map.68) | data formatting | bytes 4194304 | tf_op jit(solution)/shard_map/reshape | solution.py:249
  61.2 0.0 copy-start
  61.2 3.6 %fusion.2 = bf16[2,64,32,32]{1,2,3,0:T(8,128)(2,1)S(1)} fusion(bf16[16,2,64,32,16]{2,0,4,3,1:T(8,128)(2,1)} %bitcast.62, s32[16,16]{0,1:T(8,128)S(1)} %multiply_add_fusion, s32[32]{0:T(128)S(1)} %add_select_fusion.2, pred[32]{0:T(512)(128)(4,1)S(1)} %iota_compare_fusion), kind=kOutput, calls=%fused_computation.4 | convolution fusion | flops 67379200 | bytes 2360480 | tf_op jit(solution)/shard_map/smcxl,nsl->mcnx/dot_general | solution.py:250
  64.9 0.2 copy.91
  65.1 1.1 reshape.86
  66.2 7.2 %all-to-all-start = ((bf16[8,2,8192]{2,1,0:T(2,128)(2,1)}), bf16[8,2,8192]{2,1,0:T(2,128)(2,1)S(1)}, u32[]{:S(2)}, u32[]{:S(2)}) async-start(bf16[8,2,8192]{2,1,0:T(2,128)(2,1)} %reshape.86), calls=%async_computation | async-start | bytes 524288 | tf_op jit(solution)/shard_map/all_to_all | solution.py:254
  73.4 0.0 copy-done
  73.4 0.1 broadcast_in_dim.48
  73.5 7.7 %all-to-all-done = bf16[8,2,8192]{2,1,0:T(2,128)(2,1)S(1)} async-done(((bf16[8,2,8192]{2,1,0:T(2,128)(2,1)}), bf16[8,2,8192]{2,1,0:T(2,128)(2,1)S(1)}, u32[]{:S(2)}, u32[]{:S(2)}) %all-to-all-start) | async-done | bytes 262176 | tf_op jit(solution)/shard_map/all_to_all | solution.py:254
  81.2 0.7 broadcast_in_dim.49
  81.8 3.4 %all-to-all-start.3 = ((f32[16,1,1024]{2,1,0:T(1,128)}), f32[16,1,1024]{2,1,0:T(1,128)S(1)}, u32[]{:S(2)}, u32[]{:S(2)}) async-start(f32[16,1,1024]{2,1,0:T(1,128)} %broadcast_in_dim.49), calls=%async_computation.3 | async-start | bytes 131072 | tf_op jit(solution)/shard_map/all_to_all | solution.py:279
  85.2 0.3 reshape.87
  85.6 1.0 fusion.26
  86.6 5.2 %shard_map.69 = (f32[256,1024]{1,0:T(8,128)}, bf16[256,32]{1,0:T(8,128)(2,1)}) custom-call(f32[256,64]{1,0:T(8,128)} %bitcast.71, bf16[256,1024]{1,0:T(8,128)(2,1)} %bitcast.72), custom_call_target="tpu_custom_call" | custom-call | tf_op jit(solution)/shard_map/pallas_call | solution.py:224
  91.8 0.9 copy.67
  92.7 0.4 convolution_convert_fusion.1
  93.1 0.3 copy.68
  93.4 1.2 reshape.88
  94.6 0.0 all-to-all-done.3
  94.6 3.4 %all-to-all-start.1 = ((bf16[8,2,4096]{2,1,0:T(2,128)(2,1)}), bf16[8,2,4096]{2,1,0:T(2,128)(2,1)S(1)}, u32[]{:S(2)}, u32[]{:S(2)}) async-start(bf16[8,2,4096]{2,1,0:T(2,128)(2,1)} %reshape.88), calls=%async_computation.1 | async-start | bytes 262144 | tf_op jit(solution)/shard_map/all_to_all | solution.py:268
  98.0 0.1 reduce_sum.18
  98.0 7.0 %all-to-all-done.1 = bf16[8,2,4096]{2,1,0:T(2,128)(2,1)S(1)} async-done(((bf16[8,2,4096]{2,1,0:T(2,128)(2,1)}), bf16[8,2,4096]{2,1,0:T(2,128)(2,1)S(1)}, u32[]{:S(2)}, u32[]{:S(2)}) %all-to-all-start.1) | async-done | bytes 131104 | tf_op jit(solution)/shard_map/all_to_all | solution.py:268
  105.0 0.6 broadcast_in_dim.50
  105.6 3.5 %all-to-all-start.4 = ((f32[8,1,1024]{2,1,0:T(1,128)}), f32[8,1,1024]{2,1,0:T(1,128)S(1)}, u32[]{:S(2)}, u32[]{:S(2)}) async-start(f32[8,1,1024]{2,1,0:T(1,128)} %broadcast_in_dim.50), calls=%async_computation.4 | async-start | bytes 65536 | tf_op jit(solution)/shard_map/all_to_all | solution.py:279
  109.1 0.3 reshape.89
  109.4 0.4 copy.84
  109.8 0.6 fusion
  110.4 6.4 %copy.72 = bf16[32,32,256,2]{0,1,3,2:T(8,128)(2,1)} copy(bf16[32,32,256,2]{2,0,1,3:T(8,128)(2,1)S(1)} %fusion) | data formatting | bytes 2097152 | tf_op jit(solution)/shard_map/convert_element_type | solution.py:271
  116.9 7.4 %reshape.90 = bf16[16,2,16384]{2,1,0:T(2,128)(2,1)} reshape(bf16[256,2,32,32]{3,2,1,0:T(8,128)(2,1)} %bitcast.60) | data formatting | bytes 2097152
  124.3 0.0 all-to-all-done.4
  124.3 6.3 %all-to-all-start.2 = ((bf16[16,2,16384]{2,1,0:T(2,128)(2,1)}), bf16[16,2,16384]{2,1,0:T(2,128)(2,1)S(1)}, u32[]{:S(2)}, u32[]{:S(2)}) async-start(bf16[16,2,16384]{2,1,0:T(2,128)(2,1)} %reshape.90), calls=%async_computation.2 | async-start | bytes 2097152 | tf_op jit(solution)/shard_map/all_to_all | solution.py:272
  130.6 0.7 mul.120
  131.3 15.1 %all-to-all-done.2 = bf16[16,2,16384]{2,1,0:T(2,128)(2,1)S(1)} async-done(((bf16[16,2,16384]{2,1,0:T(2,128)(2,1)}), bf16[16,2,16384]{2,1,0:T(2,128)(2,1)S(1)}, u32[]{:S(2)}, u32[]{:S(2)}) %all-to-all-start.2) | async-done | bytes 1048608 | tf_op jit(solution)/shard_map/all_to_all | solution.py:272
  146.4 3.5 %reshape.91 = bf16[256,2,32,32]{3,2,1,0:T(8,128)(2,1)} reshape(bf16[16,2,16384]{2,1,0:T(2,128)(2,1)S(1)} %all-to-all-done.2) | data formatting | bytes 2097152
  149.9 10.8 %copy.74 = bf16[32,32,16,16,2]{0,2,1,4,3:T(8,128)(2,1)} copy(bf16[32,32,16,16,2]{0,1,4,2,3:T(8,128)(2,1)} %bitcast.61) | data formatting | bytes 2097152 | tf_op jit(solution)/shard_map/all_to_all | solution.py:272
  160.7 7.1 %copy.75.ys_ref = bf16[32,512,32]{2,1,0:T(8,128)(2,1)} copy(bf16[32,512,32]{0,1,2:T(8,128)(2,1)} %bitcast.63) | data formatting | bytes 2097152 | tf_op jit(solution)/shard_map/reshape | solution.py:273
  167.8 14.2 %shard_map.70 = bf16[32,32,16,256]{3,2,1,0:T(8,128)(2,1)} custom-call(bf16[32,32,16,256]{3,2,1,0:T(8,128)(2,1)} %h_ref.3, bf16[32,32,16,256]{3,2,1,0:T(8,128)(2,1)} %g_ref.3, bf16[32,512,32]{2,1,0:T(8,128)(2,1)} %copy.75.ys_ref, bf16[32,256]{1,0:T(8,128)(2,1)} %multiply_convert_fusion.1.tz_ref, bf16[32,32]{1,0:T(8,128)(2,1)} %sw_ref.1), custom_call_target="tpu_custom_call" | custom-call | tf_op jit(solution)/shard_map/pallas_call | solution.py:182
  (6 shorter events, 0.1 us)
Async XLA Ops:
  61.2 12.2 %copy-start = (f32[32,32]{1,0:T(8,128)S(1)}, f32[32,32]{1,0:T(8,128)}, u32[]{:S(2)}) copy-start(f32[32,32]{1,0:T(8,128)} %get-tuple-element.10) | copy-start | bytes 12292
  66.2 15.0 %all-to-all-start = ((bf16[8,2,8192]{2,1,0:T(2,128)(2,1)}), bf16[8,2,8192]{2,1,0:T(2,128)(2,1)S(1)}, u32[]{:S(2)}, u32[]{:S(2)}) async-start(bf16[8,2,8192]{2,1,0:T(2,128)(2,1)} %reshape.86), calls=%async_computation | async-start | bytes 524288 | tf_op jit(solution)/shard_map/all_to_all | solution.py:254
  81.8 12.8 %all-to-all-start.3 = ((f32[16,1,1024]{2,1,0:T(1,128)}), f32[16,1,1024]{2,1,0:T(1,128)S(1)}, u32[]{:S(2)}, u32[]{:S(2)}) async-start(f32[16,1,1024]{2,1,0:T(1,128)} %broadcast_in_dim.49), calls=%async_computation.3 | async-start | bytes 131072 | tf_op jit(solution)/shard_map/all_to_all | solution.py:279
  94.6 10.4 %all-to-all-start.1 = ((bf16[8,2,4096]{2,1,0:T(2,128)(2,1)}), bf16[8,2,4096]{2,1,0:T(2,128)(2,1)S(1)}, u32[]{:S(2)}, u32[]{:S(2)}) async-start(bf16[8,2,4096]{2,1,0:T(2,128)(2,1)} %reshape.88), calls=%async_computation.1 | async-start | bytes 262144 | tf_op jit(solution)/shard_map/all_to_all | solution.py:268
  105.6 18.7 %all-to-all-start.4 = ((f32[8,1,1024]{2,1,0:T(1,128)}), f32[8,1,1024]{2,1,0:T(1,128)S(1)}, u32[]{:S(2)}, u32[]{:S(2)}) async-start(f32[8,1,1024]{2,1,0:T(1,128)} %broadcast_in_dim.50), calls=%async_computation.4 | async-start | bytes 65536 | tf_op jit(solution)/shard_map/all_to_all | solution.py:279
  124.3 22.2 %all-to-all-start.2 = ((bf16[16,2,16384]{2,1,0:T(2,128)(2,1)}), bf16[16,2,16384]{2,1,0:T(2,128)(2,1)S(1)}, u32[]{:S(2)}, u32[]{:S(2)}) async-start(bf16[16,2,16384]{2,1,0:T(2,128)(2,1)} %reshape.90), calls=%async_computation.2 | async-start | bytes 2097152 | tf_op jit(solution)/shard_map/all_to_all | solution.py:272

commit v5 on v4

--- a/solution.py
+++ b/solution.py
@@ -165,8 +165,12 @@
 
     tz = tz_ref[...]
     ks = ks_ref[...]
+    ys = ys_ref[...].astype(jnp.float32)
     for x in range(xb):
-        spec = jnp.dot(ys_ref[x], tz, preferred_element_type=jnp.float32)
+        lo = ys[:, 2 * x, :]
+        hi = ys[:, 2 * x + 1, :]
+        lhs = jnp.concatenate([lo, hi], axis=0).T.astype(jnp.bfloat16)
+        spec = jnp.dot(lhs, tz, preferred_element_type=jnp.float32)
         spec = spec.astype(jnp.bfloat16).astype(jnp.float32)
         skip = jnp.dot(ks, g_ref[:, x].reshape(channels * ny, nz), preferred_element_type=jnp.float32)
         activ = jnp.tanh(h_ref[:, x].astype(jnp.float32)).reshape(channels * ny, nz)
@@ -185,7 +189,7 @@
         in_specs=[
             field_spec,
             field_spec,
-            pl.BlockSpec((XB, channels * ny, modes), lambda i: (i, 0, 0)),
+            pl.BlockSpec((ysynth.shape[0], 2 * XB, channels * ny), lambda i: (0, i, 0)),
             pl.BlockSpec((modes, nz), lambda i: (0, 0)),
             pl.BlockSpec((channels, channels), lambda i: (0, 0)),
         ],
@@ -267,11 +271,13 @@
     ).astype(jnp.bfloat16)
     xsynth = lax.all_to_all(xsynth, "wide", split_axis=3, concat_axis=2, tiled=True)
     ysynth = jnp.einsum(
-        "zcnx,ny->xcyz", xsynth, table_y, preferred_element_type=jnp.float32
+        "zcnx,ndy->dxzcy", xsynth, table_y.reshape(mode_count, n_narrow, ny),
+        preferred_element_type=jnp.float32,
     ).astype(jnp.bfloat16)
-    ysynth = lax.all_to_all(ysynth, "narrow", split_axis=2, concat_axis=3, tiled=True)
-    ysynth = ysynth.reshape(nx, channels * ny, mode_count)
-    grad_hidden = synthesis(hidden_pre, cotangent, ysynth, table_z, skip_weight)
+    ysynth = ysynth.reshape(n_narrow, nx * mz_local, channels * ny)
+    ysynth = exchange(ysynth, "narrow", n_narrow, 1)
+    table_zp = jnp.transpose(table_z.reshape(n_narrow, mz_local, nz), (1, 0, 2)).reshape(mode_count, nz)
+    grad_hidden = synthesis(hidden_pre, cotangent, ysynth, table_zp, skip_weight)
 
     total = gram.reshape(1, channels * channels)
     for axis, count in (("narrow", n_narrow), ("wide", n_wide)):

time: 183 us -> 185 us (1.011)
  Pallas kernels: 72.9 us -> 90.7 us
  waiting for transfers between devices: 29.8 us -> 18.7 us
  local copies, waits for them, and re-layouts: 48.2 us -> 42.4 us
  matrix products: 5.62 us -> 8.69 us
  starting transfers between devices: 23.8 us -> 21.3 us
    pallas_call x1 -> x2, Pallas kernels: 38.3 us -> 56.2 us  [exchange(): pl.pallas_call(functools.partial(exchange_kernel, axis, count), in_specs=...]
    all_to_all x1 -> x0, waiting for transfers between devices: 15.1 us -> none  [per_device(): lax.all_to_all(ysynth, 'narrow', split_axis=2, concat_axis=3, tiled=True)]
    unnamed x8 -> x4, local copies, waits for them, and re-layouts: 13.8 us -> 2.86 us
    all_to_all x1 -> x0, local copies, waits for them, and re-layouts: 10.8 us -> none  [per_device(): lax.all_to_all(ysynth, 'narrow', split_axis=2, concat_axis=3, tiled=True)]
    convert_element_type x1, local copies, waits for them, and re-layouts: 6.45 us -> 14.2 us  [per_device(): ysynth = jnp.einsum('zcnx,ndy->dxzcy', xsynth, table_y.reshape(mode_count...]
    all_to_all x2, starting transfers between devices: 6.9 us -> 14.4 us  [per_device(): total = lax.all_to_all(spread, axis, 0, 0, tiled=True).sum(0, keepdims=True)]
    all_to_all x1 -> x0, starting transfers between devices: 6.3 us -> none  [per_device(): lax.all_to_all(ysynth, 'narrow', split_axis=2, concat_axis=3, tiled=True)]
    all_to_all x2, waiting for transfers between devices: 0.01 us -> 5.26 us  [per_device(): total = lax.all_to_all(spread, axis, 0, 0, tiled=True).sum(0, keepdims=True)]
  transfers between devices with their start and end apart: 5 -> 4, of which waited for: 3 -> 3; matrix products, arithmetic and copies ran while one was open for 11% -> 6% of each run, Pallas kernels for 3% -> 20%
where the time goes in v5:
time: 185 us; the launch traced here: 184 us
  Pallas kernels  90.7 us (49%)
  local copies, waits for them, and re-layouts  42.4 us (23%)
  starting transfers between devices  21.3 us (12%)
  waiting for transfers between devices  18.7 us (10%)
  matrix products  8.69 us (5%)
    pallas_call x2, Pallas kernels, exchange(): pl.pallas_call(functools.partial(exchange_kernel, axis, count), in_specs=...  56.2 us
    pallas_call x1, Pallas kernels, analysis(): pl.pallas_call(analysis_kernel, grid=(steps,), in_specs=[field_spec, fiel...  15.2 us
    reshape x1, local copies, waits for them, and re-layouts, per_device(): ysynth = ysynth.reshape(n_narrow, nx * mz_local, channels * ny)  15.1 us
    all_to_all x2, starting transfers between devices, per_device(): total = lax.all_to_all(spread, axis, 0, 0, tiled=True).sum(0, keepdims=True)  14.4 us
    convert_element_type x1, local copies, waits for them, and re-layouts, per_device(): ysynth = jnp.einsum('zcnx,ndy->dxzcy', xsynth, table_y.reshape(mode_count...  14.2 us
    pallas_call x1, Pallas kernels, synthesis(): pl.pallas_call(synthesis_kernel, grid=(steps,), in_specs=[field_spec, fie...  14.1 us
    all_to_all x1, waiting for transfers between devices, per_device(): lax.all_to_all(ycoeffs, 'wide', split_axis=2, concat_axis=3, tiled=True)  7.47 us
    all_to_all x1, waiting for transfers between devices, per_device(): lax.all_to_all(xsynth, 'wide', split_axis=3, concat_axis=2, tiled=True)  5.96 us
  transfers between devices with their start and end apart: 4, of which 3 were waited for; matrix products, arithmetic and copies ran while one was open for 6% of the time, Pallas kernels for 20%

profile of v5, /device:TPU:1, one launch (start us, length us, event | category | flops | bytes accessed | tf_op | source)
XLA Modules:
  0.0 184.4 jit_solution(12586095194022882887)
XLA Ops:
  0.7 0.8 multiply_convert_fusion.2.tz_ref
  1.5 15.2 %shard_map.67 = (bf16[32,64,512]{2,1,0:T(8,128)(2,1)}, f32[32,32]{1,0:T(8,128)}) custom-call(bf16[32,32,16,256]{3,2,1,0:T(8,128)(2,1)} %h_ref.3, bf16[32,32,16,256]{3,2,1,0:T(8,128)(2,1)} %g_ref.3, bf16[32,256]{1,0:T(8,128)(2,1)} %multiply_convert_fusion.2.tz_ref), custom_call_target="tpu_custom_call" | custom-call | tf_op jit(solution)/shard_map/pallas_call | solution.py:73
  16.6 0.8 broadcast_in_dim.49
  17.4 0.7 broadcast_in_dim.50
  18.1 7.2 %all-to-all-start.2 = ((f32[16,1,1024]{2,1,0:T(1,128)}), f32[16,1,1024]{2,1,0:T(1,128)S(1)}, u32[]{:S(2)}, u32[]{:S(2)}) async-start(f32[16,1,1024]{2,1,0:T(1,128)} %broadcast_in_dim.50), calls=%async_computation.2 | async-start | bytes 131072 | tf_op jit(solution)/shard_map/all_to_all | solution.py:285
  25.3 37.1 %shard_map.68 = bf16[16,2,64,512]{3,2,1,0:T(8,128)(2,1)} custom-call(bf16[16,2,64,512]{3,2,1,0:T(8,128)(2,1)} %bitcast.66), custom_call_target="tpu_custom_call" | custom-call | tf_op jit(solution)/shard_map/pallas_call | solution.py:134
  62.4 4.8 %copy.39 = bf16[16,2,64,512]{2,3,1,0:T(8,128)(2,1)} copy(bf16[16,2,64,512]{3,2,1,0:T(8,128)(2,1)} %shard_map.68) | data formatting | bytes 4194304 | tf_op jit(solution)/shard_map/pallas_call | solution.py:134
  67.1 3.6 %fusion.1 = bf16[2,64,32,32]{1,2,3,0:T(8,128)(2,1)S(1)} fusion(bf16[16,2,64,32,16]{2,4,3,1,0:T(8,128)(2,1)} %bitcast.62, s32[16,16]{1,0:T(8,128)S(1)} %multiply_add_fusion, s32[32]{0:T(128)S(1)} %add_select_fusion.4, pred[32]{0:T(512)(128)(4,1)S(1)} %iota_compare_fusion), kind=kOutput, calls=%fused_computation.3 | convolution fusion | flops 67379200 | bytes 2360480 | tf_op jit(solution)/shard_map/smcxl,nsl->mcnx/dot_general | solution.py:254
  70.8 0.1 iota.97
  70.9 0.0 all-to-all-done.2
  70.9 0.1 reduce_sum.18
  70.9 0.6 broadcast_in_dim.51
  71.6 7.2 %all-to-all-start.3 = ((f32[8,1,1024]{2,1,0:T(1,128)}), f32[8,1,1024]{2,1,0:T(1,128)S(1)}, u32[]{:S(2)}, u32[]{:S(2)}) async-start(f32[8,1,1024]{2,1,0:T(1,128)} %broadcast_in_dim.51), calls=%async_computation.3 | async-start | bytes 65536 | tf_op jit(solution)/shard_map/all_to_all | solution.py:285
  78.8 0.2 copy.58
  79.0 1.1 reshape.137
  80.1 5.3 %all-to-all-done.3 = f32[8,1,1024]{2,1,0:T(1,128)S(1)} async-done(((f32[8,1,1024]{2,1,0:T(1,128)}), f32[8,1,1024]{2,1,0:T(1,128)S(1)}, u32[]{:S(2)}, u32[]{:S(2)}) %all-to-all-start.3) | async-done | bytes 32800 | tf_op jit(solution)/shard_map/all_to_all | solution.py:285
  85.3 3.4 %all-to-all-start = ((bf16[8,2,8192]{2,1,0:T(2,128)(2,1)}), bf16[8,2,8192]{2,1,0:T(2,128)(2,1)S(1)}, u32[]{:S(2)}, u32[]{:S(2)}) async-start(bf16[8,2,8192]{2,1,0:T(2,128)(2,1)} %reshape.137), calls=%async_computation | async-start | bytes 524288 | tf_op jit(solution)/shard_map/all_to_all | solution.py:258
  88.8 0.8 multiply_convert_fusion.1.tz_ref
  89.6 7.5 %all-to-all-done = bf16[8,2,8192]{2,1,0:T(2,128)(2,1)S(1)} async-done(((bf16[8,2,8192]{2,1,0:T(2,128)(2,1)}), bf16[8,2,8192]{2,1,0:T(2,128)(2,1)S(1)}, u32[]{:S(2)}, u32[]{:S(2)}) %all-to-all-start) | async-done | bytes 262176 | tf_op jit(solution)/shard_map/all_to_all | solution.py:258
  97.1 0.3 reshape.138
  97.5 1.0 fusion.28
  98.5 5.2 %shard_map.69 = (f32[256,1024]{1,0:T(8,128)}, bf16[256,32]{1,0:T(8,128)(2,1)}) custom-call(f32[256,64]{1,0:T(8,128)} %bitcast.70, bf16[256,1024]{1,0:T(8,128)(2,1)} %bitcast.71), custom_call_target="tpu_custom_call" | custom-call | tf_op jit(solution)/shard_map/pallas_call | solution.py:228
  103.6 0.9 copy.44
  104.6 0.4 convolution_convert_fusion
  104.9 0.3 copy.45
  105.3 1.2 reshape.139
  106.4 3.6 %all-to-all-start.1 = ((bf16[8,2,4096]{2,1,0:T(2,128)(2,1)}), bf16[8,2,4096]{2,1,0:T(2,128)(2,1)S(1)}, u32[]{:S(2)}, u32[]{:S(2)}) async-start(bf16[8,2,4096]{2,1,0:T(2,128)(2,1)} %reshape.139), calls=%async_computation.1 | async-start | bytes 262144 | tf_op jit(solution)/shard_map/all_to_all | solution.py:272
  110.0 0.7 mul.150
  110.7 6.0 %all-to-all-done.1 = bf16[8,2,4096]{2,1,0:T(2,128)(2,1)S(1)} async-done(((bf16[8,2,4096]{2,1,0:T(2,128)(2,1)}), bf16[8,2,4096]{2,1,0:T(2,128)(2,1)S(1)}, u32[]{:S(2)}, u32[]{:S(2)}) %all-to-all-start.1) | async-done | bytes 131104 | tf_op jit(solution)/shard_map/all_to_all | solution.py:272
  116.6 0.3 reshape.140
  116.9 1.1 copy.46
  118.0 3.7 %convert_bitcast_fusion = bf16[16,32,2,32,16]{1,4,3,2,0:T(8,128)(2,1)} fusion(bf16[2,32,32,32,1]{3,2,1,0,4:T(8,128)(2,1)S(1)} %bitcast.69, s32[16,16]{1,0:T(8,128)S(1)} %multiply_add_fusion, s32[32]{0:T(128)S(1)} %add_select_fusion.4, pred[32]{0:T(512)(128)(4,1)S(1)} %iota_compare_fusion), kind=kOutput, calls=%fused_computation | convolution fusion | flops 34217984 | bytes 1180832 | tf_op jit(solution)/shard_map/zcnx,ndy->dxzcy/dot_general | solution.py:273
  121.7 14.2 %copy.47 = bf16[16,32,2,32,16]{4,3,2,1,0:T(8,128)(2,1)} copy(bf16[16,32,2,32,16]{1,4,3,2,0:T(8,128)(2,1)} %convert_bitcast_fusion) | data formatting | bytes 2097152 | tf_op jit(solution)/shard_map/convert_element_type | solution.py:276
  136.0 15.1 %reshape.131.src_ref = bf16[16,64,512]{2,1,0:T(8,128)(2,1)} reshape(bf16[16,32,2,32,16]{4,3,2,1,0:T(8,128)(2,1)} %copy.47) | data formatting | bytes 2097152 | tf_op jit(solution)/shard_map/reshape | solution.py:277
  151.1 19.1 %shard_map.70.ys_ref = bf16[16,64,512]{2,1,0:T(8,128)(2,1)} custom-call(bf16[16,64,512]{2,1,0:T(8,128)(2,1)} %reshape.131.src_ref), custom_call_target="tpu_custom_call" | custom-call | tf_op jit(solution)/shard_map/pallas_call | solution.py:134
  170.3 14.1 %shard_map.71 = bf16[32,32,16,256]{3,2,1,0:T(8,128)(2,1)} custom-call(bf16[32,32,16,256]{3,2,1,0:T(8,128)(2,1)} %h_ref.3, bf16[32,32,16,256]{3,2,1,0:T(8,128)(2,1)} %g_ref.3, bf16[16,64,512]{2,1,0:T(8,128)(2,1)} %shard_map.70.ys_ref, bf16[32,256]{1,0:T(8,128)(2,1)} %multiply_convert_fusion.1.tz_ref, bf16[32,32]{1,0:T(8,128)(2,1)} %sw_ref.1), custom_call_target="tpu_custom_call" | custom-call | tf_op jit(solution)/shard_map/pallas_call | solution.py:186
  (9 shorter events, 0.1 us)
Async XLA Ops:
  18.1 52.8 %all-to-all-start.2 = ((f32[16,1,1024]{2,1,0:T(1,128)}), f32[16,1,1024]{2,1,0:T(1,128)S(1)}, u32[]{:S(2)}, u32[]{:S(2)}) async-start(f32[16,1,1024]{2,1,0:T(1,128)} %broadcast_in_dim.50), calls=%async_computation.2 | async-start | bytes 131072 | tf_op jit(solution)/shard_map/all_to_all | solution.py:285
  71.6 13.8 %all-to-all-start.3 = ((f32[8,1,1024]{2,1,0:T(1,128)}), f32[8,1,1024]{2,1,0:T(1,128)S(1)}, u32[]{:S(2)}, u32[]{:S(2)}) async-start(f32[8,1,1024]{2,1,0:T(1,128)} %broadcast_in_dim.51), calls=%async_computation.3 | async-start | bytes 65536 | tf_op jit(solution)/shard_map/all_to_all | solution.py:285
  85.3 11.7 %all-to-all-start = ((bf16[8,2,8192]{2,1,0:T(2,128)(2,1)}), bf16[8,2,8192]{2,1,0:T(2,128)(2,1)S(1)}, u32[]{:S(2)}, u32[]{:S(2)}) async-start(bf16[8,2,8192]{2,1,0:T(2,128)(2,1)} %reshape.137), calls=%async_computation | async-start | bytes 524288 | tf_op jit(solution)/shard_map/all_to_all | solution.py:258
  106.4 10.2 %all-to-all-start.1 = ((bf16[8,2,4096]{2,1,0:T(2,128)(2,1)}), bf16[8,2,4096]{2,1,0:T(2,128)(2,1)S(1)}, u32[]{:S(2)}, u32[]{:S(2)}) async-start(bf16[8,2,4096]{2,1,0:T(2,128)(2,1)} %reshape.139), calls=%async_computation.1 | async-start | bytes 262144 | tf_op jit(solution)/shard_map/all_to_all | solution.py:272

commit v6 on v5

--- a/solution.py
+++ b/solution.py
@@ -202,6 +202,41 @@
     )(hidden_pre, cotangent, ysynth, table_z, skip_weight)
 
 
+def y_synthesis_kernel(xs_ref, tyt_ref, out_ref, stage_ref):
+    mz_local, channels, modes, nx = xs_ref.shape
+    blocks, _, lanes = out_ref.shape
+    ny = lanes // channels
+    tyt = jnp.broadcast_to(tyt_ref[...][None], (channels,) + tyt_ref.shape)
+    for z in range(mz_local):
+        part = jnp.einsum(
+            "cym,cmx->cyx", tyt, xs_ref[z], preferred_element_type=jnp.float32
+        ).astype(jnp.bfloat16).astype(jnp.float32)
+        for d in range(blocks):
+            piece = part[:, d * ny:(d + 1) * ny, :].reshape(channels * ny, nx).T
+            for q in range(lanes // 128):
+                stage_ref[d * (lanes // 128) + q, pl.ds(z, nx, stride=mz_local), :] = (
+                    piece[:, q * 128:(q + 1) * 128])
+    for d in range(blocks):
+        for q in range(lanes // 128):
+            out_ref[d, :, q * 128:(q + 1) * 128] = (
+                stage_ref[d * (lanes // 128) + q].astype(out_ref.dtype))
+
+
+def y_synthesis(xsynth, table_yt, blocks):
+    mz_local, channels, modes, nx = xsynth.shape
+    ny = table_yt.shape[0] // blocks
+    vmem = pl.BlockSpec(memory_space=pltpu.VMEM)
+    return pl.pallas_call(
+        y_synthesis_kernel,
+        in_specs=[vmem, vmem],
+        out_specs=vmem,
+        out_shape=jax.ShapeDtypeStruct((blocks, nx * mz_local, channels * ny), jnp.bfloat16),
+        scratch_shapes=[
+            pltpu.VMEM((blocks * channels * ny // 128, nx * mz_local, 128), jnp.float32)
+        ],
+    )(xsynth, table_yt)
+
+
 def modes_kernel(sp_ref, w_ref, gm_ref, bs_ref):
     highest = lax.Precision.HIGHEST
     channels = sp_ref.shape[1] // 2
@@ -270,11 +305,7 @@
         "zcyk,kx->zcyx", back_spec, table_x, preferred_element_type=jnp.float32
     ).astype(jnp.bfloat16)
     xsynth = lax.all_to_all(xsynth, "wide", split_axis=3, concat_axis=2, tiled=True)
-    ysynth = jnp.einsum(
-        "zcnx,ndy->dxzcy", xsynth, table_y.reshape(mode_count, n_narrow, ny),
-        preferred_element_type=jnp.float32,
-    ).astype(jnp.bfloat16)
-    ysynth = ysynth.reshape(n_narrow, nx * mz_local, channels * ny)
+    ysynth = y_synthesis(xsynth, jnp.transpose(table_y), n_narrow)
     ysynth = exchange(ysynth, "narrow", n_narrow, 1)
     table_zp = jnp.transpose(table_z.reshape(n_narrow, mz_local, nz), (1, 0, 2)).reshape(mode_count, nz)
     grad_hidden = synthesis(hidden_pre, cotangent, ysynth, table_zp, skip_weight)

time: 185 us -> 158 us (0.85)
  local copies, waits for them, and re-layouts: 42.4 us -> 15.1 us
  Pallas kernels: 90.7 us -> 94.6 us
  matrix products: 8.69 us -> 4.98 us
    convert_element_type x1 -> x0, local copies, waits for them, and re-layouts: 14.2 us -> none  [per_device(): ysynth = jnp.einsum('zcnx,ndy->dxzcy', xsynth, table_y.reshape(mode_count...]
    reshape x1, local copies, waits for them, and re-layouts: 15.1 us -> 6.22 us  [per_device(): zc = zc.reshape(n_narrow, mz_local, 2 * channels, nx, ny)]
    pallas_call x1 -> x0, local copies, waits for them, and re-layouts: 4.75 us -> none  [exchange(): pl.pallas_call(functools.partial(exchange_kernel, axis, count), in_specs=...]
    pallas_call x0 -> x1, Pallas kernels: none -> 3.92 us  [y_synthesis(): pl.pallas_call(y_synthesis_kernel, in_specs=[vmem, vmem], out_specs=vmem,...]
    dot_general x1 -> x0, matrix products: 3.71 us -> none  [per_device(): jnp.einsum('zcnx,ndy->dxzcy', xsynth, table_y.reshape(mode_count, n_narro...]
  transfers between devices with their start and end apart: 4 -> 4, of which waited for: 3 -> 3; matrix products, arithmetic and copies ran while one was open for 6% -> 9% of each run, Pallas kernels for 20% -> 24%
where the time goes in v6:
time: 158 us; the launch traced here: 157 us
  Pallas kernels  94.6 us (60%)
  starting transfers between devices  21.3 us (13%)
  waiting for transfers between devices  17.5 us (11%)
  local copies, waits for them, and re-layouts  15.1 us (10%)
  matrix products  4.98 us (3%)
  other arithmetic  2.94 us (2%)
    pallas_call x2, Pallas kernels, exchange(): pl.pallas_call(functools.partial(exchange_kernel, axis, count), in_specs=...  56.2 us
    pallas_call x1, Pallas kernels, analysis(): pl.pallas_call(analysis_kernel, grid=(steps,), in_specs=[field_spec, fiel...  15.2 us
    all_to_all x2, starting transfers between devices, per_device(): total = lax.all_to_all(spread, axis, 0, 0, tiled=True).sum(0, keepdims=True)  14.4 us
    pallas_call x1, Pallas kernels, synthesis(): pl.pallas_call(synthesis_kernel, grid=(steps,), in_specs=[field_spec, fie...  14.1 us
    all_to_all x1, waiting for transfers between devices, per_device(): lax.all_to_all(ycoeffs, 'wide', split_axis=2, concat_axis=3, tiled=True)  6.31 us
    reshape x1, local copies, waits for them, and re-layouts, per_device(): zc = zc.reshape(n_narrow, mz_local, 2 * channels, nx, ny)  6.22 us
    all_to_all x1, waiting for transfers between devices, per_device(): lax.all_to_all(xsynth, 'wide', split_axis=3, concat_axis=2, tiled=True)  5.96 us
    all_to_all x2, waiting for transfers between devices, per_device(): total = lax.all_to_all(spread, axis, 0, 0, tiled=True).sum(0, keepdims=True)  5.26 us
  transfers between devices with their start and end apart: 4, of which 3 were waited for; matrix products, arithmetic and copies ran while one was open for 9% of the time, Pallas kernels for 24%

profile of v6, /device:TPU:1, one launch (start us, length us, event | category | flops | bytes accessed | tf_op | source)
XLA Modules:
  0.0 157.3 jit_solution(2922199313917283248)
XLA Ops:
  0.7 0.8 multiply_convert_fusion.3.tz_ref
  1.5 15.2 %shard_map.67 = (bf16[32,64,512]{2,1,0:T(8,128)(2,1)}, f32[32,32]{1,0:T(8,128)}) custom-call(bf16[32,32,16,256]{3,2,1,0:T(8,128)(2,1)} %h_ref.3, bf16[32,32,16,256]{3,2,1,0:T(8,128)(2,1)} %g_ref.3, bf16[32,256]{1,0:T(8,128)(2,1)} %multiply_convert_fusion.3.tz_ref), custom_call_target="tpu_custom_call" | custom-call | tf_op jit(solution)/shard_map/pallas_call | solution.py:73
  16.6 0.8 broadcast_in_dim.50
  17.4 0.7 broadcast_in_dim.51
  18.1 7.2 %all-to-all-start.2 = ((f32[16,1,1024]{2,1,0:T(1,128)}), f32[16,1,1024]{2,1,0:T(1,128)S(1)}, u32[]{:S(2)}, u32[]{:S(2)}) async-start(f32[16,1,1024]{2,1,0:T(1,128)} %broadcast_in_dim.51), calls=%async_computation.2 | async-start | bytes 131072 | tf_op jit(solution)/shard_map/all_to_all | solution.py:316
  25.3 0.1 iota.94
  25.4 37.0 %shard_map.68 = bf16[16,2,64,512]{3,2,1,0:T(8,128)(2,1)} custom-call(bf16[16,2,64,512]{3,2,1,0:T(8,128)(2,1)} %bitcast.54), custom_call_target="tpu_custom_call" | custom-call | tf_op jit(solution)/shard_map/pallas_call | solution.py:134
  62.4 6.2 %copy.47 = bf16[16,2,64,512]{2,0,3,1:T(8,128)(2,1)} copy(bf16[16,2,64,512]{3,2,1,0:T(8,128)(2,1)} %shard_map.68) | data formatting | bytes 4194304 | tf_op jit(solution)/shard_map/reshape | solution.py:288
  68.6 3.6 %fusion.1 = bf16[2,64,32,32]{1,2,3,0:T(8,128)(2,1)S(1)} fusion(bf16[16,2,64,32,16]{2,0,4,3,1:T(8,128)(2,1)} %bitcast.49, s32[16,16]{0,1:T(8,128)S(1)} %multiply_add_fusion, s32[32]{0:T(128)S(1)} %add_select_fusion.5, pred[32]{0:T(512)(128)(4,1)S(1)} %iota_compare_fusion), kind=kOutput, calls=%fused_computation.2 | convolution fusion | flops 67379200 | bytes 2360480 | tf_op jit(solution)/shard_map/smcxl,nsl->mcnx/dot_general | solution.py:289
  72.3 0.0 all-to-all-done.2
  72.3 0.1 reduce_sum.18
  72.3 0.6 broadcast_in_dim.52
  73.0 7.2 %all-to-all-start.3 = ((f32[8,1,1024]{2,1,0:T(1,128)}), f32[8,1,1024]{2,1,0:T(1,128)S(1)}, u32[]{:S(2)}, u32[]{:S(2)}) async-start(f32[8,1,1024]{2,1,0:T(1,128)} %broadcast_in_dim.52), calls=%async_computation.3 | async-start | bytes 65536 | tf_op jit(solution)/shard_map/all_to_all | solution.py:316
  80.2 0.2 copy.51
  80.4 1.1 reshape.110
  81.5 5.3 %all-to-all-done.3 = f32[8,1,1024]{2,1,0:T(1,128)S(1)} async-done(((f32[8,1,1024]{2,1,0:T(1,128)}), f32[8,1,1024]{2,1,0:T(1,128)S(1)}, u32[]{:S(2)}, u32[]{:S(2)}) %all-to-all-start.3) | async-done | bytes 32800 | tf_op jit(solution)/shard_map/all_to_all | solution.py:316
  86.8 3.4 %all-to-all-start = ((bf16[8,2,8192]{2,1,0:T(2,128)(2,1)}), bf16[8,2,8192]{2,1,0:T(2,128)(2,1)S(1)}, u32[]{:S(2)}, u32[]{:S(2)}) async-start(bf16[8,2,8192]{2,1,0:T(2,128)(2,1)} %reshape.110), calls=%async_computation | async-start | bytes 524288 | tf_op jit(solution)/shard_map/all_to_all | solution.py:293
  90.2 0.8 multiply_convert_fusion.2.tz_ref
  91.0 1.2 multiply_convert_fusion.tyt_ref
  92.2 6.3 %all-to-all-done = bf16[8,2,8192]{2,1,0:T(2,128)(2,1)S(1)} async-done(((bf16[8,2,8192]{2,1,0:T(2,128)(2,1)}), bf16[8,2,8192]{2,1,0:T(2,128)(2,1)S(1)}, u32[]{:S(2)}, u32[]{:S(2)}) %all-to-all-start) | async-done | bytes 262176 | tf_op jit(solution)/shard_map/all_to_all | solution.py:293
  98.5 0.3 reshape.111
  98.9 1.0 fusion.35
  99.9 5.2 %shard_map.69 = (f32[256,1024]{1,0:T(8,128)}, bf16[256,32]{1,0:T(8,128)(2,1)}) custom-call(f32[256,64]{1,0:T(8,128)} %bitcast.57, bf16[256,1024]{1,0:T(8,128)(2,1)} %bitcast.58), custom_call_target="tpu_custom_call" | custom-call | tf_op jit(solution)/shard_map/pallas_call | solution.py:263
  105.0 0.9 copy.38
  106.0 0.4 convolution_convert_fusion
  106.4 0.3 copy.39
  106.7 1.2 reshape.112
  107.8 3.6 %all-to-all-start.1 = ((bf16[8,2,4096]{2,1,0:T(2,128)(2,1)}), bf16[8,2,4096]{2,1,0:T(2,128)(2,1)S(1)}, u32[]{:S(2)}, u32[]{:S(2)}) async-start(bf16[8,2,4096]{2,1,0:T(2,128)(2,1)} %reshape.112), calls=%async_computation.1 | async-start | bytes 262144 | tf_op jit(solution)/shard_map/all_to_all | solution.py:307
  111.4 0.7 mul.142
  112.1 6.0 %all-to-all-done.1 = bf16[8,2,4096]{2,1,0:T(2,128)(2,1)S(1)} async-done(((bf16[8,2,4096]{2,1,0:T(2,128)(2,1)}), bf16[8,2,4096]{2,1,0:T(2,128)(2,1)S(1)}, u32[]{:S(2)}, u32[]{:S(2)}) %all-to-all-start.1) | async-done | bytes 131104 | tf_op jit(solution)/shard_map/all_to_all | solution.py:307
  118.1 0.3 reshape.113
  118.3 1.7 %copy.40 = bf16[2,32,4,8,32]{4,2,3,1,0:T(4,128)(2,1)} copy(bf16[2,32,4,8,32]{1,2,0,4,3:T(4,128)(2,1)S(1)} %bitcast.53) | data formatting | bytes 262144 | tf_op jit(solution)/shard_map/all_to_all | solution.py:307
  120.0 3.9 %shard_map.70.src_ref = bf16[16,64,512]{2,1,0:T(8,128)(2,1)} custom-call(bf16[2,32,32,32]{3,2,1,0:T(8,128)(2,1)} %bitcast.50, bf16[256,32]{1,0:T(8,128)(2,1)} %multiply_convert_fusion.tyt_ref), custom_call_target="tpu_custom_call" | custom-call | tf_op jit(solution)/shard_map/pallas_call | solution.py:229
  124.0 19.2 %shard_map.71.ys_ref = bf16[16,64,512]{2,1,0:T(8,128)(2,1)} custom-call(bf16[16,64,512]{2,1,0:T(8,128)(2,1)} %shard_map.70.src_ref), custom_call_target="tpu_custom_call" | custom-call | tf_op jit(solution)/shard_map/pallas_call | solution.py:134
  143.1 14.1 %shard_map.72 = bf16[32,32,16,256]{3,2,1,0:T(8,128)(2,1)} custom-call(bf16[32,32,16,256]{3,2,1,0:T(8,128)(2,1)} %h_ref.3, bf16[32,32,16,256]{3,2,1,0:T(8,128)(2,1)} %g_ref.3, bf16[16,64,512]{2,1,0:T(8,128)(2,1)} %shard_map.71.ys_ref, bf16[32,256]{1,0:T(8,128)(2,1)} %multiply_convert_fusion.2.tz_ref, bf16[32,32]{1,0:T(8,128)(2,1)} %sw_ref.1), custom_call_target="tpu_custom_call" | custom-call | tf_op jit(solution)/shard_map/pallas_call | solution.py:186
  (9 shorter events, 0.1 us)
Async XLA Ops:
  18.1 54.2 %all-to-all-start.2 = ((f32[16,1,1024]{2,1,0:T(1,128)}), f32[16,1,1024]{2,1,0:T(1,128)S(1)}, u32[]{:S(2)}, u32[]{:S(2)}) async-start(f32[16,1,1024]{2,1,0:T(1,128)} %broadcast_in_dim.51), calls=%async_computation.2 | async-start | bytes 131072 | tf_op jit(solution)/shard_map/all_to_all | solution.py:316
  73.0 13.8 %all-to-all-start.3 = ((f32[8,1,1024]{2,1,0:T(1,128)}), f32[8,1,1024]{2,1,0:T(1,128)S(1)}, u32[]{:S(2)}, u32[]{:S(2)}) async-start(f32[8,1,1024]{2,1,0:T(1,128)} %broadcast_in_dim.52), calls=%async_computation.3 | async-start | bytes 65536 | tf_op jit(solution)/shard_map/all_to_all | solution.py:316
  86.8 11.7 %all-to-all-start = ((bf16[8,2,8192]{2,1,0:T(2,128)(2,1)}), bf16[8,2,8192]{2,1,0:T(2,128)(2,1)S(1)}, u32[]{:S(2)}, u32[]{:S(2)}) async-start(bf16[8,2,8192]{2,1,0:T(2,128)(2,1)} %reshape.110), calls=%async_computation | async-start | bytes 524288 | tf_op jit(solution)/shard_map/all_to_all | solution.py:293
  107.8 10.2 %all-to-all-start.1 = ((bf16[8,2,4096]{2,1,0:T(2,128)(2,1)}), bf16[8,2,4096]{2,1,0:T(2,128)(2,1)S(1)}, u32[]{:S(2)}, u32[]{:S(2)}) async-start(bf16[8,2,4096]{2,1,0:T(2,128)(2,1)} %reshape.112), calls=%async_computation.1 | async-start | bytes 262144 | tf_op jit(solution)/shard_map/all_to_all | solution.py:307

commit v7 on v6

--- a/solution.py
+++ b/solution.py
@@ -29,28 +29,73 @@
     return lax.dot_general(a, b, (((1,), (1,)), ((), ())), preferred_element_type=jnp.float32)
 
 
-def analysis_kernel(h_ref, g_ref, tz_ref, zc_ref, gram_ref, acc_ref, stage_ref):
+def analysis_kernel(axis, count, h_ref, g_ref, tz_ref, zc_ref, gram_ref, acc_ref, stage_ref,
+                    slot_ref, local_sems, send_sems, recv_sems):
+    mesh_ids = pl.DeviceIdType.MESH
     step = pl.program_id(0)
+    steps = pl.num_programs(0)
     channels, xb, ny, nz = h_ref.shape
+    width = xb * ny
+    mz_local = slot_ref.shape[1] // count
+    me = lax.axis_index(axis)
+
+    def copies(at):
+        slot = lax.rem(at, 2)
+        cols = pl.ds(pl.multiple_of(at * width, width), width)
+        local = pltpu.make_async_copy(
+            slot_ref.at[slot, pl.ds(me * mz_local, mz_local)],
+            zc_ref.at[me, :, :, cols],
+            local_sems.at[at],
+        )
+        remote = []
+        for k in range(1, count):
+            peer = lax.rem(me + k, count)
+            remote.append(pltpu.make_async_remote_copy(
+                src_ref=slot_ref.at[slot, pl.ds(peer * mz_local, mz_local)],
+                dst_ref=zc_ref.at[me, :, :, cols],
+                send_sem=send_sems.at[at, k],
+                recv_sem=recv_sems.at[at, k],
+                device_id={axis: peer},
+                device_id_type=mesh_ids,
+            ))
+        return local, remote
+
+    def wait_sent(at):
+        local, remote = copies(at)
+        local.wait()
+        for copy in remote:
+            copy.wait_send()
 
     @pl.when(step == 0)
     def _():
         acc_ref[...] = jnp.zeros_like(acc_ref)
+        barrier = pltpu.get_barrier_semaphore()
+        for k in range(1, count):
+            peer = lax.rem(me + k, count)
+            pl.semaphore_signal(barrier, inc=1, device_id={axis: peer}, device_id_type=mesh_ids)
+        pl.semaphore_wait(barrier, count - 1)
+
+    @pl.when(step >= 2)
+    def _():
+        wait_sent(step - 2)
 
     tz = tz_ref[...]
     li = jnp.tanh(h_ref[...].astype(jnp.float32)).astype(jnp.bfloat16)
     g = g_ref[...]
-    width = xb * ny
     zl = _nt(tz, li.reshape(channels * width, nz))
     zg = _nt(tz, g.reshape(channels * width, nz))
     for c in range(channels):
         stage_ref[:, c, :] = zl[:, c * width:(c + 1) * width]
         stage_ref[:, channels + c, :] = zg[:, c * width:(c + 1) * width]
-    zc_ref[...] = stage_ref[...].astype(jnp.bfloat16)
+    slot_ref[lax.rem(step, 2)] = stage_ref[...].astype(jnp.bfloat16)
+    local, remote = copies(step)
+    local.start()
+    for copy in remote:
+        copy.start()
     for x in range(xb):
         acc_ref[...] += _nt(li[:, x].reshape(channels * ny, nz), g[:, x].reshape(channels * ny, nz))
 
-    @pl.when(step == pl.num_programs(0) - 1)
+    @pl.when(step == steps - 1)
     def _():
         rows = channels * ny
         ri = lax.broadcasted_iota(jnp.int32, (rows, rows), 0)
@@ -63,31 +108,51 @@
         gram_ref[...] = lax.dot_general(
             part, gather, (((1,), (1,)), ((), ())), precision=lax.Precision.HIGHEST,
             preferred_element_type=jnp.float32)
-
-
-def analysis(hidden_pre, cotangent, table_z):
+        wait_sent(step - 1)
+        wait_sent(step)
+        for at in range(zc_ref.shape[3] // width):
+            cols = pl.ds(at * width, width)
+            for k in range(1, count):
+                origin = lax.rem(me + count - k, count)
+                pltpu.make_async_remote_copy(
+                    src_ref=slot_ref.at[0, pl.ds(me * mz_local, mz_local)],
+                    dst_ref=zc_ref.at[origin, :, :, cols],
+                    send_sem=send_sems.at[at, k],
+                    recv_sem=recv_sems.at[at, k],
+                    device_id={axis: origin},
+                    device_id_type=mesh_ids,
+                ).wait_recv()
+
+
+def analysis(hidden_pre, cotangent, table_z, axis, count):
     channels, nx, ny, nz = hidden_pre.shape
     modes = table_z.shape[0]
     steps = nx // XB
     field_spec = pl.BlockSpec((channels, XB, ny, nz), lambda i: (0, i, 0, 0))
     return pl.pallas_call(
-        analysis_kernel,
+        functools.partial(analysis_kernel, axis, count),
         grid=(steps,),
         in_specs=[field_spec, field_spec, pl.BlockSpec((modes, nz), lambda i: (0, 0))],
         out_specs=[
-            pl.BlockSpec((modes, 2 * channels, XB * ny), lambda i: (0, 0, i)),
+            pl.BlockSpec(memory_space=pl.ANY),
             pl.BlockSpec((channels, channels), lambda i: (0, 0)),
         ],
         out_shape=[
-            jax.ShapeDtypeStruct((modes, 2 * channels, nx * ny), jnp.bfloat16),
+            jax.ShapeDtypeStruct(
+                (count, modes // count, 2 * channels, nx * ny), jnp.bfloat16),
             jax.ShapeDtypeStruct((channels, channels), jnp.float32),
         ],
         scratch_shapes=[
             pltpu.VMEM((channels * ny, channels * ny), jnp.float32),
             pltpu.VMEM((modes, 2 * channels, XB * ny), jnp.float32),
+            pltpu.VMEM((2, modes, 2 * channels, XB * ny), jnp.bfloat16),
+            pltpu.SemaphoreType.DMA((steps,)),
+            pltpu.SemaphoreType.DMA((steps, count)),
+            pltpu.SemaphoreType.DMA((steps, count)),
         ],
         compiler_params=pltpu.CompilerParams(
-            dimension_semantics=("arbitrary",), vmem_limit_bytes=60 * 1024 * 1024
+            dimension_semantics=("arbitrary",), vmem_limit_bytes=60 * 1024 * 1024,
+            collective_id=0, has_side_effects=True,
         ),
     )(hidden_pre, cotangent, table_z)
 
@@ -281,10 +346,8 @@
     table_y = basis_table(mode_count, NY)
     table_z = basis_table(mode_count, NZ)
 
-    zc, gram = analysis(hidden_pre, cotangent, table_z)
+    zc, gram = analysis(hidden_pre, cotangent, table_z, "narrow", n_narrow)
     mz_local = mode_count // n_narrow
-    zc = zc.reshape(n_narrow, mz_local, 2 * channels, nx * ny)
-    zc = exchange(zc, "narrow", n_narrow, 0)
     zc = zc.reshape(n_narrow, mz_local, 2 * channels, nx, ny)
     ycoeffs = jnp.einsum(
         "smcxl,nsl->mcnx", zc, table_y.reshape(mode_count, n_narrow, ny),

time: 158 us -> 143 us (0.905)
  Pallas kernels: 94.6 us -> 82.8 us
  starting transfers between devices: 21.3 us -> 19 us
    pallas_call x2 -> x1, Pallas kernels: 56.2 us -> 23 us  [exchange(): pl.pallas_call(functools.partial(exchange_kernel, axis, count), in_specs=...]
    pallas_call x1, Pallas kernels: 15.2 us -> 36.5 us  [analysis(): pl.pallas_call(functools.partial(analysis_kernel, axis, count), grid=(ste...]
    all_to_all x2, starting transfers between devices: 14.4 us -> 12.1 us  [per_device(): total = lax.all_to_all(spread, axis, 0, 0, tiled=True).sum(0, keepdims=True)]
  transfers between devices with their start and end apart: 4 -> 4, of which waited for: 3 -> 3; matrix products, arithmetic and copies ran while one was open for 9% -> 10% of each run, Pallas kernels for 24% -> 0%
where the time goes in v7:
time: 143 us; the launch traced here: 142 us
  Pallas kernels  82.8 us (58%)
  starting transfers between devices  19 us (13%)
  waiting for transfers between devices  16.3 us (11%)
  local copies, waits for them, and re-layouts  15.1 us (11%)
  matrix products  4.98 us (3%)
  other arithmetic  2.94 us (2%)
    pallas_call x1, Pallas kernels, analysis(): pl.pallas_call(functools.partial(analysis_kernel, axis, count), grid=(ste...  36.5 us
    pallas_call x1, Pallas kernels, exchange(): pl.pallas_call(functools.partial(exchange_kernel, axis, count), in_specs=...  23 us
    pallas_call x1, Pallas kernels, synthesis(): pl.pallas_call(synthesis_kernel, grid=(steps,), in_specs=[field_spec, fie...  14.1 us
    all_to_all x2, starting transfers between devices, per_device(): total = lax.all_to_all(spread, axis, 0, 0, tiled=True).sum(0, keepdims=True)  12.1 us
    reshape x1, local copies, waits for them, and re-layouts, per_device(): zc = zc.reshape(n_narrow, mz_local, 2 * channels, nx, ny)  6.21 us
    all_to_all x1, waiting for transfers between devices, per_device(): lax.all_to_all(xsynth, 'wide', split_axis=3, concat_axis=2, tiled=True)  5.83 us
    all_to_all x2, waiting for transfers between devices, per_device(): total = lax.all_to_all(spread, axis, 0, 0, tiled=True).sum(0, keepdims=True)  5.26 us
    all_to_all x1, waiting for transfers between devices, per_device(): lax.all_to_all(ycoeffs, 'wide', split_axis=2, concat_axis=3, tiled=True)  5.2 us
  transfers between devices with their start and end apart: 4, of which 3 were waited for; matrix products, arithmetic and copies ran while one was open for 10% of the time, Pallas kernels for 0%

profile of v7, /device:TPU:1, one launch (start us, length us, event | category | flops | bytes accessed | tf_op | source)
XLA Modules:
  0.0 141.9 jit_solution(2163027450691986666)
XLA Ops:
  0.7 0.8 multiply_convert_fusion.3.tz_ref
  1.5 36.5 %shard_map.67 = (bf16[16,2,64,512]{3,2,1,0:T(8,128)(2,1)}, f32[32,32]{1,0:T(8,128)}) custom-call(bf16[32,32,16,256]{3,2,1,0:T(8,128)(2,1)} %h_ref.3, bf16[32,32,16,256]{3,2,1,0:T(8,128)(2,1)} %g_ref.3, bf16[32,256]{1,0:T(8,128)(2,1)} %multiply_convert_fusion.3.tz_ref), custom_call_target="tpu_custom_call" | custom-call | tf_op jit(solution)/shard_map/pallas_call | solution.py:132
  38.0 0.8 broadcast_in_dim.50
  38.8 0.7 broadcast_in_dim.51
  39.4 4.8 %all-to-all-start.2 = ((f32[16,1,1024]{2,1,0:T(1,128)}), f32[16,1,1024]{2,1,0:T(1,128)S(1)}, u32[]{:S(2)}, u32[]{:S(2)}) async-start(f32[16,1,1024]{2,1,0:T(1,128)} %broadcast_in_dim.51), calls=%async_computation.2 | async-start | bytes 131072 | tf_op jit(solution)/shard_map/all_to_all | solution.py:379
  44.3 0.1 iota.94
  44.4 6.2 %copy.47 = bf16[16,2,64,512]{2,0,3,1:T(8,128)(2,1)} copy(bf16[16,2,64,512]{3,2,1,0:T(8,128)(2,1)} %get-tuple-element.7) | data formatting | bytes 4194304 | tf_op jit(solution)/shard_map/reshape | solution.py:351
  50.6 3.6 %fusion.1 = bf16[2,64,32,32]{1,2,3,0:T(8,128)(2,1)S(1)} fusion(bf16[16,2,64,32,16]{2,0,4,3,1:T(8,128)(2,1)} %bitcast.48, s32[16,16]{0,1:T(8,128)S(1)} %multiply_add_fusion, s32[32]{0:T(128)S(1)} %add_select_fusion.5, pred[32]{0:T(512)(128)(4,1)S(1)} %iota_compare_fusion), kind=kOutput, calls=%fused_computation.2 | convolution fusion | flops 67379200 | bytes 2360480 | tf_op jit(solution)/shard_map/smcxl,nsl->mcnx/dot_general | solution.py:352
  54.2 0.0 all-to-all-done.2
  54.2 0.1 reduce_sum.18
  54.3 0.6 broadcast_in_dim.52
  54.9 7.2 %all-to-all-start.3 = ((f32[8,1,1024]{2,1,0:T(1,128)}), f32[8,1,1024]{2,1,0:T(1,128)S(1)}, u32[]{:S(2)}, u32[]{:S(2)}) async-start(f32[8,1,1024]{2,1,0:T(1,128)} %broadcast_in_dim.52), calls=%async_computation.3 | async-start | bytes 65536 | tf_op jit(solution)/shard_map/all_to_all | solution.py:379
  62.2 0.2 copy.51
  62.4 1.1 reshape.106
  63.5 5.3 %all-to-all-done.3 = f32[8,1,1024]{2,1,0:T(1,128)S(1)} async-done(((f32[8,1,1024]{2,1,0:T(1,128)}), f32[8,1,1024]{2,1,0:T(1,128)S(1)}, u32[]{:S(2)}, u32[]{:S(2)}) %all-to-all-start.3) | async-done | bytes 32800 | tf_op jit(solution)/shard_map/all_to_all | solution.py:379
  68.7 3.4 %all-to-all-start = ((bf16[8,2,8192]{2,1,0:T(2,128)(2,1)}), bf16[8,2,8192]{2,1,0:T(2,128)(2,1)S(1)}, u32[]{:S(2)}, u32[]{:S(2)}) async-start(bf16[8,2,8192]{2,1,0:T(2,128)(2,1)} %reshape.106), calls=%async_computation | async-start | bytes 524288 | tf_op jit(solution)/shard_map/all_to_all | solution.py:356
  72.2 0.8 multiply_convert_fusion.2.tz_ref
  73.0 1.2 multiply_convert_fusion.tyt_ref
  74.2 5.2 %all-to-all-done = bf16[8,2,8192]{2,1,0:T(2,128)(2,1)S(1)} async-done(((bf16[8,2,8192]{2,1,0:T(2,128)(2,1)}), bf16[8,2,8192]{2,1,0:T(2,128)(2,1)S(1)}, u32[]{:S(2)}, u32[]{:S(2)}) %all-to-all-start) | async-done | bytes 262176 | tf_op jit(solution)/shard_map/all_to_all | solution.py:356
  79.4 0.3 reshape.107
  79.8 1.0 fusion.35
  80.8 5.2 %shard_map.68 = (f32[256,1024]{1,0:T(8,128)}, bf16[256,32]{1,0:T(8,128)(2,1)}) custom-call(f32[256,64]{1,0:T(8,128)} %bitcast.55, bf16[256,1024]{1,0:T(8,128)(2,1)} %bitcast.56), custom_call_target="tpu_custom_call" | custom-call | tf_op jit(solution)/shard_map/pallas_call | solution.py:328
  85.9 0.9 copy.38
  86.9 0.4 convolution_convert_fusion
  87.2 0.3 copy.39
  87.6 1.2 reshape.108
  88.7 3.6 %all-to-all-start.1 = ((bf16[8,2,4096]{2,1,0:T(2,128)(2,1)}), bf16[8,2,4096]{2,1,0:T(2,128)(2,1)S(1)}, u32[]{:S(2)}, u32[]{:S(2)}) async-start(bf16[8,2,4096]{2,1,0:T(2,128)(2,1)} %reshape.108), calls=%async_computation.1 | async-start | bytes 262144 | tf_op jit(solution)/shard_map/all_to_all | solution.py:370
  92.3 0.7 mul.142
  93.0 5.8 %all-to-all-done.1 = bf16[8,2,4096]{2,1,0:T(2,128)(2,1)S(1)} async-done(((bf16[8,2,4096]{2,1,0:T(2,128)(2,1)}), bf16[8,2,4096]{2,1,0:T(2,128)(2,1)S(1)}, u32[]{:S(2)}, u32[]{:S(2)}) %all-to-all-start.1) | async-done | bytes 131104 | tf_op jit(solution)/shard_map/all_to_all | solution.py:370
  98.8 0.3 reshape.109
  99.1 1.7 %copy.40 = bf16[2,32,4,8,32]{4,2,3,1,0:T(4,128)(2,1)} copy(bf16[2,32,4,8,32]{1,2,0,4,3:T(4,128)(2,1)S(1)} %bitcast.52) | data formatting | bytes 262144 | tf_op jit(solution)/shard_map/all_to_all | solution.py:370
  100.8 3.9 %shard_map.69.src_ref = bf16[16,64,512]{2,1,0:T(8,128)(2,1)} custom-call(bf16[2,32,32,32]{3,2,1,0:T(8,128)(2,1)} %bitcast.49, bf16[256,32]{1,0:T(8,128)(2,1)} %multiply_convert_fusion.tyt_ref), custom_call_target="tpu_custom_call" | custom-call | tf_op jit(solution)/shard_map/pallas_call | solution.py:294
  104.7 23.0 %shard_map.70.ys_ref = bf16[16,64,512]{2,1,0:T(8,128)(2,1)} custom-call(bf16[16,64,512]{2,1,0:T(8,128)(2,1)} %shard_map.69.src_ref), custom_call_target="tpu_custom_call" | custom-call | tf_op jit(solution)/shard_map/pallas_call | solution.py:199
  127.8 14.1 %shard_map.71 = bf16[32,32,16,256]{3,2,1,0:T(8,128)(2,1)} custom-call(bf16[32,32,16,256]{3,2,1,0:T(8,128)(2,1)} %h_ref.3, bf16[32,32,16,256]{3,2,1,0:T(8,128)(2,1)} %g_ref.3, bf16[16,64,512]{2,1,0:T(8,128)(2,1)} %shard_map.70.ys_ref, bf16[32,256]{1,0:T(8,128)(2,1)} %multiply_convert_fusion.2.tz_ref, bf16[32,32]{1,0:T(8,128)(2,1)} %sw_ref.1), custom_call_target="tpu_custom_call" | custom-call | tf_op jit(solution)/shard_map/pallas_call | solution.py:251
  (9 shorter events, 0.1 us)
Async XLA Ops:
  39.4 14.8 %all-to-all-start.2 = ((f32[16,1,1024]{2,1,0:T(1,128)}), f32[16,1,1024]{2,1,0:T(1,128)S(1)}, u32[]{:S(2)}, u32[]{:S(2)}) async-start(f32[16,1,1024]{2,1,0:T(1,128)} %broadcast_in_dim.51), calls=%async_computation.2 | async-start | bytes 131072 | tf_op jit(solution)/shard_map/all_to_all | solution.py:379
  54.9 13.8 %all-to-all-start.3 = ((f32[8,1,1024]{2,1,0:T(1,128)}), f32[8,1,1024]{2,1,0:T(1,128)S(1)}, u32[]{:S(2)}, u32[]{:S(2)}) async-start(f32[8,1,1024]{2,1,0:T(1,128)} %broadcast_in_dim.52), calls=%async_computation.3 | async-start | bytes 65536 | tf_op jit(solution)/shard_map/all_to_all | solution.py:379
  68.7 10.6 %all-to-all-start = ((bf16[8,2,8192]{2,1,0:T(2,128)(2,1)}), bf16[8,2,8192]{2,1,0:T(2,128)(2,1)S(1)}, u32[]{:S(2)}, u32[]{:S(2)}) async-start(bf16[8,2,8192]{2,1,0:T(2,128)(2,1)} %reshape.106), calls=%async_computation | async-start | bytes 524288 | tf_op jit(solution)/shard_map/all_to_all | solution.py:356
  88.7 10.1 %all-to-all-start.1 = ((bf16[8,2,4096]{2,1,0:T(2,128)(2,1)}), bf16[8,2,4096]{2,1,0:T(2,128)(2,1)S(1)}, u32[]{:S(2)}, u32[]{:S(2)}) async-start(bf16[8,2,4096]{2,1,0:T(2,128)(2,1)} %reshape.108), calls=%async_computation.1 | async-start | bytes 262144 | tf_op jit(solution)/shard_map/all_to_all | solution.py:370

commit v8 on v7

--- a/solution.py
+++ b/solution.py
@@ -157,65 +157,46 @@
     )(hidden_pre, cotangent, table_z)
 
 
-def exchange_kernel(axis, count, src_ref, dst_ref, local_sem, send_sems, recv_sems):
+def synthesis_kernel(axis, count, h_ref, g_ref, xs_ref, tyt_ref, tz_ref, sw_ref, out_ref,
+                     ks_ref, stage_ref, send_ref, recv_ref, local_sems, send_sems, recv_sems):
     mesh_ids = pl.DeviceIdType.MESH
-    me = lax.axis_index(axis)
-    barrier = pltpu.get_barrier_semaphore()
-    for k in range(1, count):
-        peer = lax.rem(me + k, count)
-        pl.semaphore_signal(barrier, inc=1, device_id={axis: peer}, device_id_type=mesh_ids)
-    pl.semaphore_wait(barrier, count - 1)
-    local = pltpu.make_async_copy(src_ref.at[me], dst_ref.at[me], local_sem)
-    local.start()
-    sends = []
-    for k in range(1, count):
-        peer = lax.rem(me + k, count)
-        copy = pltpu.make_async_remote_copy(
-            src_ref=src_ref.at[peer],
-            dst_ref=dst_ref.at[me],
-            send_sem=send_sems.at[k],
-            recv_sem=recv_sems.at[k],
-            device_id={axis: peer},
-            device_id_type=mesh_ids,
-        )
-        copy.start()
-        sends.append(copy)
-    local.wait()
-    for k in range(1, count):
-        sends[k - 1].wait_send()
-        origin = lax.rem(me + count - k, count)
-        incoming = pltpu.make_async_remote_copy(
-            src_ref=src_ref.at[me],
-            dst_ref=dst_ref.at[origin],
-            send_sem=send_sems.at[k],
-            recv_sem=recv_sems.at[k],
-            device_id={axis: origin},
-            device_id_type=mesh_ids,
-        )
-        incoming.wait_recv()
-
-
-def exchange(chunks, axis, count, collective_id):
-    return pl.pallas_call(
-        functools.partial(exchange_kernel, axis, count),
-        in_specs=[pl.BlockSpec(memory_space=pl.ANY)],
-        out_specs=pl.BlockSpec(memory_space=pl.ANY),
-        out_shape=jax.ShapeDtypeStruct(chunks.shape, chunks.dtype),
-        scratch_shapes=[
-            pltpu.SemaphoreType.DMA,
-            pltpu.SemaphoreType.DMA((count,)),
-            pltpu.SemaphoreType.DMA((count,)),
-        ],
-        compiler_params=pltpu.CompilerParams(collective_id=collective_id, has_side_effects=True),
-    )(chunks)
-
-
-def synthesis_kernel(h_ref, g_ref, ys_ref, tz_ref, sw_ref, out_ref, ks_ref):
+    step = pl.program_id(0)
+    steps = pl.num_programs(0)
     channels, xb, ny, nz = h_ref.shape
     rows = channels * ny
-
-    @pl.when(pl.program_id(0) == 0)
-    def _():
+    chunk = 2 * xb
+    me = lax.axis_index(axis)
+
+    def copies(at):
+        part = pl.ds(pl.multiple_of(at * chunk, chunk), chunk)
+        local = pltpu.make_async_copy(
+            send_ref.at[me, part], recv_ref.at[me, part], local_sems.at[at])
+        remote = []
+        for k in range(1, count):
+            peer = lax.rem(me + k, count)
+            remote.append(pltpu.make_async_remote_copy(
+                src_ref=send_ref.at[peer, part],
+                dst_ref=recv_ref.at[me, part],
+                send_sem=send_sems.at[at, k],
+                recv_sem=recv_sems.at[at, k],
+                device_id={axis: peer},
+                device_id_type=mesh_ids,
+            ))
+        return local, remote
+
+    @pl.when(step == 0)
+    def _():
+        barrier = pltpu.get_barrier_semaphore()
+        for k in range(1, count):
+            peer = lax.rem(me + k, count)
+            pl.semaphore_signal(barrier, inc=1, device_id={axis: peer}, device_id_type=mesh_ids)
+        pl.semaphore_wait(barrier, count - 1)
+        y_synthesis_body(xs_ref, tyt_ref, send_ref, stage_ref)
+        for at in range(recv_ref.shape[1] // chunk):
+            local, remote = copies(at)
+            local.start()
+            for copy in remote:
+                copy.start()
         r = lax.broadcasted_iota(jnp.int32, (rows, channels), 0)
         k = lax.broadcasted_iota(jnp.int32, (rows, channels), 1)
         expand = (r // ny == k).astype(jnp.float32)
@@ -228,9 +209,23 @@
         ci = lax.broadcasted_iota(jnp.int32, (rows, rows), 1)
         ks_ref[...] = jnp.where(ri % ny == ci % ny, full, 0.0).astype(ks_ref.dtype)
 
+    local, _ = copies(step)
+    local.wait()
+    part = pl.ds(pl.multiple_of(step * chunk, chunk), chunk)
+    for k in range(1, count):
+        origin = lax.rem(me + count - k, count)
+        pltpu.make_async_remote_copy(
+            src_ref=send_ref.at[me, part],
+            dst_ref=recv_ref.at[origin, part],
+            send_sem=send_sems.at[step, k],
+            recv_sem=recv_sems.at[step, k],
+            device_id={axis: origin},
+            device_id_type=mesh_ids,
+        ).wait_recv()
+
     tz = tz_ref[...]
     ks = ks_ref[...]
-    ys = ys_ref[...].astype(jnp.float32)
+    ys = recv_ref[:, part, :].astype(jnp.float32)
     for x in range(xb):
         lo = ys[:, 2 * x, :]
         hi = ys[:, 2 * x + 1, :]
@@ -242,32 +237,52 @@
         grad = (spec + skip) * (1.0 - activ * activ)
         out_ref[:, x] = grad.astype(jnp.bfloat16).reshape(channels, ny, nz)
 
-
-def synthesis(hidden_pre, cotangent, ysynth, table_z, skip_weight):
+    @pl.when(step == steps - 1)
+    def _():
+        for at in range(recv_ref.shape[1] // chunk):
+            _, remote = copies(at)
+            for copy in remote:
+                copy.wait_send()
+
+
+def synthesis(hidden_pre, cotangent, xsynth, table_yt, table_z, skip_weight, axis, count):
     channels, nx, ny, nz = hidden_pre.shape
     modes = table_z.shape[0]
+    mz_local = xsynth.shape[0]
     steps = nx // XB
     field_spec = pl.BlockSpec((channels, XB, ny, nz), lambda i: (0, i, 0, 0))
+    whole = pl.BlockSpec(memory_space=pltpu.VMEM)
+    lanes = channels * ny
     return pl.pallas_call(
-        synthesis_kernel,
+        functools.partial(synthesis_kernel, axis, count),
         grid=(steps,),
         in_specs=[
             field_spec,
             field_spec,
-            pl.BlockSpec((ysynth.shape[0], 2 * XB, channels * ny), lambda i: (0, i, 0)),
+            whole,
+            whole,
             pl.BlockSpec((modes, nz), lambda i: (0, 0)),
             pl.BlockSpec((channels, channels), lambda i: (0, 0)),
         ],
         out_specs=field_spec,
         out_shape=jax.ShapeDtypeStruct(hidden_pre.shape, jnp.bfloat16),
-        scratch_shapes=[pltpu.VMEM((channels * ny, channels * ny), jnp.bfloat16)],
+        scratch_shapes=[
+            pltpu.VMEM((lanes, lanes), jnp.bfloat16),
+            pltpu.VMEM((count * lanes // 128, nx * mz_local, 128), jnp.float32),
+            pltpu.VMEM((count, nx * mz_local, lanes), jnp.bfloat16),
+            pltpu.VMEM((count, nx * mz_local, lanes), jnp.bfloat16),
+            pltpu.SemaphoreType.DMA((steps,)),
+            pltpu.SemaphoreType.DMA((steps, count)),
+            pltpu.SemaphoreType.DMA((steps, count)),
+        ],
         compiler_params=pltpu.CompilerParams(
-            dimension_semantics=("arbitrary",), vmem_limit_bytes=60 * 1024 * 1024
+            dimension_semantics=("arbitrary",), vmem_limit_bytes=60 * 1024 * 1024,
+            collective_id=1, has_side_effects=True,
         ),
-    )(hidden_pre, cotangent, ysynth, table_z, skip_weight)
-
-
-def y_synthesis_kernel(xs_ref, tyt_ref, out_ref, stage_ref):
+    )(hidden_pre, cotangent, xsynth, table_yt, table_z, skip_weight)
+
+
+def y_synthesis_body(xs_ref, tyt_ref, out_ref, stage_ref):
     mz_local, channels, modes, nx = xs_ref.shape
     blocks, _, lanes = out_ref.shape
     ny = lanes // channels
@@ -285,21 +300,6 @@
         for q in range(lanes // 128):
             out_ref[d, :, q * 128:(q + 1) * 128] = (
                 stage_ref[d * (lanes // 128) + q].astype(out_ref.dtype))
-
-
-def y_synthesis(xsynth, table_yt, blocks):
-    mz_local, channels, modes, nx = xsynth.shape
-    ny = table_yt.shape[0] // blocks
-    vmem = pl.BlockSpec(memory_space=pltpu.VMEM)
-    return pl.pallas_call(
-        y_synthesis_kernel,
-        in_specs=[vmem, vmem],
-        out_specs=vmem,
-        out_shape=jax.ShapeDtypeStruct((blocks, nx * mz_local, channels * ny), jnp.bfloat16),
-        scratch_shapes=[
-            pltpu.VMEM((blocks * channels * ny // 128, nx * mz_local, 128), jnp.float32)
-        ],
-    )(xsynth, table_yt)
 
 
 def modes_kernel(sp_ref, w_ref, gm_ref, bs_ref):
@@ -368,10 +368,10 @@
         "zcyk,kx->zcyx", back_spec, table_x, preferred_element_type=jnp.float32
     ).astype(jnp.bfloat16)
     xsynth = lax.all_to_all(xsynth, "wide", split_axis=3, concat_axis=2, tiled=True)
-    ysynth = y_synthesis(xsynth, jnp.transpose(table_y), n_narrow)
-    ysynth = exchange(ysynth, "narrow", n_narrow, 1)
     table_zp = jnp.transpose(table_z.reshape(n_narrow, mz_local, nz), (1, 0, 2)).reshape(mode_count, nz)
-    grad_hidden = synthesis(hidden_pre, cotangent, ysynth, table_zp, skip_weight)
+    grad_hidden = synthesis(
+        hidden_pre, cotangent, xsynth, jnp.transpose(table_y), table_zp, skip_weight,
+        "narrow", n_narrow)
 
     total = gram.reshape(1, channels * channels)
     for axis, count in (("narrow", n_narrow), ("wide", n_wide)):

time: 143 us -> 141 us (0.986)
  Pallas kernels: 82.8 us -> 73.7 us
  local copies, waits for them, and re-layouts: 15.1 us -> 22.8 us
    pallas_call x3 -> x1, Pallas kernels: 41.1 us -> 32.1 us  [synthesis(): pl.pallas_call(functools.partial(synthesis_kernel, axis, count), grid=(st...]
    unnamed x4 -> x5, local copies, waits for them, and re-layouts: 2.86 us -> 10.5 us
where the time goes in v8:
time: 141 us
  Pallas kernels  73.7 us (52%)
  local copies, waits for them, and re-layouts  22.8 us (16%)
  starting transfers between devices  19 us (13%)
  waiting for transfers between devices  16.3 us (12%)
  matrix products  4.98 us (4%)
  other arithmetic  2.94 us (2%)
    pallas_call x1, Pallas kernels, analysis(): pl.pallas_call(functools.partial(analysis_kernel, axis, count), grid=(ste...  36.5 us
    pallas_call x1, Pallas kernels, synthesis(): pl.pallas_call(functools.partial(synthesis_kernel, axis, count), grid=(st...  32.1 us
    all_to_all x2, starting transfers between devices, per_device(): total = lax.all_to_all(spread, axis, 0, 0, tiled=True).sum(0, keepdims=True)  12.1 us
    unnamed x5, local copies, waits for them, and re-layouts  10.5 us
    reshape x1, local copies, waits for them, and re-layouts, per_device(): zc = zc.reshape(n_narrow, mz_local, 2 * channels, nx, ny)  6.21 us
    all_to_all x1, waiting for transfers between devices, per_device(): lax.all_to_all(xsynth, 'wide', split_axis=3, concat_axis=2, tiled=True)  5.83 us
    all_to_all x2, waiting for transfers between devices, per_device(): total = lax.all_to_all(spread, axis, 0, 0, tiled=True).sum(0, keepdims=True)  5.26 us
    all_to_all x1, waiting for transfers between devices, per_device(): lax.all_to_all(ycoeffs, 'wide', split_axis=2, concat_axis=3, tiled=True)  5.2 us
  transfers between devices with their start and end apart: 4, of which 3 were waited for; matrix products, arithmetic and copies ran while one was open for 10% of the time, Pallas kernels for 0%

profile of v8, /device:TPU:1, one launch (start us, length us, event | category | flops | bytes accessed | tf_op | source)
XLA Modules:
  0.0 140.6 jit_solution(11379020716525270783)
XLA Ops:
  0.7 0.8 multiply_convert_fusion.3.tz_ref
  1.5 36.5 %shard_map.67 = (bf16[16,2,64,512]{3,2,1,0:T(8,128)(2,1)}, f32[32,32]{1,0:T(8,128)}) custom-call(bf16[32,32,16,256]{3,2,1,0:T(8,128)(2,1)} %h_ref.3, bf16[32,32,16,256]{3,2,1,0:T(8,128)(2,1)} %g_ref.3, bf16[32,256]{1,0:T(8,128)(2,1)} %multiply_convert_fusion.3.tz_ref), custom_call_target="tpu_custom_call" | custom-call | tf_op jit(solution)/shard_map/pallas_call | solution.py:132
  38.0 0.8 broadcast_in_dim.50
  38.8 0.7 broadcast_in_dim.51
  39.4 4.8 %all-to-all-start.2 = ((f32[16,1,1024]{2,1,0:T(1,128)}), f32[16,1,1024]{2,1,0:T(1,128)S(1)}, u32[]{:S(2)}, u32[]{:S(2)}) async-start(f32[16,1,1024]{2,1,0:T(1,128)} %broadcast_in_dim.51), calls=%async_computation.2 | async-start | bytes 131072 | tf_op jit(solution)/shard_map/all_to_all | solution.py:379
  44.3 0.1 iota.94
  44.4 6.2 %copy.47 = bf16[16,2,64,512]{2,0,3,1:T(8,128)(2,1)} copy(bf16[16,2,64,512]{3,2,1,0:T(8,128)(2,1)} %get-tuple-element.7) | data formatting | bytes 4194304 | tf_op jit(solution)/shard_map/reshape | solution.py:351
  50.6 3.6 %fusion.1 = bf16[2,64,32,32]{1,2,3,0:T(8,128)(2,1)S(1)} fusion(bf16[16,2,64,32,16]{2,0,4,3,1:T(8,128)(2,1)} %bitcast.48, s32[16,16]{0,1:T(8,128)S(1)} %multiply_add_fusion, s32[32]{0:T(128)S(1)} %add_select_fusion.5, pred[32]{0:T(512)(128)(4,1)S(1)} %iota_compare_fusion), kind=kOutput, calls=%fused_computation.2 | convolution fusion | flops 67379200 | bytes 2360480 | tf_op jit(solution)/shard_map/smcxl,nsl->mcnx/dot_general | solution.py:352
  54.2 0.0 all-to-all-done.2
  54.2 0.1 reduce_sum.18
  54.3 0.6 broadcast_in_dim.52
  54.9 7.2 %all-to-all-start.3 = ((f32[8,1,1024]{2,1,0:T(1,128)}), f32[8,1,1024]{2,1,0:T(1,128)S(1)}, u32[]{:S(2)}, u32[]{:S(2)}) async-start(f32[8,1,1024]{2,1,0:T(1,128)} %broadcast_in_dim.52), calls=%async_computation.3 | async-start | bytes 65536 | tf_op jit(solution)/shard_map/all_to_all | solution.py:379
  62.2 0.2 copy.51
  62.4 1.1 reshape.106
  63.5 5.3 %all-to-all-done.3 = f32[8,1,1024]{2,1,0:T(1,128)S(1)} async-done(((f32[8,1,1024]{2,1,0:T(1,128)}), f32[8,1,1024]{2,1,0:T(1,128)S(1)}, u32[]{:S(2)}, u32[]{:S(2)}) %all-to-all-start.3) | async-done | bytes 32800 | tf_op jit(solution)/shard_map/all_to_all | solution.py:379
  68.7 3.4 %all-to-all-start = ((bf16[8,2,8192]{2,1,0:T(2,128)(2,1)}), bf16[8,2,8192]{2,1,0:T(2,128)(2,1)S(1)}, u32[]{:S(2)}, u32[]{:S(2)}) async-start(bf16[8,2,8192]{2,1,0:T(2,128)(2,1)} %reshape.106), calls=%async_computation | async-start | bytes 524288 | tf_op jit(solution)/shard_map/all_to_all | solution.py:356
  72.2 0.8 multiply_convert_fusion.2.tz_ref
  73.0 1.2 multiply_convert_fusion.tyt_ref
  74.2 5.2 %all-to-all-done = bf16[8,2,8192]{2,1,0:T(2,128)(2,1)S(1)} async-done(((bf16[8,2,8192]{2,1,0:T(2,128)(2,1)}), bf16[8,2,8192]{2,1,0:T(2,128)(2,1)S(1)}, u32[]{:S(2)}, u32[]{:S(2)}) %all-to-all-start) | async-done | bytes 262176 | tf_op jit(solution)/shard_map/all_to_all | solution.py:356
  79.4 0.3 reshape.107
  79.8 1.0 fusion.35
  80.8 5.2 %shard_map.68 = (f32[256,1024]{1,0:T(8,128)}, bf16[256,32]{1,0:T(8,128)(2,1)}) custom-call(f32[256,64]{1,0:T(8,128)} %bitcast.55, bf16[256,1024]{1,0:T(8,128)(2,1)} %bitcast.56), custom_call_target="tpu_custom_call" | custom-call | tf_op jit(solution)/shard_map/pallas_call | solution.py:328
  85.9 0.9 copy.38
  86.9 0.4 convolution_convert_fusion
  87.2 0.3 copy.39
  87.6 1.2 reshape.108
  88.7 3.6 %all-to-all-start.1 = ((bf16[8,2,4096]{2,1,0:T(2,128)(2,1)}), bf16[8,2,4096]{2,1,0:T(2,128)(2,1)S(1)}, u32[]{:S(2)}, u32[]{:S(2)}) async-start(bf16[8,2,4096]{2,1,0:T(2,128)(2,1)} %reshape.108), calls=%async_computation.1 | async-start | bytes 262144 | tf_op jit(solution)/shard_map/all_to_all | solution.py:370
  92.3 0.7 mul.142
  93.0 5.8 %all-to-all-done.1 = bf16[8,2,4096]{2,1,0:T(2,128)(2,1)S(1)} async-done(((bf16[8,2,4096]{2,1,0:T(2,128)(2,1)}), bf16[8,2,4096]{2,1,0:T(2,128)(2,1)S(1)}, u32[]{:S(2)}, u32[]{:S(2)}) %all-to-all-start.1) | async-done | bytes 131104 | tf_op jit(solution)/shard_map/all_to_all | solution.py:370
  98.8 0.3 reshape.109
  99.1 1.7 %copy.40 = bf16[2,32,4,8,32]{4,2,3,1,0:T(4,128)(2,1)} copy(bf16[2,32,4,8,32]{1,2,0,4,3:T(4,128)(2,1)S(1)} %bitcast.51) | data formatting | bytes 262144 | tf_op jit(solution)/shard_map/all_to_all | solution.py:370
  100.8 32.1 %shard_map.69 = bf16[32,32,16,256]{3,2,1,0:T(8,128)(2,1)} custom-call(bf16[32,32,16,256]{3,2,1,0:T(8,128)(2,1)} %h_ref.3, bf16[32,32,16,256]{3,2,1,0:T(8,128)(2,1)} %g_ref.3, bf16[2,32,32,32]{3,2,1,0:T(8,128)(2,1)} %bitcast.54, bf16[256,32]{1,0:T(8,128)(2,1)} %multiply_convert_fusion.tyt_ref, bf16[32,256]{1,0:T(8,128)(2,1)} %multiply_convert_fusion.2.tz_ref, ...), custom_call_target="tpu_custom_call" | custom-call | tf_op jit(solution)/shard_map/pallas_call | solution.py:256
  132.9 7.7 %copy.53 = bf16[32,32,16,256]{3,2,1,0:T(8,128)(2,1)} copy(bf16[32,32,16,256]{3,2,1,0:T(8,128)(2,1)} %shard_map.69) | data formatting | bytes 16777216
  (9 shorter events, 0.1 us)
Async XLA Ops:
  39.4 14.8 %all-to-all-start.2 = ((f32[16,1,1024]{2,1,0:T(1,128)}), f32[16,1,1024]{2,1,0:T(1,128)S(1)}, u32[]{:S(2)}, u32[]{:S(2)}) async-start(f32[16,1,1024]{2,1,0:T(1,128)} %broadcast_in_dim.51), calls=%async_computation.2 | async-start | bytes 131072 | tf_op jit(solution)/shard_map/all_to_all | solution.py:379
  54.9 13.8 %all-to-all-start.3 = ((f32[8,1,1024]{2,1,0:T(1,128)}), f32[8,1,1024]{2,1,0:T(1,128)S(1)}, u32[]{:S(2)}, u32[]{:S(2)}) async-start(f32[8,1,1024]{2,1,0:T(1,128)} %broadcast_in_dim.52), calls=%async_computation.3 | async-start | bytes 65536 | tf_op jit(solution)/shard_map/all_to_all | solution.py:379
  68.7 10.6 %all-to-all-start = ((bf16[8,2,8192]{2,1,0:T(2,128)(2,1)}), bf16[8,2,8192]{2,1,0:T(2,128)(2,1)S(1)}, u32[]{:S(2)}, u32[]{:S(2)}) async-start(bf16[8,2,8192]{2,1,0:T(2,128)(2,1)} %reshape.106), calls=%async_computation | async-start | bytes 524288 | tf_op jit(solution)/shard_map/all_to_all | solution.py:356
  88.7 10.1 %all-to-all-start.1 = ((bf16[8,2,4096]{2,1,0:T(2,128)(2,1)}), bf16[8,2,4096]{2,1,0:T(2,128)(2,1)S(1)}, u32[]{:S(2)}, u32[]{:S(2)}) async-start(bf16[8,2,4096]{2,1,0:T(2,128)(2,1)} %reshape.108), calls=%async_computation.1 | async-start | bytes 262144 | tf_op jit(solution)/shard_map/all_to_all | solution.py:370

commit v9 on v8

--- a/solution.py
+++ b/solution.py
@@ -30,7 +30,8 @@
 
 
 def analysis_kernel(axis, count, h_ref, g_ref, tz_ref, zc_ref, gram_ref, acc_ref, stage_ref,
-                    slot_ref, local_sems, send_sems, recv_sems):
+                    slot_ref, local_sems, send_sems, recv_sems, gstage_ref, gbuf_ref, glocal_sem,
+                    gsend_sems, grecv_sems):
     mesh_ids = pl.DeviceIdType.MESH
     step = pl.program_id(0)
     steps = pl.num_programs(0)
@@ -105,9 +106,40 @@
         ec = lax.broadcasted_iota(jnp.int32, (channels, rows), 1)
         gather = (ec // ny == er).astype(jnp.float32)
         part = jnp.dot(gather, diag, precision=lax.Precision.HIGHEST, preferred_element_type=jnp.float32)
-        gram_ref[...] = lax.dot_general(
+        gstage_ref[...] = lax.dot_general(
             part, gather, (((1,), (1,)), ((), ())), precision=lax.Precision.HIGHEST,
             preferred_element_type=jnp.float32)
+        glocal = pltpu.make_async_copy(gstage_ref, gbuf_ref.at[me], glocal_sem)
+        glocal.start()
+        gsends = []
+        for k in range(1, count):
+            peer = lax.rem(me + k, count)
+            copy = pltpu.make_async_remote_copy(
+                src_ref=gstage_ref,
+                dst_ref=gbuf_ref.at[me],
+                send_sem=gsend_sems.at[k],
+                recv_sem=grecv_sems.at[k],
+                device_id={axis: peer},
+                device_id_type=mesh_ids,
+            )
+            copy.start()
+            gsends.append(copy)
+        glocal.wait()
+        for k in range(1, count):
+            gsends[k - 1].wait_send()
+            origin = lax.rem(me + count - k, count)
+            pltpu.make_async_remote_copy(
+                src_ref=gstage_ref,
+                dst_ref=gbuf_ref.at[origin],
+                send_sem=gsend_sems.at[k],
+                recv_sem=grecv_sems.at[k],
+                device_id={axis: origin},
+                device_id_type=mesh_ids,
+            ).wait_recv()
+        total = gbuf_ref[0]
+        for src in range(1, count):
+            total = total + gbuf_ref[src]
+        gram_ref[...] = total
         wait_sent(step - 1)
         wait_sent(step)
         for at in range(zc_ref.shape[3] // width):
@@ -149,6 +181,11 @@
             pltpu.SemaphoreType.DMA((steps,)),
             pltpu.SemaphoreType.DMA((steps, count)),
             pltpu.SemaphoreType.DMA((steps, count)),
+            pltpu.VMEM((channels, channels), jnp.float32),
+            pltpu.VMEM((count, channels, channels), jnp.float32),
+            pltpu.SemaphoreType.DMA,
+            pltpu.SemaphoreType.DMA((count,)),
+            pltpu.SemaphoreType.DMA((count,)),
         ],
         compiler_params=pltpu.CompilerParams(
             dimension_semantics=("arbitrary",), vmem_limit_bytes=60 * 1024 * 1024,
@@ -157,8 +194,10 @@
     )(hidden_pre, cotangent, table_z)
 
 
-def synthesis_kernel(axis, count, h_ref, g_ref, xs_ref, tyt_ref, tz_ref, sw_ref, out_ref,
-                     ks_ref, stage_ref, send_ref, recv_ref, local_sems, send_sems, recv_sems):
+def synthesis_kernel(axis, count, other, others, h_ref, g_ref, xs_ref, tyt_ref, tz_ref, sw_ref,
+                     gs_ref, out_ref, skip_out_ref, ks_ref, stage_ref, send_ref, recv_ref,
+                     local_sems, send_sems, recv_sems, wbuf_ref, wlocal_sem, wsend_sems,
+                     wrecv_sems):
     mesh_ids = pl.DeviceIdType.MESH
     step = pl.program_id(0)
     steps = pl.num_programs(0)
@@ -166,6 +205,22 @@
     rows = channels * ny
     chunk = 2 * xb
     me = lax.axis_index(axis)
+    me_w = lax.axis_index(other)
+
+    def wide_copies():
+        local = pltpu.make_async_copy(gs_ref, wbuf_ref.at[me_w], wlocal_sem)
+        remote = []
+        for k in range(1, others):
+            peer = lax.rem(me_w + k, others)
+            remote.append(pltpu.make_async_remote_copy(
+                src_ref=gs_ref,
+                dst_ref=wbuf_ref.at[me_w],
+                send_sem=wsend_sems.at[k],
+                recv_sem=wrecv_sems.at[k],
+                device_id={other: peer},
+                device_id_type=mesh_ids,
+            ))
+        return local, remote
 
     def copies(at):
         part = pl.ds(pl.multiple_of(at * chunk, chunk), chunk)
@@ -190,7 +245,14 @@
         for k in range(1, count):
             peer = lax.rem(me + k, count)
             pl.semaphore_signal(barrier, inc=1, device_id={axis: peer}, device_id_type=mesh_ids)
-        pl.semaphore_wait(barrier, count - 1)
+        for k in range(1, others):
+            peer = lax.rem(me_w + k, others)
+            pl.semaphore_signal(barrier, inc=1, device_id={other: peer}, device_id_type=mesh_ids)
+        pl.semaphore_wait(barrier, count - 1 + others - 1)
+        wlocal, wremote = wide_copies()
+        wlocal.start()
+        for copy in wremote:
+            copy.start()
         y_synthesis_body(xs_ref, tyt_ref, send_ref, stage_ref)
         for at in range(recv_ref.shape[1] // chunk):
             local, remote = copies(at)
@@ -243,9 +305,27 @@
             _, remote = copies(at)
             for copy in remote:
                 copy.wait_send()
-
-
-def synthesis(hidden_pre, cotangent, xsynth, table_yt, table_z, skip_weight, axis, count):
+        wlocal, wremote = wide_copies()
+        wlocal.wait()
+        for k in range(1, others):
+            wremote[k - 1].wait_send()
+            origin = lax.rem(me_w + others - k, others)
+            pltpu.make_async_remote_copy(
+                src_ref=gs_ref,
+                dst_ref=wbuf_ref.at[origin],
+                send_sem=wsend_sems.at[k],
+                recv_sem=wrecv_sems.at[k],
+                device_id={other: origin},
+                device_id_type=mesh_ids,
+            ).wait_recv()
+        total = wbuf_ref[0]
+        for src in range(1, others):
+            total = total + wbuf_ref[src]
+        skip_out_ref[...] = total * (1.0 / math.sqrt(NX * NY * NZ))
+
+
+def synthesis(hidden_pre, cotangent, xsynth, table_yt, table_z, skip_weight, skip_terms, axis,
+              count, other, others):
     channels, nx, ny, nz = hidden_pre.shape
     modes = table_z.shape[0]
     mz_local = xsynth.shape[0]
@@ -254,7 +334,7 @@
     whole = pl.BlockSpec(memory_space=pltpu.VMEM)
     lanes = channels * ny
     return pl.pallas_call(
-        functools.partial(synthesis_kernel, axis, count),
+        functools.partial(synthesis_kernel, axis, count, other, others),
         grid=(steps,),
         in_specs=[
             field_spec,
@@ -263,9 +343,13 @@
             whole,
             pl.BlockSpec((modes, nz), lambda i: (0, 0)),
             pl.BlockSpec((channels, channels), lambda i: (0, 0)),
-        ],
-        out_specs=field_spec,
-        out_shape=jax.ShapeDtypeStruct(hidden_pre.shape, jnp.bfloat16),
+            whole,
+        ],
+        out_specs=[field_spec, pl.BlockSpec((channels, channels), lambda i: (0, 0))],
+        out_shape=[
+            jax.ShapeDtypeStruct(hidden_pre.shape, jnp.bfloat16),
+            jax.ShapeDtypeStruct((channels, channels), jnp.float32),
+        ],
         scratch_shapes=[
             pltpu.VMEM((lanes, lanes), jnp.bfloat16),
             pltpu.VMEM((count * lanes // 128, nx * mz_local, 128), jnp.float32),
@@ -274,12 +358,16 @@
             pltpu.SemaphoreType.DMA((steps,)),
             pltpu.SemaphoreType.DMA((steps, count)),
             pltpu.SemaphoreType.DMA((steps, count)),
+            pltpu.VMEM((others, channels, channels), jnp.float32),
+            pltpu.SemaphoreType.DMA,
+            pltpu.SemaphoreType.DMA((others,)),
+            pltpu.SemaphoreType.DMA((others,)),
         ],
         compiler_params=pltpu.CompilerParams(
             dimension_semantics=("arbitrary",), vmem_limit_bytes=60 * 1024 * 1024,
             collective_id=1, has_side_effects=True,
         ),
-    )(hidden_pre, cotangent, xsynth, table_yt, table_z, skip_weight)
+    )(hidden_pre, cotangent, xsynth, table_yt, table_z, skip_weight, skip_terms)
 
 
 def y_synthesis_body(xs_ref, tyt_ref, out_ref, stage_ref):
@@ -369,15 +457,10 @@
     ).astype(jnp.bfloat16)
     xsynth = lax.all_to_all(xsynth, "wide", split_axis=3, concat_axis=2, tiled=True)
     table_zp = jnp.transpose(table_z.reshape(n_narrow, mz_local, nz), (1, 0, 2)).reshape(mode_count, nz)
-    grad_hidden = synthesis(
-        hidden_pre, cotangent, xsynth, jnp.transpose(table_y), table_zp, skip_weight,
-        "narrow", n_narrow)
-
-    total = gram.reshape(1, channels * channels)
-    for axis, count in (("narrow", n_narrow), ("wide", n_wide)):
-        spread = jnp.broadcast_to(total, (count, channels * channels))
-        total = lax.all_to_all(spread, axis, 0, 0, tiled=True).sum(0, keepdims=True)
-    grad_skip = total.reshape(channels, channels) * (1.0 / math.sqrt(NX * NY * NZ))
+    grad_hidden, grad_skip = synthesis(
+        hidden_pre, cotangent, xsynth, jnp.transpose(table_y), table_zp, skip_weight, gram,
+        "narrow", n_narrow, "wide", n_wide)
+
     return (grad_hidden, grad_modes, grad_skip)
 
 

time: 141 us -> 128 us (0.908)
  starting transfers between devices: 19 us -> 10.8 us
  waiting for transfers between devices: 16.3 us -> 12.2 us
  local copies, waits for them, and re-layouts: 22.8 us -> 20.7 us
  Pallas kernels: 73.7 us -> 75.4 us
    all_to_all x2 -> x0, starting transfers between devices: 12.1 us -> none  [per_device(): total = lax.all_to_all(spread, axis, 0, 0, tiled=True).sum(0, keepdims=True)]
    all_to_all x2 -> x0, waiting for transfers between devices: 5.26 us -> none  [per_device(): total = lax.all_to_all(spread, axis, 0, 0, tiled=True).sum(0, keepdims=True)]
    all_to_all x1, starting transfers between devices: 3.41 us -> 7.21 us  [per_device(): lax.all_to_all(ycoeffs, 'wide', split_axis=2, concat_axis=3, tiled=True)]
    pallas_call x1, Pallas kernels: 36.5 us -> 39.8 us  [analysis(): pl.pallas_call(functools.partial(analysis_kernel, axis, count), grid=(ste...]
    broadcast_in_dim x3 -> x0, local copies, waits for them, and re-layouts: 2.09 us -> none  [per_device(): spread = jnp.broadcast_to(total, (count, channels * channels))]
    pallas_call x1, Pallas kernels: 32.1 us -> 30.4 us  [synthesis(): pl.pallas_call(functools.partial(synthesis_kernel, axis, count, other, ot...]
    unnamed x5 -> x8, local copies, waits for them, and re-layouts: 10.5 us -> 11.1 us
  transfers between devices with their start and end apart: 4 -> 2, of which waited for: 3 -> 2; matrix products, arithmetic and copies ran while one was open for 10% -> 2% of each run, Pallas kernels for 0% -> 0%
where the time goes in v9:
time: 128 us
  Pallas kernels  75.4 us (59%)
  local copies, waits for them, and re-layouts  20.7 us (16%)
  waiting for transfers between devices  12.2 us (10%)
  starting transfers between devices  10.8 us (8%)
  matrix products  4.98 us (4%)
  other arithmetic  2.84 us (2%)
    pallas_call x1, Pallas kernels, analysis(): pl.pallas_call(functools.partial(analysis_kernel, axis, count), grid=(ste...  39.8 us
    pallas_call x1, Pallas kernels, synthesis(): pl.pallas_call(functools.partial(synthesis_kernel, axis, count, other, ot...  30.4 us
    unnamed x8, local copies, waits for them, and re-layouts  11.1 us
    all_to_all x1, starting transfers between devices, per_device(): lax.all_to_all(ycoeffs, 'wide', split_axis=2, concat_axis=3, tiled=True)  7.21 us
    reshape x1, local copies, waits for them, and re-layouts, per_device(): zc = zc.reshape(n_narrow, mz_local, 2 * channels, nx, ny)  6.22 us
    all_to_all x1, waiting for transfers between devices, per_device(): lax.all_to_all(ycoeffs, 'wide', split_axis=2, concat_axis=3, tiled=True)  6.18 us
    all_to_all x1, waiting for transfers between devices, per_device(): lax.all_to_all(xsynth, 'wide', split_axis=3, concat_axis=2, tiled=True)  6.02 us
    pallas_call x1, Pallas kernels, modes_step(): pl.pallas_call(modes_kernel, in_specs=[vmem, vmem], out_specs=[vmem, vmem...  5.16 us
  transfers between devices with their start and end apart: 2, of which 2 were waited for; matrix products, arithmetic and copies ran while one was open for 2% of the time, Pallas kernels for 0%

profile of v9, /device:TPU:1, one launch (start us, length us, event | category | flops | bytes accessed | tf_op | source)
XLA Modules:
  0.0 127.6 jit_solution(3016408467423869519)
XLA Ops:
  0.7 0.8 multiply_convert_fusion.3.tz_ref
  1.5 39.8 %shard_map.67 = (bf16[16,2,64,512]{3,2,1,0:T(8,128)(2,1)}, f32[32,32]{1,0:T(8,128)}) custom-call(bf16[32,32,16,256]{3,2,1,0:T(8,128)(2,1)} %h_ref.3, bf16[32,32,16,256]{3,2,1,0:T(8,128)(2,1)} %g_ref.3, bf16[32,256]{1,0:T(8,128)(2,1)} %multiply_convert_fusion.3.tz_ref), custom_call_target="tpu_custom_call" | custom-call | tf_op jit(solution)/shard_map/pallas_call | solution.py:164
  41.3 6.2 %copy.29 = bf16[16,2,64,512]{2,0,3,1:T(8,128)(2,1)} copy(bf16[16,2,64,512]{3,2,1,0:T(8,128)(2,1)} %get-tuple-element.9) | data formatting | bytes 4194304 | tf_op jit(solution)/shard_map/reshape | solution.py:439
  47.5 3.6 %fusion.1 = bf16[2,64,32,32]{1,2,3,0:T(8,128)(2,1)S(1)} fusion(bf16[16,2,64,32,16]{2,0,4,3,1:T(8,128)(2,1)} %bitcast.48, s32[16,16]{0,1:T(8,128)S(1)} %multiply_add_fusion, s32[32]{0:T(128)S(1)} %add_select_fusion.5, pred[32]{0:T(512)(128)(4,1)S(1)} %iota_compare_fusion), kind=kOutput, calls=%fused_computation.2 | convolution fusion | flops 67379200 | bytes 2360480 | tf_op jit(solution)/shard_map/smcxl,nsl->mcnx/dot_general | solution.py:440
  51.1 0.2 copy.31
  51.4 1.1 reshape.89
  52.4 7.2 %all-to-all-start = ((bf16[8,2,8192]{2,1,0:T(2,128)(2,1)}), bf16[8,2,8192]{2,1,0:T(2,128)(2,1)S(1)}, u32[]{:S(2)}, u32[]{:S(2)}) async-start(bf16[8,2,8192]{2,1,0:T(2,128)(2,1)} %reshape.89), calls=%async_computation | async-start | bytes 524288 | tf_op jit(solution)/shard_map/all_to_all | solution.py:444
  59.7 0.1 iota.94
  59.8 1.2 multiply_convert_fusion.tyt_ref
  60.9 6.2 %all-to-all-done = bf16[8,2,8192]{2,1,0:T(2,128)(2,1)S(1)} async-done(((bf16[8,2,8192]{2,1,0:T(2,128)(2,1)}), bf16[8,2,8192]{2,1,0:T(2,128)(2,1)S(1)}, u32[]{:S(2)}, u32[]{:S(2)}) %all-to-all-start) | async-done | bytes 262176 | tf_op jit(solution)/shard_map/all_to_all | solution.py:444
  67.1 0.3 reshape.90
  67.5 1.0 fusion.35
  68.5 5.2 %shard_map.68 = (f32[256,1024]{1,0:T(8,128)}, bf16[256,32]{1,0:T(8,128)(2,1)}) custom-call(f32[256,64]{1,0:T(8,128)} %bitcast.55, bf16[256,1024]{1,0:T(8,128)(2,1)} %bitcast.56), custom_call_target="tpu_custom_call" | custom-call | tf_op jit(solution)/shard_map/pallas_call | solution.py:416
  73.7 0.9 copy.22
  74.6 0.4 convolution_convert_fusion
  75.0 0.3 copy.23
  75.3 1.2 reshape.91
  76.5 3.6 %all-to-all-start.1 = ((bf16[8,2,4096]{2,1,0:T(2,128)(2,1)}), bf16[8,2,4096]{2,1,0:T(2,128)(2,1)S(1)}, u32[]{:S(2)}, u32[]{:S(2)}) async-start(bf16[8,2,4096]{2,1,0:T(2,128)(2,1)} %reshape.91), calls=%async_computation.1 | async-start | bytes 262144 | tf_op jit(solution)/shard_map/all_to_all | solution.py:458
  80.0 0.8 multiply_convert_fusion.2.tz_ref
  80.8 6.0 %all-to-all-done.1 = bf16[8,2,4096]{2,1,0:T(2,128)(2,1)S(1)} async-done(((bf16[8,2,4096]{2,1,0:T(2,128)(2,1)}), bf16[8,2,4096]{2,1,0:T(2,128)(2,1)S(1)}, u32[]{:S(2)}, u32[]{:S(2)}) %all-to-all-start.1) | async-done | bytes 131104 | tf_op jit(solution)/shard_map/all_to_all | solution.py:458
  86.9 0.3 reshape.92
  87.1 1.7 %copy.24 = bf16[2,32,4,8,32]{4,2,3,1,0:T(4,128)(2,1)} copy(bf16[2,32,4,8,32]{1,2,0,4,3:T(4,128)(2,1)S(1)} %bitcast.52) | data formatting | bytes 262144 | tf_op jit(solution)/shard_map/all_to_all | solution.py:458
  88.9 30.4 %shard_map.69 = (bf16[32,32,16,256]{3,2,1,0:T(8,128)(2,1)}, f32[32,32]{1,0:T(8,128)}) custom-call(bf16[32,32,16,256]{3,2,1,0:T(8,128)(2,1)} %h_ref.3, bf16[32,32,16,256]{3,2,1,0:T(8,128)(2,1)} %g_ref.3, bf16[2,32,32,32]{3,2,1,0:T(8,128)(2,1)} %bitcast.49, bf16[256,32]{1,0:T(8,128)(2,1)} %multiply_convert_fusion.tyt_ref, ...), custom_call_target="tpu_custom_call" | custom-call | tf_op jit(solution)/shard_map/pallas_call | solution.py:336
  119.3 0.0 copy-start
  119.3 7.7 %copy.34 = bf16[32,32,16,256]{3,2,1,0:T(8,128)(2,1)} copy(bf16[32,32,16,256]{3,2,1,0:T(8,128)(2,1)} %get-tuple-element.18) | data formatting | bytes 16777216
  127.0 0.0 copy-done
  127.0 0.6 copy.35
  (7 shorter events, 0.1 us)
Async XLA Ops:
  52.4 14.7 %all-to-all-start = ((bf16[8,2,8192]{2,1,0:T(2,128)(2,1)}), bf16[8,2,8192]{2,1,0:T(2,128)(2,1)S(1)}, u32[]{:S(2)}, u32[]{:S(2)}) async-start(bf16[8,2,8192]{2,1,0:T(2,128)(2,1)} %reshape.89), calls=%async_computation | async-start | bytes 524288 | tf_op jit(solution)/shard_map/all_to_all | solution.py:444
  76.5 10.4 %all-to-all-start.1 = ((bf16[8,2,4096]{2,1,0:T(2,128)(2,1)}), bf16[8,2,4096]{2,1,0:T(2,128)(2,1)S(1)}, u32[]{:S(2)}, u32[]{:S(2)}) async-start(bf16[8,2,4096]{2,1,0:T(2,128)(2,1)} %reshape.91), calls=%async_computation.1 | async-start | bytes 262144 | tf_op jit(solution)/shard_map/all_to_all | solution.py:458
  119.3 7.7 %copy-start = (f32[32,32]{1,0:T(8,128)S(1)}, f32[32,32]{1,0:T(8,128)}, u32[]{:S(2)}) copy-start(f32[32,32]{1,0:T(8,128)} %get-tuple-element.20) | copy-start | bytes 12292

commit v10 on v9

--- a/solution.py
+++ b/solution.py
@@ -30,8 +30,7 @@
 
 
 def analysis_kernel(axis, count, h_ref, g_ref, tz_ref, zc_ref, gram_ref, acc_ref, stage_ref,
-                    slot_ref, local_sems, send_sems, recv_sems, gstage_ref, gbuf_ref, glocal_sem,
-                    gsend_sems, grecv_sems):
+                    slot_ref, local_sems, send_sems, recv_sems):
     mesh_ids = pl.DeviceIdType.MESH
     step = pl.program_id(0)
     steps = pl.num_programs(0)
@@ -106,40 +105,9 @@
         ec = lax.broadcasted_iota(jnp.int32, (channels, rows), 1)
         gather = (ec // ny == er).astype(jnp.float32)
         part = jnp.dot(gather, diag, precision=lax.Precision.HIGHEST, preferred_element_type=jnp.float32)
-        gstage_ref[...] = lax.dot_general(
+        gram_ref[...] = lax.dot_general(
             part, gather, (((1,), (1,)), ((), ())), precision=lax.Precision.HIGHEST,
             preferred_element_type=jnp.float32)
-        glocal = pltpu.make_async_copy(gstage_ref, gbuf_ref.at[me], glocal_sem)
-        glocal.start()
-        gsends = []
-        for k in range(1, count):
-            peer = lax.rem(me + k, count)
-            copy = pltpu.make_async_remote_copy(
-                src_ref=gstage_ref,
-                dst_ref=gbuf_ref.at[me],
-                send_sem=gsend_sems.at[k],
-                recv_sem=grecv_sems.at[k],
-                device_id={axis: peer},
-                device_id_type=mesh_ids,
-            )
-            copy.start()
-            gsends.append(copy)
-        glocal.wait()
-        for k in range(1, count):
-            gsends[k - 1].wait_send()
-            origin = lax.rem(me + count - k, count)
-            pltpu.make_async_remote_copy(
-                src_ref=gstage_ref,
-                dst_ref=gbuf_ref.at[origin],
-                send_sem=gsend_sems.at[k],
-                recv_sem=grecv_sems.at[k],
-                device_id={axis: origin},
-                device_id_type=mesh_ids,
-            ).wait_recv()
-        total = gbuf_ref[0]
-        for src in range(1, count):
-            total = total + gbuf_ref[src]
-        gram_ref[...] = total
         wait_sent(step - 1)
         wait_sent(step)
         for at in range(zc_ref.shape[3] // width):
@@ -181,11 +149,6 @@
             pltpu.SemaphoreType.DMA((steps,)),
             pltpu.SemaphoreType.DMA((steps, count)),
             pltpu.SemaphoreType.DMA((steps, count)),
-            pltpu.VMEM((channels, channels), jnp.float32),
-            pltpu.VMEM((count, channels, channels), jnp.float32),
-            pltpu.SemaphoreType.DMA,
-            pltpu.SemaphoreType.DMA((count,)),
-            pltpu.SemaphoreType.DMA((count,)),
         ],
         compiler_params=pltpu.CompilerParams(
             dimension_semantics=("arbitrary",), vmem_limit_bytes=60 * 1024 * 1024,
@@ -197,7 +160,7 @@
 def synthesis_kernel(axis, count, other, others, h_ref, g_ref, xs_ref, tyt_ref, tz_ref, sw_ref,
                      gs_ref, out_ref, skip_out_ref, ks_ref, stage_ref, send_ref, recv_ref,
                      local_sems, send_sems, recv_sems, wbuf_ref, wlocal_sem, wsend_sems,
-                     wrecv_sems):
+                     wrecv_sems, nbuf_ref, nlocal_sem, nsend_sems, nrecv_sems, wstage_ref):
     mesh_ids = pl.DeviceIdType.MESH
     step = pl.program_id(0)
     steps = pl.num_programs(0)
@@ -207,13 +170,28 @@
     me = lax.axis_index(axis)
     me_w = lax.axis_index(other)
 
+    def narrow_copies():
+        local = pltpu.make_async_copy(gs_ref, nbuf_ref.at[me], nlocal_sem)
+        remote = []
+        for k in range(1, count):
+            peer = lax.rem(me + k, count)
+            remote.append(pltpu.make_async_remote_copy(
+                src_ref=gs_ref,
+                dst_ref=nbuf_ref.at[me],
+                send_sem=nsend_sems.at[k],
+                recv_sem=nrecv_sems.at[k],
+                device_id={axis: peer},
+                device_id_type=mesh_ids,
+            ))
+        return local, remote
+
     def wide_copies():
-        local = pltpu.make_async_copy(gs_ref, wbuf_ref.at[me_w], wlocal_sem)
+        local = pltpu.make_async_copy(wstage_ref, wbuf_ref.at[me_w], wlocal_sem)
         remote = []
         for k in range(1, others):
             peer = lax.rem(me_w + k, others)
             remote.append(pltpu.make_async_remote_copy(
-                src_ref=gs_ref,
+                src_ref=wstage_ref,
                 dst_ref=wbuf_ref.at[me_w],
                 send_sem=wsend_sems.at[k],
                 recv_sem=wrecv_sems.at[k],
@@ -249,9 +227,9 @@
             peer = lax.rem(me_w + k, others)
             pl.semaphore_signal(barrier, inc=1, device_id={other: peer}, device_id_type=mesh_ids)
         pl.semaphore_wait(barrier, count - 1 + others - 1)
-        wlocal, wremote = wide_copies()
-        wlocal.start()
-        for copy in wremote:
+        nlocal, nremote = narrow_copies()
+        nlocal.start()
+        for copy in nremote:
             copy.start()
         y_synthesis_body(xs_ref, tyt_ref, send_ref, stage_ref)
         for at in range(recv_ref.shape[1] // chunk):
@@ -271,6 +249,30 @@
         ci = lax.broadcasted_iota(jnp.int32, (rows, rows), 1)
         ks_ref[...] = jnp.where(ri % ny == ci % ny, full, 0.0).astype(ks_ref.dtype)
 
+    @pl.when(step == 1)
+    def _():
+        nlocal, nremote = narrow_copies()
+        nlocal.wait()
+        for k in range(1, count):
+            nremote[k - 1].wait_send()
+            origin = lax.rem(me + count - k, count)
+            pltpu.make_async_remote_copy(
+                src_ref=gs_ref,
+                dst_ref=nbuf_ref.at[origin],
+                send_sem=nsend_sems.at[k],
+                recv_sem=nrecv_sems.at[k],
+                device_id={axis: origin},
+                device_id_type=mesh_ids,
+            ).wait_recv()
+        total = nbuf_ref[0]
+        for src in range(1, count):
+            total = total + nbuf_ref[src]
+        wstage_ref[...] = total
+        wlocal, wremote = wide_copies()
+        wlocal.start()
+        for copy in wremote:
+            copy.start()
+
     local, _ = copies(step)
     local.wait()
     part = pl.ds(pl.multiple_of(step * chunk, chunk), chunk)
@@ -311,7 +313,7 @@
             wremote[k - 1].wait_send()
             origin = lax.rem(me_w + others - k, others)
             pltpu.make_async_remote_copy(
-                src_ref=gs_ref,
+                src_ref=wstage_ref,
                 dst_ref=wbuf_ref.at[origin],
                 send_sem=wsend_sems.at[k],
                 recv_sem=wrecv_sems.at[k],
@@ -362,6 +364,11 @@
             pltpu.SemaphoreType.DMA,
             pltpu.SemaphoreType.DMA((others,)),
             pltpu.SemaphoreType.DMA((others,)),
+            pltpu.VMEM((count, channels, channels), jnp.float32),
+            pltpu.SemaphoreType.DMA,
+            pltpu.SemaphoreType.DMA((count,)),
+            pltpu.SemaphoreType.DMA((count,)),
+            pltpu.VMEM((channels, channels), jnp.float32),
         ],
         compiler_params=pltpu.CompilerParams(
             dimension_semantics=("arbitrary",), vmem_limit_bytes=60 * 1024 * 1024,

time: 128 us -> 126 us (0.984)
  Pallas kernels: 75.4 us -> 73.8 us
    pallas_call x1, Pallas kernels: 39.8 us -> 36.5 us  [analysis(): pl.pallas_call(functools.partial(analysis_kernel, axis, count), grid=(ste...]
    pallas_call x1, Pallas kernels: 30.4 us -> 32.1 us  [synthesis(): pl.pallas_call(functools.partial(synthesis_kernel, axis, count, other, ot...]
where the time goes in v10:
time: 126 us
  Pallas kernels  73.8 us (59%)
  local copies, waits for them, and re-layouts  20.7 us (16%)
  waiting for transfers between devices  12.1 us (10%)
  starting transfers between devices  10.8 us (9%)
  matrix products  4.98 us (4%)
  other arithmetic  2.84 us (2%)
    pallas_call x1, Pallas kernels, analysis(): pl.pallas_call(functools.partial(analysis_kernel, axis, count), grid=(ste...  36.5 us
    pallas_call x1, Pallas kernels, synthesis(): pl.pallas_call(functools.partial(synthesis_kernel, axis, count, other, ot...  32.1 us
    unnamed x8, local copies, waits for them, and re-layouts  11.1 us
    all_to_all x1, starting transfers between devices, per_device(): lax.all_to_all(ycoeffs, 'wide', split_axis=2, concat_axis=3, tiled=True)  7.21 us
    reshape x1, local copies, waits for them, and re-layouts, per_device(): zc = zc.reshape(n_narrow, mz_local, 2 * channels, nx, ny)  6.22 us
    all_to_all x1, waiting for transfers between devices, per_device(): lax.all_to_all(ycoeffs, 'wide', split_axis=2, concat_axis=3, tiled=True)  6.18 us
    all_to_all x1, waiting for transfers between devices, per_device(): lax.all_to_all(xsynth, 'wide', split_axis=3, concat_axis=2, tiled=True)  5.96 us
    pallas_call x1, Pallas kernels, modes_step(): pl.pallas_call(modes_kernel, in_specs=[vmem, vmem], out_specs=[vmem, vmem...  5.16 us
  transfers between devices with their start and end apart: 2, of which 2 were waited for; matrix products, arithmetic and copies ran while one was open for 2% of the time, Pallas kernels for 0%

profile of v10, /device:TPU:1, one launch (start us, length us, event | category | flops | bytes accessed | tf_op | source)
XLA Modules:
  0.0 125.9 jit_solution(15566439204268125112)
XLA Ops:
  0.7 0.8 multiply_convert_fusion.3.tz_ref
  1.5 36.5 %shard_map.67 = (bf16[16,2,64,512]{3,2,1,0:T(8,128)(2,1)}, f32[32,32]{1,0:T(8,128)}) custom-call(bf16[32,32,16,256]{3,2,1,0:T(8,128)(2,1)} %h_ref.3, bf16[32,32,16,256]{3,2,1,0:T(8,128)(2,1)} %g_ref.3, bf16[32,256]{1,0:T(8,128)(2,1)} %multiply_convert_fusion.3.tz_ref), custom_call_target="tpu_custom_call" | custom-call | tf_op jit(solution)/shard_map/pallas_call | solution.py:132
  38.0 6.2 %copy.29 = bf16[16,2,64,512]{2,0,3,1:T(8,128)(2,1)} copy(bf16[16,2,64,512]{3,2,1,0:T(8,128)(2,1)} %get-tuple-element.9) | data formatting | bytes 4194304 | tf_op jit(solution)/shard_map/reshape | solution.py:446
  44.2 3.6 %fusion.1 = bf16[2,64,32,32]{1,2,3,0:T(8,128)(2,1)S(1)} fusion(bf16[16,2,64,32,16]{2,0,4,3,1:T(8,128)(2,1)} %bitcast.48, s32[16,16]{0,1:T(8,128)S(1)} %multiply_add_fusion, s32[32]{0:T(128)S(1)} %add_select_fusion.5, pred[32]{0:T(512)(128)(4,1)S(1)} %iota_compare_fusion), kind=kOutput, calls=%fused_computation.2 | convolution fusion | flops 67379200 | bytes 2360480 | tf_op jit(solution)/shard_map/smcxl,nsl->mcnx/dot_general | solution.py:447
  47.8 0.2 copy.31
  48.1 1.1 reshape.89
  49.2 7.2 %all-to-all-start = ((bf16[8,2,8192]{2,1,0:T(2,128)(2,1)}), bf16[8,2,8192]{2,1,0:T(2,128)(2,1)S(1)}, u32[]{:S(2)}, u32[]{:S(2)}) async-start(bf16[8,2,8192]{2,1,0:T(2,128)(2,1)} %reshape.89), calls=%async_computation | async-start | bytes 524288 | tf_op jit(solution)/shard_map/all_to_all | solution.py:451
  56.4 0.1 iota.94
  56.5 1.2 multiply_convert_fusion.tyt_ref
  57.6 6.2 %all-to-all-done = bf16[8,2,8192]{2,1,0:T(2,128)(2,1)S(1)} async-done(((bf16[8,2,8192]{2,1,0:T(2,128)(2,1)}), bf16[8,2,8192]{2,1,0:T(2,128)(2,1)S(1)}, u32[]{:S(2)}, u32[]{:S(2)}) %all-to-all-start) | async-done | bytes 262176 | tf_op jit(solution)/shard_map/all_to_all | solution.py:451
  63.8 0.3 reshape.90
  64.2 1.0 fusion.35
  65.2 5.2 %shard_map.68 = (f32[256,1024]{1,0:T(8,128)}, bf16[256,32]{1,0:T(8,128)(2,1)}) custom-call(f32[256,64]{1,0:T(8,128)} %bitcast.55, bf16[256,1024]{1,0:T(8,128)(2,1)} %bitcast.56), custom_call_target="tpu_custom_call" | custom-call | tf_op jit(solution)/shard_map/pallas_call | solution.py:423
  70.4 0.9 copy.22
  71.3 0.4 convolution_convert_fusion
  71.7 0.3 copy.23
  72.0 1.2 reshape.91
  73.2 3.6 %all-to-all-start.1 = ((bf16[8,2,4096]{2,1,0:T(2,128)(2,1)}), bf16[8,2,4096]{2,1,0:T(2,128)(2,1)S(1)}, u32[]{:S(2)}, u32[]{:S(2)}) async-start(bf16[8,2,4096]{2,1,0:T(2,128)(2,1)} %reshape.91), calls=%async_computation.1 | async-start | bytes 262144 | tf_op jit(solution)/shard_map/all_to_all | solution.py:465
  76.7 0.8 multiply_convert_fusion.2.tz_ref
  77.5 6.0 %all-to-all-done.1 = bf16[8,2,4096]{2,1,0:T(2,128)(2,1)S(1)} async-done(((bf16[8,2,4096]{2,1,0:T(2,128)(2,1)}), bf16[8,2,4096]{2,1,0:T(2,128)(2,1)S(1)}, u32[]{:S(2)}, u32[]{:S(2)}) %all-to-all-start.1) | async-done | bytes 131104 | tf_op jit(solution)/shard_map/all_to_all | solution.py:465
  83.5 0.3 reshape.92
  83.8 1.7 %copy.24 = bf16[2,32,4,8,32]{4,2,3,1,0:T(4,128)(2,1)} copy(bf16[2,32,4,8,32]{1,2,0,4,3:T(4,128)(2,1)S(1)} %bitcast.52) | data formatting | bytes 262144 | tf_op jit(solution)/shard_map/all_to_all | solution.py:465
  85.5 32.1 %shard_map.69 = (bf16[32,32,16,256]{3,2,1,0:T(8,128)(2,1)}, f32[32,32]{1,0:T(8,128)}) custom-call(bf16[32,32,16,256]{3,2,1,0:T(8,128)(2,1)} %h_ref.3, bf16[32,32,16,256]{3,2,1,0:T(8,128)(2,1)} %g_ref.3, bf16[2,32,32,32]{3,2,1,0:T(8,128)(2,1)} %bitcast.49, bf16[256,32]{1,0:T(8,128)(2,1)} %multiply_convert_fusion.tyt_ref, ...), custom_call_target="tpu_custom_call" | custom-call | tf_op jit(solution)/shard_map/pallas_call | solution.py:338
  117.7 0.0 copy-start
  117.7 7.7 %copy.34 = bf16[32,32,16,256]{3,2,1,0:T(8,128)(2,1)} copy(bf16[32,32,16,256]{3,2,1,0:T(8,128)(2,1)} %get-tuple-element.18) | data formatting | bytes 16777216
  125.3 0.0 copy-done
  125.3 0.6 copy.35
  (7 shorter events, 0.1 us)
Async XLA Ops:
  49.2 14.7 %all-to-all-start = ((bf16[8,2,8192]{2,1,0:T(2,128)(2,1)}), bf16[8,2,8192]{2,1,0:T(2,128)(2,1)S(1)}, u32[]{:S(2)}, u32[]{:S(2)}) async-start(bf16[8,2,8192]{2,1,0:T(2,128)(2,1)} %reshape.89), calls=%async_computation | async-start | bytes 524288 | tf_op jit(solution)/shard_map/all_to_all | solution.py:451
  73.2 10.3 %all-to-all-start.1 = ((bf16[8,2,4096]{2,1,0:T(2,128)(2,1)}), bf16[8,2,4096]{2,1,0:T(2,128)(2,1)S(1)}, u32[]{:S(2)}, u32[]{:S(2)}) async-start(bf16[8,2,4096]{2,1,0:T(2,128)(2,1)} %reshape.91), calls=%async_computation.1 | async-start | bytes 262144 | tf_op jit(solution)/shard_map/all_to_all | solution.py:465
  117.7 7.7 %copy-start = (f32[32,32]{1,0:T(8,128)S(1)}, f32[32,32]{1,0:T(8,128)}, u32[]{:S(2)}) copy-start(f32[32,32]{1,0:T(8,128)} %get-tuple-element.20) | copy-start | bytes 12292

commit v11 on v10

--- a/solution.py
+++ b/solution.py
@@ -398,22 +398,15 @@
 
 
 def modes_kernel(sp_ref, w_ref, gm_ref, bs_ref):
-    highest = lax.Precision.HIGHEST
     channels = sp_ref.shape[1] // 2
-    width = channels * channels
     sp = sp_ref[...]
-    er = lax.broadcasted_iota(jnp.int32, (channels, width), 0)
-    ec = lax.broadcasted_iota(jnp.int32, (channels, width), 1)
-    spread = (ec // channels == er).astype(jnp.float32)
-    tile = (ec % channels == er).astype(jnp.float32)
-    s_rep = jnp.dot(sp[:, :channels], spread, precision=highest, preferred_element_type=jnp.float32)
-    q_rep = jnp.dot(sp[:, channels:], tile, precision=highest, preferred_element_type=jnp.float32)
-    gm_ref[...] = s_rep * q_rep
-    weighted = w_ref[...].astype(jnp.float32) * q_rep
-    back = lax.dot_general(
-        weighted, spread, (((1,), (1,)), ((), ())), precision=highest,
-        preferred_element_type=jnp.float32)
-    bs_ref[...] = back.astype(bs_ref.dtype)
+    q = sp[:, channels:]
+    columns = []
+    for c in range(channels):
+        gm_ref[:, c * channels:(c + 1) * channels] = sp[:, c:c + 1] * q
+        weights = w_ref[:, c * channels:(c + 1) * channels].astype(jnp.float32)
+        columns.append(jnp.sum(weights * q, axis=1, keepdims=True))
+    bs_ref[...] = jnp.concatenate(columns, axis=1).astype(bs_ref.dtype)
 
 
 def modes_step(spectra, weights):

time: 126 us -> 130 us (1.032)
  Pallas kernels: 73.8 us -> 76.9 us
    pallas_call x1, Pallas kernels: 5.16 us -> 8.24 us  [modes_step(): pl.pallas_call(modes_kernel, in_specs=[vmem, vmem], out_specs=[vmem, vmem...]
where the time goes in v11:
time: 130 us; the launch traced here: 129 us
  Pallas kernels  76.9 us (59%)
  local copies, waits for them, and re-layouts  20.7 us (16%)
  waiting for transfers between devices  12.1 us (9%)
  starting transfers between devices  10.8 us (8%)
  matrix products  4.98 us (4%)
  other arithmetic  2.84 us (2%)
    pallas_call x1, Pallas kernels, analysis(): pl.pallas_call(functools.partial(analysis_kernel, axis, count), grid=(ste...  36.5 us
    pallas_call x1, Pallas kernels, synthesis(): pl.pallas_call(functools.partial(synthesis_kernel, axis, count, other, ot...  32.1 us
    unnamed x8, local copies, waits for them, and re-layouts  11.1 us
    pallas_call x1, Pallas kernels, modes_step(): pl.pallas_call(modes_kernel, in_specs=[vmem, vmem], out_specs=[vmem, vmem...  8.24 us
    all_to_all x1, starting transfers between devices, per_device(): lax.all_to_all(ycoeffs, 'wide', split_axis=2, concat_axis=3, tiled=True)  7.21 us
    reshape x1, local copies, waits for them, and re-layouts, per_device(): zc = zc.reshape(n_narrow, mz_local, 2 * channels, nx, ny)  6.22 us
    all_to_all x1, waiting for transfers between devices, per_device(): lax.all_to_all(ycoeffs, 'wide', split_axis=2, concat_axis=3, tiled=True)  6.18 us
    all_to_all x1, waiting for transfers between devices, per_device(): lax.all_to_all(xsynth, 'wide', split_axis=3, concat_axis=2, tiled=True)  5.92 us
  transfers between devices with their start and end apart: 2, of which 2 were waited for; matrix products, arithmetic and copies ran while one was open for 2% of the time, Pallas kernels for 0%

profile of v11, /device:TPU:1, one launch (start us, length us, event | category | flops | bytes accessed | tf_op | source)
XLA Modules:
  0.0 129.0 jit_solution(10464968607662984018)
XLA Ops:
  0.7 0.8 multiply_convert_fusion.3.tz_ref
  1.5 36.5 %shard_map.67 = (bf16[16,2,64,512]{3,2,1,0:T(8,128)(2,1)}, f32[32,32]{1,0:T(8,128)}) custom-call(bf16[32,32,16,256]{3,2,1,0:T(8,128)(2,1)} %h_ref.3, bf16[32,32,16,256]{3,2,1,0:T(8,128)(2,1)} %g_ref.3, bf16[32,256]{1,0:T(8,128)(2,1)} %multiply_convert_fusion.3.tz_ref), custom_call_target="tpu_custom_call" | custom-call | tf_op jit(solution)/shard_map/pallas_call | solution.py:132
  38.0 6.2 %copy.29 = bf16[16,2,64,512]{2,0,3,1:T(8,128)(2,1)} copy(bf16[16,2,64,512]{3,2,1,0:T(8,128)(2,1)} %get-tuple-element.9) | data formatting | bytes 4194304 | tf_op jit(solution)/shard_map/reshape | solution.py:439
  44.2 3.6 %fusion.1 = bf16[2,64,32,32]{1,2,3,0:T(8,128)(2,1)S(1)} fusion(bf16[16,2,64,32,16]{2,0,4,3,1:T(8,128)(2,1)} %bitcast.48, s32[16,16]{0,1:T(8,128)S(1)} %multiply_add_fusion, s32[32]{0:T(128)S(1)} %add_select_fusion.5, pred[32]{0:T(512)(128)(4,1)S(1)} %iota_compare_fusion), kind=kOutput, calls=%fused_computation.2 | convolution fusion | flops 67379200 | bytes 2360480 | tf_op jit(solution)/shard_map/smcxl,nsl->mcnx/dot_general | solution.py:440
  47.8 0.2 copy.31
  48.1 1.1 reshape.89
  49.2 7.2 %all-to-all-start = ((bf16[8,2,8192]{2,1,0:T(2,128)(2,1)}), bf16[8,2,8192]{2,1,0:T(2,128)(2,1)S(1)}, u32[]{:S(2)}, u32[]{:S(2)}) async-start(bf16[8,2,8192]{2,1,0:T(2,128)(2,1)} %reshape.89), calls=%async_computation | async-start | bytes 524288 | tf_op jit(solution)/shard_map/all_to_all | solution.py:444
  56.4 0.1 iota.94
  56.5 1.2 multiply_convert_fusion.tyt_ref
  57.6 6.2 %all-to-all-done = bf16[8,2,8192]{2,1,0:T(2,128)(2,1)S(1)} async-done(((bf16[8,2,8192]{2,1,0:T(2,128)(2,1)}), bf16[8,2,8192]{2,1,0:T(2,128)(2,1)S(1)}, u32[]{:S(2)}, u32[]{:S(2)}) %all-to-all-start) | async-done | bytes 262176 | tf_op jit(solution)/shard_map/all_to_all | solution.py:444
  63.8 0.3 reshape.90
  64.2 1.0 fusion.35
  65.2 8.2 %shard_map.68 = (f32[256,1024]{1,0:T(8,128)}, bf16[256,32]{1,0:T(8,128)(2,1)}) custom-call(f32[256,64]{1,0:T(8,128)} %bitcast.55, bf16[256,1024]{1,0:T(8,128)(2,1)} %bitcast.56), custom_call_target="tpu_custom_call" | custom-call | tf_op jit(solution)/shard_map/pallas_call | solution.py:416
  73.4 0.9 copy.22
  74.4 0.4 convolution_convert_fusion
  74.8 0.3 copy.23
  75.1 1.2 reshape.91
  76.2 3.6 %all-to-all-start.1 = ((bf16[8,2,4096]{2,1,0:T(2,128)(2,1)}), bf16[8,2,4096]{2,1,0:T(2,128)(2,1)S(1)}, u32[]{:S(2)}, u32[]{:S(2)}) async-start(bf16[8,2,4096]{2,1,0:T(2,128)(2,1)} %reshape.91), calls=%async_computation.1 | async-start | bytes 262144 | tf_op jit(solution)/shard_map/all_to_all | solution.py:458
  79.8 0.8 multiply_convert_fusion.2.tz_ref
  80.7 5.9 %all-to-all-done.1 = bf16[8,2,4096]{2,1,0:T(2,128)(2,1)S(1)} async-done(((bf16[8,2,4096]{2,1,0:T(2,128)(2,1)}), bf16[8,2,4096]{2,1,0:T(2,128)(2,1)S(1)}, u32[]{:S(2)}, u32[]{:S(2)}) %all-to-all-start.1) | async-done | bytes 131104 | tf_op jit(solution)/shard_map/all_to_all | solution.py:458
  86.6 0.3 reshape.92
  86.9 1.7 %copy.24 = bf16[2,32,4,8,32]{4,2,3,1,0:T(4,128)(2,1)} copy(bf16[2,32,4,8,32]{1,2,0,4,3:T(4,128)(2,1)S(1)} %bitcast.52) | data formatting | bytes 262144 | tf_op jit(solution)/shard_map/all_to_all | solution.py:458
  88.6 32.1 %shard_map.69 = (bf16[32,32,16,256]{3,2,1,0:T(8,128)(2,1)}, f32[32,32]{1,0:T(8,128)}) custom-call(bf16[32,32,16,256]{3,2,1,0:T(8,128)(2,1)} %h_ref.3, bf16[32,32,16,256]{3,2,1,0:T(8,128)(2,1)} %g_ref.3, bf16[2,32,32,32]{3,2,1,0:T(8,128)(2,1)} %bitcast.49, bf16[256,32]{1,0:T(8,128)(2,1)} %multiply_convert_fusion.tyt_ref, ...), custom_call_target="tpu_custom_call" | custom-call | tf_op jit(solution)/shard_map/pallas_call | solution.py:338
  120.8 0.0 copy-start
  120.8 7.7 %copy.34 = bf16[32,32,16,256]{3,2,1,0:T(8,128)(2,1)} copy(bf16[32,32,16,256]{3,2,1,0:T(8,128)(2,1)} %get-tuple-element.18) | data formatting | bytes 16777216
  128.4 0.0 copy-done
  128.4 0.6 copy.35
  (7 shorter events, 0.1 us)
Async XLA Ops:
  49.2 14.7 %all-to-all-start = ((bf16[8,2,8192]{2,1,0:T(2,128)(2,1)}), bf16[8,2,8192]{2,1,0:T(2,128)(2,1)S(1)}, u32[]{:S(2)}, u32[]{:S(2)}) async-start(bf16[8,2,8192]{2,1,0:T(2,128)(2,1)} %reshape.89), calls=%async_computation | async-start | bytes 524288 | tf_op jit(solution)/shard_map/all_to_all | solution.py:444
  76.2 10.3 %all-to-all-start.1 = ((bf16[8,2,4096]{2,1,0:T(2,128)(2,1)}), bf16[8,2,4096]{2,1,0:T(2,128)(2,1)S(1)}, u32[]{:S(2)}, u32[]{:S(2)}) async-start(bf16[8,2,4096]{2,1,0:T(2,128)(2,1)} %reshape.91), calls=%async_computation.1 | async-start | bytes 262144 | tf_op jit(solution)/shard_map/all_to_all | solution.py:458
  120.8 7.7 %copy-start = (f32[32,32]{1,0:T(8,128)S(1)}, f32[32,32]{1,0:T(8,128)}, u32[]{:S(2)}) copy-start(f32[32,32]{1,0:T(8,128)} %get-tuple-element.20) | copy-start | bytes 12292

commit v12 on v10

--- a/solution.py
+++ b/solution.py
@@ -155,6 +155,59 @@
             collective_id=0, has_side_effects=True,
         ),
     )(hidden_pre, cotangent, table_z)
+
+
+def exchange_kernel(axis, count, src_ref, dst_ref, local_sem, send_sems, recv_sems):
+    mesh_ids = pl.DeviceIdType.MESH
+    me = lax.axis_index(axis)
+    barrier = pltpu.get_barrier_semaphore()
+    for k in range(1, count):
+        peer = lax.rem(me + k, count)
+        pl.semaphore_signal(barrier, inc=1, device_id={axis: peer}, device_id_type=mesh_ids)
+    pl.semaphore_wait(barrier, count - 1)
+    local = pltpu.make_async_copy(src_ref.at[me], dst_ref.at[me], local_sem)
+    local.start()
+    sends = []
+    for k in range(1, count):
+        peer = lax.rem(me + k, count)
+        copy = pltpu.make_async_remote_copy(
+            src_ref=src_ref.at[peer],
+            dst_ref=dst_ref.at[me],
+            send_sem=send_sems.at[k],
+            recv_sem=recv_sems.at[k],
+            device_id={axis: peer},
+            device_id_type=mesh_ids,
+        )
+        copy.start()
+        sends.append(copy)
+    local.wait()
+    for k in range(1, count):
+        sends[k - 1].wait_send()
+        origin = lax.rem(me + count - k, count)
+        incoming = pltpu.make_async_remote_copy(
+            src_ref=src_ref.at[me],
+            dst_ref=dst_ref.at[origin],
+            send_sem=send_sems.at[k],
+            recv_sem=recv_sems.at[k],
+            device_id={axis: origin},
+            device_id_type=mesh_ids,
+        )
+        incoming.wait_recv()
+
+
+def exchange(chunks, axis, count, collective_id):
+    return pl.pallas_call(
+        functools.partial(exchange_kernel, axis, count),
+        in_specs=[pl.BlockSpec(memory_space=pl.ANY)],
+        out_specs=pl.BlockSpec(memory_space=pl.ANY),
+        out_shape=jax.ShapeDtypeStruct(chunks.shape, chunks.dtype),
+        scratch_shapes=[
+            pltpu.SemaphoreType.DMA,
+            pltpu.SemaphoreType.DMA((count,)),
+            pltpu.SemaphoreType.DMA((count,)),
+        ],
+        compiler_params=pltpu.CompilerParams(collective_id=collective_id, has_side_effects=True),
+    )(chunks)
 
 
 def synthesis_kernel(axis, count, other, others, h_ref, g_ref, xs_ref, tyt_ref, tz_ref, sw_ref,
@@ -444,12 +497,18 @@
     zc, gram = analysis(hidden_pre, cotangent, table_z, "narrow", n_narrow)
     mz_local = mode_count // n_narrow
     zc = zc.reshape(n_narrow, mz_local, 2 * channels, nx, ny)
+    my_local = mode_count // n_wide
     ycoeffs = jnp.einsum(
-        "smcxl,nsl->mcnx", zc, table_y.reshape(mode_count, n_narrow, ny),
+        "smcxl,dnsl->dnmcx", zc, table_y.reshape(n_wide, my_local, n_narrow, ny),
         preferred_element_type=jnp.float32,
     ).astype(jnp.bfloat16)
-    ycoeffs = lax.all_to_all(ycoeffs, "wide", split_axis=2, concat_axis=3, tiled=True)
-    spectra = jnp.einsum("zcyx,kx->zykc", ycoeffs, table_x, preferred_element_type=jnp.float32)
+    ycoeffs = ycoeffs.reshape(n_wide, 16, -1)
+    ycoeffs = exchange(ycoeffs, "wide", n_wide, 2)
+    ycoeffs = ycoeffs.reshape(n_wide, my_local, mz_local, 2 * channels, nx)
+    spectra = jnp.einsum(
+        "snmcx,ksx->mnkc", ycoeffs, table_x.reshape(mode_count, n_wide, nx),
+        preferred_element_type=jnp.float32,
+    )
     z_local, y_local = (spectra.shape[0], spectra.shape[1])
     grad_modes, back_spec = modes_step(
         spectra.reshape(z_local * y_local * mode_count, 2 * channels),
@@ -460,9 +519,13 @@
         back_spec.reshape(z_local, y_local, mode_count, channels), (0, 3, 1, 2)
     )
     xsynth = jnp.einsum(
-        "zcyk,kx->zcyx", back_spec, table_x, preferred_element_type=jnp.float32
+        "zcyk,kdx->dzcyx", back_spec, table_x.reshape(mode_count, n_wide, nx),
+        preferred_element_type=jnp.float32,
     ).astype(jnp.bfloat16)
-    xsynth = lax.all_to_all(xsynth, "wide", split_axis=3, concat_axis=2, tiled=True)
+    xsynth = xsynth.reshape(n_wide, mz_local * channels, -1)
+    xsynth = exchange(xsynth, "wide", n_wide, 3)
+    xsynth = xsynth.reshape(n_wide, mz_local, channels, my_local, nx)
+    xsynth = jnp.transpose(xsynth, (1, 2, 0, 3, 4)).reshape(mz_local, channels, mode_count, nx)
     table_zp = jnp.transpose(table_z.reshape(n_narrow, mz_local, nz), (1, 0, 2)).reshape(mode_count, nz)
     grad_hidden, grad_skip = synthesis(
         hidden_pre, cotangent, xsynth, jnp.transpose(table_y), table_zp, skip_weight, gram,

time: 126 us -> 126 us (level)
  Pallas kernels: 73.8 us -> 91.9 us
  waiting for transfers between devices: 12.1 us -> 0 us
  starting transfers between devices: 10.8 us -> 0 us
  local copies, waits for them, and re-layouts: 20.7 us -> 23.9 us
  matrix products: 4.98 us -> 6.31 us
    pallas_call x0 -> x2, Pallas kernels: none -> 18.8 us  [exchange(): pl.pallas_call(functools.partial(exchange_kernel, axis, count), in_specs=...]
    all_to_all x2 -> x0, waiting for transfers between devices: 12.1 us -> none  [the longest x1 6.18 us: per_device(): lax.all_to_all(ycoeffs, 'wide', split_axis=2, concat_axis=3, tiled=True)]
    all_to_all x2 -> x0, starting transfers between devices: 10.8 us -> none  [the longest x1 7.21 us: per_device(): lax.all_to_all(ycoeffs, 'wide', split_axis=2, concat_axis=3, tiled=True)]
    reshape x0 -> x5, local copies, waits for them, and re-layouts: none -> 6.89 us  [the longest x2 2.12 us: per_device(): xsynth = xsynth.reshape(n_wide, mz_local, channels, my_local, nx)]
    unnamed x8 -> x4, local copies, waits for them, and re-layouts: 11.1 us -> 8.27 us
    all_to_all x2 -> x0, local copies, waits for them, and re-layouts: 1.77 us -> none  [the longest x1 1.73 us: per_device(): lax.all_to_all(xsynth, 'wide', split_axis=3, concat_axis=2, tiled=True)]
    dot_general x3, matrix products: 4.98 us -> 6.31 us  [the longest x1 4.48 us: per_device(): jnp.einsum('smcxl,dnsl->dnmcx', zc, table_y.reshape(n_wide, my_local, n_n...]
  transfers between devices with their start and end apart: 2 -> 0, of which waited for: 2 -> 0; matrix products, arithmetic and copies ran while one was open for 2% -> 0% of each run, Pallas kernels for 0% -> 0%
where the time goes in v12:
time: 126 us
  Pallas kernels  91.9 us (73%)
  local copies, waits for them, and re-layouts  23.9 us (19%)
  matrix products  6.31 us (5%)
  other arithmetic  2.85 us (2%)
    pallas_call x1, Pallas kernels, analysis(): pl.pallas_call(functools.partial(analysis_kernel, axis, count), grid=(ste...  36.5 us
    pallas_call x1, Pallas kernels, synthesis(): pl.pallas_call(functools.partial(synthesis_kernel, axis, count, other, ot...  31.5 us
    pallas_call x2, Pallas kernels, exchange(): pl.pallas_call(functools.partial(exchange_kernel, axis, count), in_specs=...  18.8 us
    unnamed x4, local copies, waits for them, and re-layouts  8.27 us
    reshape x1, local copies, waits for them, and re-layouts, per_device(): zc = zc.reshape(n_narrow, mz_local, 2 * channels, nx, ny)  6.22 us
    pallas_call x1, Pallas kernels, modes_step(): pl.pallas_call(modes_kernel, in_specs=[vmem, vmem], out_specs=[vmem, vmem...  5.16 us
    dot_general x1, matrix products, per_device(): jnp.einsum('smcxl,dnsl->dnmcx', zc, table_y.reshape(n_wide, my_local, n_n...  4.48 us
    convert_element_type x3, other arithmetic, basis_table(): return (values_table * (1.0 / math.sqrt(length))).astype(jnp.bfloat16)  2.8 us

profile of v12, /device:TPU:1, one launch (start us, length us, event | category | flops | bytes accessed | tf_op | source)
XLA Modules:
  0.0 125.8 jit_solution(16726928143716678968)
XLA Ops:
  0.7 0.1 iota.131
  0.8 0.8 multiply_convert_fusion.3.tz_ref
  1.6 0.8 multiply_convert_fusion.4.tz_ref
  2.4 1.2 multiply_convert_fusion.1.tyt_ref
  3.6 36.5 %shard_map.67 = (bf16[16,2,64,512]{3,2,1,0:T(8,128)(2,1)}, f32[32,32]{1,0:T(8,128)}) custom-call(bf16[32,32,16,256]{3,2,1,0:T(8,128)(2,1)} %h_ref.3, bf16[32,32,16,256]{3,2,1,0:T(8,128)(2,1)} %g_ref.3, bf16[32,256]{1,0:T(8,128)(2,1)} %multiply_convert_fusion.4.tz_ref), custom_call_target="tpu_custom_call" | custom-call | tf_op jit(solution)/shard_map/pallas_call | solution.py:132
  40.1 6.2 %copy.31 = bf16[16,2,64,512]{2,0,3,1:T(8,128)(2,1)} copy(bf16[16,2,64,512]{3,2,1,0:T(8,128)(2,1)} %get-tuple-element.9) | data formatting | bytes 4194304 | tf_op jit(solution)/shard_map/reshape | solution.py:499
  46.3 4.5 %fusion = bf16[8,4,2,64,32]{3,0,4,2,1:T(8,128)(2,1)S(1)} fusion(bf16[16,2,64,32,16,1]{2,0,4,3,1,5:T(8,128)(2,1)} %bitcast.48, s32[16,16]{0,1:T(8,128)S(1)} %multiply_add_fusion, s32[8,4]{0,1:T(4,128)S(1)} %add_select_fusion.5, pred[8,4]{0,1:T(4,128)(4,1)S(1)} %fusion.46), kind=kOutput, calls=%fused_computation.1 | convolution fusion | flops 67379200 | bytes 2360480 | tf_op jit(solution)/shard_map/smcxl,dnsl->dnmcx/dot_general | solution.py:501
  50.8 0.6 copy.17
  51.4 1.8 %reshape.143.src_ref = bf16[8,16,1024]{2,1,0:T(8,128)(2,1)} reshape(bf16[8,4,2,64,32]{4,3,2,1,0:T(8,128)(2,1)S(1)} %copy.17) | data formatting | bytes 524288 | tf_op jit(solution)/shard_map/reshape | solution.py:505
  53.2 10.0 %shard_map.68 = bf16[8,16,1024]{2,1,0:T(8,128)(2,1)} custom-call(bf16[8,16,1024]{2,1,0:T(8,128)(2,1)} %reshape.143.src_ref), custom_call_target="tpu_custom_call" | custom-call | tf_op jit(solution)/shard_map/pallas_call | solution.py:199
  63.2 2.0 %reshape.144 = bf16[8,4,2,64,32]{4,3,2,1,0:T(8,128)(2,1)S(1)} reshape(bf16[8,16,1024]{2,1,0:T(8,128)(2,1)} %shard_map.68) | data formatting | bytes 524288 | tf_op jit(solution)/shard_map/reshape | solution.py:507
  65.2 1.0 convolution_bitcast_fusion.1
  66.3 0.7 copy.20
  66.9 5.2 %shard_map.69 = (f32[256,1024]{1,0:T(8,128)}, bf16[256,32]{1,0:T(8,128)(2,1)}) custom-call(f32[256,64]{1,0:T(8,128)} %bitcast.51, bf16[256,1024]{1,0:T(8,128)(2,1)} %bitcast.50), custom_call_target="tpu_custom_call" | custom-call | tf_op jit(solution)/shard_map/pallas_call | solution.py:476
  72.1 0.9 copy.21
  73.0 0.8 fusion.1
  73.8 0.3 copy.22
  74.2 0.9 reshape.148.src_ref
  75.1 8.8 %shard_map.70 = bf16[8,64,128]{2,1,0:T(8,128)(2,1)} custom-call(bf16[8,64,128]{2,1,0:T(8,128)(2,1)} %reshape.148.src_ref), custom_call_target="tpu_custom_call" | custom-call | tf_op jit(solution)/shard_map/pallas_call | solution.py:199
  83.9 1.1 reshape.149
  85.0 1.0 copy.23
  86.0 31.5 %shard_map.71 = (bf16[32,32,16,256]{3,2,1,0:T(8,128)(2,1)}, f32[32,32]{1,0:T(8,128)}) custom-call(bf16[32,32,16,256]{3,2,1,0:T(8,128)(2,1)} %h_ref.3, bf16[32,32,16,256]{3,2,1,0:T(8,128)(2,1)} %g_ref.3, bf16[2,32,32,32]{3,2,1,0:T(8,128)(2,1)} %bitcast.49, bf16[256,32]{1,0:T(8,128)(2,1)} %multiply_convert_fusion.1.tyt_ref, ...), custom_call_target="tpu_custom_call" | custom-call | tf_op jit(solution)/shard_map/pallas_call | solution.py:391
  117.5 0.0 copy-start
  117.5 7.7 %copy.35 = bf16[32,32,16,256]{3,2,1,0:T(8,128)(2,1)} copy(bf16[32,32,16,256]{3,2,1,0:T(8,128)(2,1)} %get-tuple-element.18) | data formatting | bytes 16777216
  125.2 0.0 copy-done
  125.2 0.6 copy.36
  (9 shorter events, 0.1 us)
Async XLA Ops:
  117.5 7.7 %copy-start = (f32[32,32]{1,0:T(8,128)S(1)}, f32[32,32]{1,0:T(8,128)}, u32[]{:S(2)}) copy-start(f32[32,32]{1,0:T(8,128)} %get-tuple-element.20) | copy-start | bytes 12292

commit v13 on v10

--- a/solution.py
+++ b/solution.py
@@ -231,12 +231,7 @@
         nlocal.start()
         for copy in nremote:
             copy.start()
-        y_synthesis_body(xs_ref, tyt_ref, send_ref, stage_ref)
-        for at in range(recv_ref.shape[1] // chunk):
-            local, remote = copies(at)
-            local.start()
-            for copy in remote:
-                copy.start()
+        y_synthesis_body(xs_ref, tyt_ref, send_ref, stage_ref, chunk, copies)
         r = lax.broadcasted_iota(jnp.int32, (rows, channels), 0)
         k = lax.broadcasted_iota(jnp.int32, (rows, channels), 1)
         expand = (r // ny == k).astype(jnp.float32)
@@ -377,24 +372,34 @@
     )(hidden_pre, cotangent, xsynth, table_yt, table_z, skip_weight, skip_terms)
 
 
-def y_synthesis_body(xs_ref, tyt_ref, out_ref, stage_ref):
+def y_synthesis_body(xs_ref, tyt_ref, out_ref, stage_ref, chunk, copies):
     mz_local, channels, modes, nx = xs_ref.shape
     blocks, _, lanes = out_ref.shape
     ny = lanes // channels
+    quarters = lanes // 128
+    xs_per = chunk // mz_local
     tyt = jnp.broadcast_to(tyt_ref[...][None], (channels,) + tyt_ref.shape)
+    parts = []
     for z in range(mz_local):
-        part = jnp.einsum(
+        parts.append(jnp.einsum(
             "cym,cmx->cyx", tyt, xs_ref[z], preferred_element_type=jnp.float32
-        ).astype(jnp.bfloat16).astype(jnp.float32)
+        ).astype(jnp.bfloat16).astype(jnp.float32))
+    for at in range(nx // xs_per):
+        for z in range(mz_local):
+            for d in range(blocks):
+                piece = parts[z][:, d * ny:(d + 1) * ny, at * xs_per:(at + 1) * xs_per]
+                piece = piece.reshape(channels * ny, xs_per).T
+                for q in range(quarters):
+                    stage_ref[d * quarters + q, pl.ds(at * chunk + z, xs_per, stride=mz_local), :] = (
+                        piece[:, q * 128:(q + 1) * 128])
         for d in range(blocks):
-            piece = part[:, d * ny:(d + 1) * ny, :].reshape(channels * ny, nx).T
-            for q in range(lanes // 128):
-                stage_ref[d * (lanes // 128) + q, pl.ds(z, nx, stride=mz_local), :] = (
-                    piece[:, q * 128:(q + 1) * 128])
-    for d in range(blocks):
-        for q in range(lanes // 128):
-            out_ref[d, :, q * 128:(q + 1) * 128] = (
-                stage_ref[d * (lanes // 128) + q].astype(out_ref.dtype))
+            for q in range(quarters):
+                out_ref[d, at * chunk:(at + 1) * chunk, q * 128:(q + 1) * 128] = (
+                    stage_ref[d * quarters + q, at * chunk:(at + 1) * chunk].astype(out_ref.dtype))
+        local, remote = copies(at)
+        local.start()
+        for copy in remote:
+            copy.start()
 
 
 def modes_kernel(sp_ref, w_ref, gm_ref, bs_ref):

time: 126 us -> 128 us (1.016)
  no operation moved by 1% of the time
where the time goes in v13:
time: 128 us; the launch traced here: 127 us
  Pallas kernels  74.9 us (59%)
  local copies, waits for them, and re-layouts  20.7 us (16%)
  waiting for transfers between devices  12.1 us (9%)
  starting transfers between devices  10.8 us (8%)
  matrix products  4.98 us (4%)
  other arithmetic  2.84 us (2%)
    pallas_call x1, Pallas kernels, analysis(): pl.pallas_call(functools.partial(analysis_kernel, axis, count), grid=(ste...  36.5 us
    pallas_call x1, Pallas kernels, synthesis(): pl.pallas_call(functools.partial(synthesis_kernel, axis, count, other, ot...  33.3 us
    unnamed x8, local copies, waits for them, and re-layouts  11.1 us
    all_to_all x1, starting transfers between devices, per_device(): lax.all_to_all(ycoeffs, 'wide', split_axis=2, concat_axis=3, tiled=True)  7.21 us
    reshape x1, local copies, waits for them, and re-layouts, per_device(): zc = zc.reshape(n_narrow, mz_local, 2 * channels, nx, ny)  6.22 us
    all_to_all x1, waiting for transfers between devices, per_device(): lax.all_to_all(ycoeffs, 'wide', split_axis=2, concat_axis=3, tiled=True)  6.18 us
    all_to_all x1, waiting for transfers between devices, per_device(): lax.all_to_all(xsynth, 'wide', split_axis=3, concat_axis=2, tiled=True)  5.96 us
    pallas_call x1, Pallas kernels, modes_step(): pl.pallas_call(modes_kernel, in_specs=[vmem, vmem], out_specs=[vmem, vmem...  5.16 us
  transfers between devices with their start and end apart: 2, of which 2 were waited for; matrix products, arithmetic and copies ran while one was open for 2% of the time, Pallas kernels for 0%

profile of v13, /device:TPU:1, one launch (start us, length us, event | category | flops | bytes accessed | tf_op | source)
XLA Modules:
  0.0 127.1 jit_solution(13971567027644673122)
XLA Ops:
  0.7 0.8 multiply_convert_fusion.3.tz_ref
  1.5 36.5 %shard_map.67 = (bf16[16,2,64,512]{3,2,1,0:T(8,128)(2,1)}, f32[32,32]{1,0:T(8,128)}) custom-call(bf16[32,32,16,256]{3,2,1,0:T(8,128)(2,1)} %h_ref.3, bf16[32,32,16,256]{3,2,1,0:T(8,128)(2,1)} %g_ref.3, bf16[32,256]{1,0:T(8,128)(2,1)} %multiply_convert_fusion.3.tz_ref), custom_call_target="tpu_custom_call" | custom-call | tf_op jit(solution)/shard_map/pallas_call | solution.py:132
  38.0 6.2 %copy.29 = bf16[16,2,64,512]{2,0,3,1:T(8,128)(2,1)} copy(bf16[16,2,64,512]{3,2,1,0:T(8,128)(2,1)} %get-tuple-element.9) | data formatting | bytes 4194304 | tf_op jit(solution)/shard_map/reshape | solution.py:451
  44.2 3.6 %fusion.1 = bf16[2,64,32,32]{1,2,3,0:T(8,128)(2,1)S(1)} fusion(bf16[16,2,64,32,16]{2,0,4,3,1:T(8,128)(2,1)} %bitcast.48, s32[16,16]{0,1:T(8,128)S(1)} %multiply_add_fusion, s32[32]{0:T(128)S(1)} %add_select_fusion.5, pred[32]{0:T(512)(128)(4,1)S(1)} %iota_compare_fusion), kind=kOutput, calls=%fused_computation.2 | convolution fusion | flops 67379200 | bytes 2360480 | tf_op jit(solution)/shard_map/smcxl,nsl->mcnx/dot_general | solution.py:452
  47.8 0.2 copy.31
  48.1 1.1 reshape.89
  49.2 7.2 %all-to-all-start = ((bf16[8,2,8192]{2,1,0:T(2,128)(2,1)}), bf16[8,2,8192]{2,1,0:T(2,128)(2,1)S(1)}, u32[]{:S(2)}, u32[]{:S(2)}) async-start(bf16[8,2,8192]{2,1,0:T(2,128)(2,1)} %reshape.89), calls=%async_computation | async-start | bytes 524288 | tf_op jit(solution)/shard_map/all_to_all | solution.py:456
  56.4 0.1 iota.94
  56.5 1.2 multiply_convert_fusion.tyt_ref
  57.6 6.2 %all-to-all-done = bf16[8,2,8192]{2,1,0:T(2,128)(2,1)S(1)} async-done(((bf16[8,2,8192]{2,1,0:T(2,128)(2,1)}), bf16[8,2,8192]{2,1,0:T(2,128)(2,1)S(1)}, u32[]{:S(2)}, u32[]{:S(2)}) %all-to-all-start) | async-done | bytes 262176 | tf_op jit(solution)/shard_map/all_to_all | solution.py:456
  63.8 0.3 reshape.90
  64.2 1.0 fusion.35
  65.2 5.2 %shard_map.68 = (f32[256,1024]{1,0:T(8,128)}, bf16[256,32]{1,0:T(8,128)(2,1)}) custom-call(f32[256,64]{1,0:T(8,128)} %bitcast.55, bf16[256,1024]{1,0:T(8,128)(2,1)} %bitcast.56), custom_call_target="tpu_custom_call" | custom-call | tf_op jit(solution)/shard_map/pallas_call | solution.py:428
  70.4 0.9 copy.22
  71.3 0.4 convolution_convert_fusion
  71.7 0.3 copy.23
  72.0 1.2 reshape.91
  73.2 3.6 %all-to-all-start.1 = ((bf16[8,2,4096]{2,1,0:T(2,128)(2,1)}), bf16[8,2,4096]{2,1,0:T(2,128)(2,1)S(1)}, u32[]{:S(2)}, u32[]{:S(2)}) async-start(bf16[8,2,4096]{2,1,0:T(2,128)(2,1)} %reshape.91), calls=%async_computation.1 | async-start | bytes 262144 | tf_op jit(solution)/shard_map/all_to_all | solution.py:470
  76.7 0.8 multiply_convert_fusion.2.tz_ref
  77.5 6.0 %all-to-all-done.1 = bf16[8,2,4096]{2,1,0:T(2,128)(2,1)S(1)} async-done(((bf16[8,2,4096]{2,1,0:T(2,128)(2,1)}), bf16[8,2,4096]{2,1,0:T(2,128)(2,1)S(1)}, u32[]{:S(2)}, u32[]{:S(2)}) %all-to-all-start.1) | async-done | bytes 131104 | tf_op jit(solution)/shard_map/all_to_all | solution.py:470
  83.5 0.3 reshape.92
  83.8 1.7 %copy.24 = bf16[2,32,4,8,32]{4,2,3,1,0:T(4,128)(2,1)} copy(bf16[2,32,4,8,32]{1,2,0,4,3:T(4,128)(2,1)S(1)} %bitcast.52) | data formatting | bytes 262144 | tf_op jit(solution)/shard_map/all_to_all | solution.py:470
  85.5 33.3 %shard_map.69 = (bf16[32,32,16,256]{3,2,1,0:T(8,128)(2,1)}, f32[32,32]{1,0:T(8,128)}) custom-call(bf16[32,32,16,256]{3,2,1,0:T(8,128)(2,1)} %h_ref.3, bf16[32,32,16,256]{3,2,1,0:T(8,128)(2,1)} %g_ref.3, bf16[2,32,32,32]{3,2,1,0:T(8,128)(2,1)} %bitcast.49, bf16[256,32]{1,0:T(8,128)(2,1)} %multiply_convert_fusion.tyt_ref, ...), custom_call_target="tpu_custom_call" | custom-call | tf_op jit(solution)/shard_map/pallas_call | solution.py:333
  118.8 0.0 copy-start
  118.8 7.7 %copy.34 = bf16[32,32,16,256]{3,2,1,0:T(8,128)(2,1)} copy(bf16[32,32,16,256]{3,2,1,0:T(8,128)(2,1)} %get-tuple-element.18) | data formatting | bytes 16777216
  126.4 0.0 copy-done
  126.4 0.6 copy.35
  (7 shorter events, 0.1 us)
Async XLA Ops:
  49.2 14.7 %all-to-all-start = ((bf16[8,2,8192]{2,1,0:T(2,128)(2,1)}), bf16[8,2,8192]{2,1,0:T(2,128)(2,1)S(1)}, u32[]{:S(2)}, u32[]{:S(2)}) async-start(bf16[8,2,8192]{2,1,0:T(2,128)(2,1)} %reshape.89), calls=%async_computation | async-start | bytes 524288 | tf_op jit(solution)/shard_map/all_to_all | solution.py:456
  73.2 10.3 %all-to-all-start.1 = ((bf16[8,2,4096]{2,1,0:T(2,128)(2,1)}), bf16[8,2,4096]{2,1,0:T(2,128)(2,1)S(1)}, u32[]{:S(2)}, u32[]{:S(2)}) async-start(bf16[8,2,4096]{2,1,0:T(2,128)(2,1)} %reshape.91), calls=%async_computation.1 | async-start | bytes 262144 | tf_op jit(solution)/shard_map/all_to_all | solution.py:470
  118.8 7.7 %copy-start = (f32[32,32]{1,0:T(8,128)S(1)}, f32[32,32]{1,0:T(8,128)}, u32[]{:S(2)}) copy-start(f32[32,32]{1,0:T(8,128)} %get-tuple-element.20) | copy-start | bytes 12292

commit v14 on v10

--- a/solution.py
+++ b/solution.py
@@ -406,9 +406,10 @@
     ec = lax.broadcasted_iota(jnp.int32, (channels, width), 1)
     spread = (ec // channels == er).astype(jnp.float32)
     tile = (ec % channels == er).astype(jnp.float32)
-    s_rep = jnp.dot(sp[:, :channels], spread, precision=highest, preferred_element_type=jnp.float32)
     q_rep = jnp.dot(sp[:, channels:], tile, precision=highest, preferred_element_type=jnp.float32)
-    gm_ref[...] = s_rep * q_rep
+    q = sp[:, channels:]
+    for c in range(channels):
+        gm_ref[:, c * channels:(c + 1) * channels] = sp[:, c:c + 1] * q
     weighted = w_ref[...].astype(jnp.float32) * q_rep
     back = lax.dot_general(
         weighted, spread, (((1,), (1,)), ((), ())), precision=highest,

time: 126 us -> 126 us (level)
  no operation moved by 1% of the time
where the time goes in v14:
time: 126 us
  Pallas kernels  73.6 us (58%)
  local copies, waits for them, and re-layouts  20.7 us (16%)
  waiting for transfers between devices  12.1 us (10%)
  starting transfers between devices  10.8 us (9%)
  matrix products  4.98 us (4%)
  other arithmetic  2.84 us (2%)
    pallas_call x1, Pallas kernels, analysis(): pl.pallas_call(functools.partial(analysis_kernel, axis, count), grid=(ste...  36.5 us
    pallas_call x1, Pallas kernels, synthesis(): pl.pallas_call(functools.partial(synthesis_kernel, axis, count, other, ot...  32.1 us
    unnamed x8, local copies, waits for them, and re-layouts  11.1 us
    all_to_all x1, starting transfers between devices, per_device(): lax.all_to_all(ycoeffs, 'wide', split_axis=2, concat_axis=3, tiled=True)  7.21 us
    reshape x1, local copies, waits for them, and re-layouts, per_device(): zc = zc.reshape(n_narrow, mz_local, 2 * channels, nx, ny)  6.22 us
    all_to_all x1, waiting for transfers between devices, per_device(): lax.all_to_all(ycoeffs, 'wide', split_axis=2, concat_axis=3, tiled=True)  6.18 us
    all_to_all x1, waiting for transfers between devices, per_device(): lax.all_to_all(xsynth, 'wide', split_axis=3, concat_axis=2, tiled=True)  5.96 us
    pallas_call x1, Pallas kernels, modes_step(): pl.pallas_call(modes_kernel, in_specs=[vmem, vmem], out_specs=[vmem, vmem...  4.99 us
  transfers between devices with their start and end apart: 2, of which 2 were waited for; matrix products, arithmetic and copies ran while one was open for 2% of the time, Pallas kernels for 0%

profile of v14, /device:TPU:1, one launch (start us, length us, event | category | flops | bytes accessed | tf_op | source)
XLA Modules:
  0.0 125.8 jit_solution(3973680995760651997)
XLA Ops:
  0.7 0.8 multiply_convert_fusion.3.tz_ref
  1.5 36.5 %shard_map.67 = (bf16[16,2,64,512]{3,2,1,0:T(8,128)(2,1)}, f32[32,32]{1,0:T(8,128)}) custom-call(bf16[32,32,16,256]{3,2,1,0:T(8,128)(2,1)} %h_ref.3, bf16[32,32,16,256]{3,2,1,0:T(8,128)(2,1)} %g_ref.3, bf16[32,256]{1,0:T(8,128)(2,1)} %multiply_convert_fusion.3.tz_ref), custom_call_target="tpu_custom_call" | custom-call | tf_op jit(solution)/shard_map/pallas_call | solution.py:132
  38.0 6.2 %copy.29 = bf16[16,2,64,512]{2,0,3,1:T(8,128)(2,1)} copy(bf16[16,2,64,512]{3,2,1,0:T(8,128)(2,1)} %get-tuple-element.9) | data formatting | bytes 4194304 | tf_op jit(solution)/shard_map/reshape | solution.py:447
  44.2 3.6 %fusion.1 = bf16[2,64,32,32]{1,2,3,0:T(8,128)(2,1)S(1)} fusion(bf16[16,2,64,32,16]{2,0,4,3,1:T(8,128)(2,1)} %bitcast.48, s32[16,16]{0,1:T(8,128)S(1)} %multiply_add_fusion, s32[32]{0:T(128)S(1)} %add_select_fusion.5, pred[32]{0:T(512)(128)(4,1)S(1)} %iota_compare_fusion), kind=kOutput, calls=%fused_computation.2 | convolution fusion | flops 67379200 | bytes 2360480 | tf_op jit(solution)/shard_map/smcxl,nsl->mcnx/dot_general | solution.py:448
  47.8 0.2 copy.31
  48.1 1.1 reshape.89
  49.2 7.2 %all-to-all-start = ((bf16[8,2,8192]{2,1,0:T(2,128)(2,1)}), bf16[8,2,8192]{2,1,0:T(2,128)(2,1)S(1)}, u32[]{:S(2)}, u32[]{:S(2)}) async-start(bf16[8,2,8192]{2,1,0:T(2,128)(2,1)} %reshape.89), calls=%async_computation | async-start | bytes 524288 | tf_op jit(solution)/shard_map/all_to_all | solution.py:452
  56.4 0.1 iota.94
  56.5 1.2 multiply_convert_fusion.tyt_ref
  57.6 6.2 %all-to-all-done = bf16[8,2,8192]{2,1,0:T(2,128)(2,1)S(1)} async-done(((bf16[8,2,8192]{2,1,0:T(2,128)(2,1)}), bf16[8,2,8192]{2,1,0:T(2,128)(2,1)S(1)}, u32[]{:S(2)}, u32[]{:S(2)}) %all-to-all-start) | async-done | bytes 262176 | tf_op jit(solution)/shard_map/all_to_all | solution.py:452
  63.8 0.3 reshape.90
  64.2 1.0 fusion.35
  65.2 5.0 %shard_map.68 = (f32[256,1024]{1,0:T(8,128)}, bf16[256,32]{1,0:T(8,128)(2,1)}) custom-call(f32[256,64]{1,0:T(8,128)} %bitcast.55, bf16[256,1024]{1,0:T(8,128)(2,1)} %bitcast.56), custom_call_target="tpu_custom_call" | custom-call | tf_op jit(solution)/shard_map/pallas_call | solution.py:424
  70.2 0.9 copy.22
  71.1 0.4 convolution_convert_fusion
  71.5 0.3 copy.23
  71.8 1.2 reshape.91
  73.0 3.6 %all-to-all-start.1 = ((bf16[8,2,4096]{2,1,0:T(2,128)(2,1)}), bf16[8,2,4096]{2,1,0:T(2,128)(2,1)S(1)}, u32[]{:S(2)}, u32[]{:S(2)}) async-start(bf16[8,2,4096]{2,1,0:T(2,128)(2,1)} %reshape.91), calls=%async_computation.1 | async-start | bytes 262144 | tf_op jit(solution)/shard_map/all_to_all | solution.py:466
  76.6 0.8 multiply_convert_fusion.2.tz_ref
  77.4 6.0 %all-to-all-done.1 = bf16[8,2,4096]{2,1,0:T(2,128)(2,1)S(1)} async-done(((bf16[8,2,4096]{2,1,0:T(2,128)(2,1)}), bf16[8,2,4096]{2,1,0:T(2,128)(2,1)S(1)}, u32[]{:S(2)}, u32[]{:S(2)}) %all-to-all-start.1) | async-done | bytes 131104 | tf_op jit(solution)/shard_map/all_to_all | solution.py:466
  83.3 0.3 reshape.92
  83.6 1.7 %copy.24 = bf16[2,32,4,8,32]{4,2,3,1,0:T(4,128)(2,1)} copy(bf16[2,32,4,8,32]{1,2,0,4,3:T(4,128)(2,1)S(1)} %bitcast.52) | data formatting | bytes 262144 | tf_op jit(solution)/shard_map/all_to_all | solution.py:466
  85.3 32.1 %shard_map.69 = (bf16[32,32,16,256]{3,2,1,0:T(8,128)(2,1)}, f32[32,32]{1,0:T(8,128)}) custom-call(bf16[32,32,16,256]{3,2,1,0:T(8,128)(2,1)} %h_ref.3, bf16[32,32,16,256]{3,2,1,0:T(8,128)(2,1)} %g_ref.3, bf16[2,32,32,32]{3,2,1,0:T(8,128)(2,1)} %bitcast.49, bf16[256,32]{1,0:T(8,128)(2,1)} %multiply_convert_fusion.tyt_ref, ...), custom_call_target="tpu_custom_call" | custom-call | tf_op jit(solution)/shard_map/pallas_call | solution.py:338
  117.5 0.0 copy-start
  117.5 7.7 %copy.34 = bf16[32,32,16,256]{3,2,1,0:T(8,128)(2,1)} copy(bf16[32,32,16,256]{3,2,1,0:T(8,128)(2,1)} %get-tuple-element.18) | data formatting | bytes 16777216
  125.2 0.0 copy-done
  125.2 0.6 copy.35
  (7 shorter events, 0.1 us)
Async XLA Ops:
  49.2 14.7 %all-to-all-start = ((bf16[8,2,8192]{2,1,0:T(2,128)(2,1)}), bf16[8,2,8192]{2,1,0:T(2,128)(2,1)S(1)}, u32[]{:S(2)}, u32[]{:S(2)}) async-start(bf16[8,2,8192]{2,1,0:T(2,128)(2,1)} %reshape.89), calls=%async_computation | async-start | bytes 524288 | tf_op jit(solution)/shard_map/all_to_all | solution.py:452
  73.0 10.3 %all-to-all-start.1 = ((bf16[8,2,4096]{2,1,0:T(2,128)(2,1)}), bf16[8,2,4096]{2,1,0:T(2,128)(2,1)S(1)}, u32[]{:S(2)}, u32[]{:S(2)}) async-start(bf16[8,2,4096]{2,1,0:T(2,128)(2,1)} %reshape.91), calls=%async_computation.1 | async-start | bytes 262144 | tf_op jit(solution)/shard_map/all_to_all | solution.py:466
  117.5 7.7 %copy-start = (f32[32,32]{1,0:T(8,128)S(1)}, f32[32,32]{1,0:T(8,128)}, u32[]{:S(2)}) copy-start(f32[32,32]{1,0:T(8,128)} %get-tuple-element.20) | copy-start | bytes 12292

commit v15 on v14

--- a/solution.py
+++ b/solution.py
@@ -48,7 +48,8 @@
             local_sems.at[at],
         )
         remote = []
-        for k in range(1, count):
+        order = [k for pair in zip(range(1, count), range(count - 1, 0, -1)) for k in pair]
+        for k in sorted(set(order), key=order.index):
             peer = lax.rem(me + k, count)
             remote.append(pltpu.make_async_remote_copy(
                 src_ref=slot_ref.at[slot, pl.ds(peer * mz_local, mz_local)],

time: 126 us -> 124 us (0.984)
  Pallas kernels: 73.6 us -> 72 us
    pallas_call x1, Pallas kernels: 32.1 us -> 30.5 us  [synthesis(): pl.pallas_call(functools.partial(synthesis_kernel, axis, count, other, ot...]
where the time goes in v15:
time: 124 us
  Pallas kernels  72 us (58%)
  local copies, waits for them, and re-layouts  20.7 us (17%)
  waiting for transfers between devices  11.9 us (10%)
  starting transfers between devices  10.8 us (9%)
  matrix products  4.98 us (4%)
  other arithmetic  2.84 us (2%)
    pallas_call x1, Pallas kernels, analysis(): pl.pallas_call(functools.partial(analysis_kernel, axis, count), grid=(ste...  36.5 us
    pallas_call x1, Pallas kernels, synthesis(): pl.pallas_call(functools.partial(synthesis_kernel, axis, count, other, ot...  30.5 us
    unnamed x8, local copies, waits for them, and re-layouts  11.1 us
    all_to_all x1, starting transfers between devices, per_device(): lax.all_to_all(ycoeffs, 'wide', split_axis=2, concat_axis=3, tiled=True)  7.21 us
    reshape x1, local copies, waits for them, and re-layouts, per_device(): zc = zc.reshape(n_narrow, mz_local, 2 * channels, nx, ny)  6.22 us
    all_to_all x1, waiting for transfers between devices, per_device(): lax.all_to_all(ycoeffs, 'wide', split_axis=2, concat_axis=3, tiled=True)  6.17 us
    all_to_all x1, waiting for transfers between devices, per_device(): lax.all_to_all(xsynth, 'wide', split_axis=3, concat_axis=2, tiled=True)  5.69 us
    pallas_call x1, Pallas kernels, modes_step(): pl.pallas_call(modes_kernel, in_specs=[vmem, vmem], out_specs=[vmem, vmem...  4.99 us
  transfers between devices with their start and end apart: 2, of which 2 were waited for; matrix products, arithmetic and copies ran while one was open for 2% of the time, Pallas kernels for 0%

profile of v15, /device:TPU:1, one launch (start us, length us, event | category | flops | bytes accessed | tf_op | source)
XLA Modules:
  0.0 123.9 jit_solution(6389535986028599132)
XLA Ops:
  0.7 0.8 multiply_convert_fusion.3.tz_ref
  1.5 36.5 %shard_map.67 = (bf16[16,2,64,512]{3,2,1,0:T(8,128)(2,1)}, f32[32,32]{1,0:T(8,128)}) custom-call(bf16[32,32,16,256]{3,2,1,0:T(8,128)(2,1)} %h_ref.3, bf16[32,32,16,256]{3,2,1,0:T(8,128)(2,1)} %g_ref.3, bf16[32,256]{1,0:T(8,128)(2,1)} %multiply_convert_fusion.3.tz_ref), custom_call_target="tpu_custom_call" | custom-call | tf_op jit(solution)/shard_map/pallas_call | solution.py:133
  38.0 6.2 %copy.29 = bf16[16,2,64,512]{2,0,3,1:T(8,128)(2,1)} copy(bf16[16,2,64,512]{3,2,1,0:T(8,128)(2,1)} %get-tuple-element.9) | data formatting | bytes 4194304 | tf_op jit(solution)/shard_map/reshape | solution.py:448
  44.2 3.6 %fusion.1 = bf16[2,64,32,32]{1,2,3,0:T(8,128)(2,1)S(1)} fusion(bf16[16,2,64,32,16]{2,0,4,3,1:T(8,128)(2,1)} %bitcast.48, s32[16,16]{0,1:T(8,128)S(1)} %multiply_add_fusion, s32[32]{0:T(128)S(1)} %add_select_fusion.5, pred[32]{0:T(512)(128)(4,1)S(1)} %iota_compare_fusion), kind=kOutput, calls=%fused_computation.2 | convolution fusion | flops 67379200 | bytes 2360480 | tf_op jit(solution)/shard_map/smcxl,nsl->mcnx/dot_general | solution.py:449
  47.9 0.2 copy.31
  48.1 1.1 reshape.89
  49.2 7.2 %all-to-all-start = ((bf16[8,2,8192]{2,1,0:T(2,128)(2,1)}), bf16[8,2,8192]{2,1,0:T(2,128)(2,1)S(1)}, u32[]{:S(2)}, u32[]{:S(2)}) async-start(bf16[8,2,8192]{2,1,0:T(2,128)(2,1)} %reshape.89), calls=%async_computation | async-start | bytes 524288 | tf_op jit(solution)/shard_map/all_to_all | solution.py:453
  56.4 0.1 iota.94
  56.5 1.2 multiply_convert_fusion.tyt_ref
  57.6 6.2 %all-to-all-done = bf16[8,2,8192]{2,1,0:T(2,128)(2,1)S(1)} async-done(((bf16[8,2,8192]{2,1,0:T(2,128)(2,1)}), bf16[8,2,8192]{2,1,0:T(2,128)(2,1)S(1)}, u32[]{:S(2)}, u32[]{:S(2)}) %all-to-all-start) | async-done | bytes 262176 | tf_op jit(solution)/shard_map/all_to_all | solution.py:453
  63.8 0.3 reshape.90
  64.2 1.0 fusion.35
  65.2 5.0 %shard_map.68 = (f32[256,1024]{1,0:T(8,128)}, bf16[256,32]{1,0:T(8,128)(2,1)}) custom-call(f32[256,64]{1,0:T(8,128)} %bitcast.55, bf16[256,1024]{1,0:T(8,128)(2,1)} %bitcast.56), custom_call_target="tpu_custom_call" | custom-call | tf_op jit(solution)/shard_map/pallas_call | solution.py:425
  70.2 0.9 copy.22
  71.1 0.4 convolution_convert_fusion
  71.5 0.3 copy.23
  71.8 1.2 reshape.91
  73.0 3.6 %all-to-all-start.1 = ((bf16[8,2,4096]{2,1,0:T(2,128)(2,1)}), bf16[8,2,4096]{2,1,0:T(2,128)(2,1)S(1)}, u32[]{:S(2)}, u32[]{:S(2)}) async-start(bf16[8,2,4096]{2,1,0:T(2,128)(2,1)} %reshape.91), calls=%async_computation.1 | async-start | bytes 262144 | tf_op jit(solution)/shard_map/all_to_all | solution.py:467
  76.6 0.8 multiply_convert_fusion.2.tz_ref
  77.4 5.7 %all-to-all-done.1 = bf16[8,2,4096]{2,1,0:T(2,128)(2,1)S(1)} async-done(((bf16[8,2,4096]{2,1,0:T(2,128)(2,1)}), bf16[8,2,4096]{2,1,0:T(2,128)(2,1)S(1)}, u32[]{:S(2)}, u32[]{:S(2)}) %all-to-all-start.1) | async-done | bytes 131104 | tf_op jit(solution)/shard_map/all_to_all | solution.py:467
  83.1 0.3 reshape.92
  83.3 1.7 %copy.24 = bf16[2,32,4,8,32]{4,2,3,1,0:T(4,128)(2,1)} copy(bf16[2,32,4,8,32]{1,2,0,4,3:T(4,128)(2,1)S(1)} %bitcast.52) | data formatting | bytes 262144 | tf_op jit(solution)/shard_map/all_to_all | solution.py:467
  85.1 30.5 %shard_map.69 = (bf16[32,32,16,256]{3,2,1,0:T(8,128)(2,1)}, f32[32,32]{1,0:T(8,128)}) custom-call(bf16[32,32,16,256]{3,2,1,0:T(8,128)(2,1)} %h_ref.3, bf16[32,32,16,256]{3,2,1,0:T(8,128)(2,1)} %g_ref.3, bf16[2,32,32,32]{3,2,1,0:T(8,128)(2,1)} %bitcast.49, bf16[256,32]{1,0:T(8,128)(2,1)} %multiply_convert_fusion.tyt_ref, ...), custom_call_target="tpu_custom_call" | custom-call | tf_op jit(solution)/shard_map/pallas_call | solution.py:339
  115.6 0.0 copy-start
  115.6 7.7 %copy.34 = bf16[32,32,16,256]{3,2,1,0:T(8,128)(2,1)} copy(bf16[32,32,16,256]{3,2,1,0:T(8,128)(2,1)} %get-tuple-element.18) | data formatting | bytes 16777216
  123.3 0.0 copy-done
  123.3 0.6 copy.35
  (7 shorter events, 0.1 us)
Async XLA Ops:
  49.2 14.6 %all-to-all-start = ((bf16[8,2,8192]{2,1,0:T(2,128)(2,1)}), bf16[8,2,8192]{2,1,0:T(2,128)(2,1)S(1)}, u32[]{:S(2)}, u32[]{:S(2)}) async-start(bf16[8,2,8192]{2,1,0:T(2,128)(2,1)} %reshape.89), calls=%async_computation | async-start | bytes 524288 | tf_op jit(solution)/shard_map/all_to_all | solution.py:453
  73.0 10.1 %all-to-all-start.1 = ((bf16[8,2,4096]{2,1,0:T(2,128)(2,1)}), bf16[8,2,4096]{2,1,0:T(2,128)(2,1)S(1)}, u32[]{:S(2)}, u32[]{:S(2)}) async-start(bf16[8,2,4096]{2,1,0:T(2,128)(2,1)} %reshape.91), calls=%async_computation.1 | async-start | bytes 262144 | tf_op jit(solution)/shard_map/all_to_all | solution.py:467
  115.6 7.7 %copy-start = (f32[32,32]{1,0:T(8,128)S(1)}, f32[32,32]{1,0:T(8,128)}, u32[]{:S(2)}) copy-start(f32[32,32]{1,0:T(8,128)} %get-tuple-element.20) | copy-start | bytes 12292

commit v16 on v15

--- a/solution.py
+++ b/solution.py
@@ -206,7 +206,8 @@
         local = pltpu.make_async_copy(
             send_ref.at[me, part], recv_ref.at[me, part], local_sems.at[at])
         remote = []
-        for k in range(1, count):
+        order = [k for pair in zip(range(1, count), range(count - 1, 0, -1)) for k in pair]
+        for k in sorted(set(order), key=order.index):
             peer = lax.rem(me + k, count)
             remote.append(pltpu.make_async_remote_copy(
                 src_ref=send_ref.at[peer, part],

time: 124 us -> 125 us (level)
  no operation moved by 1% of the time
where the time goes in v16:
time: 125 us; the launch traced here: 124 us
  Pallas kernels  71.8 us (57%)
  local copies, waits for them, and re-layouts  20.7 us (17%)
  waiting for transfers between devices  11.9 us (10%)
  starting transfers between devices  10.8 us (9%)
  matrix products  4.98 us (4%)
  other arithmetic  2.84 us (2%)
    pallas_call x1, Pallas kernels, analysis(): pl.pallas_call(functools.partial(analysis_kernel, axis, count), grid=(ste...  36.5 us
    pallas_call x1, Pallas kernels, synthesis(): pl.pallas_call(functools.partial(synthesis_kernel, axis, count, other, ot...  30.3 us
    unnamed x8, local copies, waits for them, and re-layouts  11.1 us
    all_to_all x1, starting transfers between devices, per_device(): lax.all_to_all(ycoeffs, 'wide', split_axis=2, concat_axis=3, tiled=True)  7.21 us
    reshape x1, local copies, waits for them, and re-layouts, per_device(): zc = zc.reshape(n_narrow, mz_local, 2 * channels, nx, ny)  6.22 us
    all_to_all x1, waiting for transfers between devices, per_device(): lax.all_to_all(ycoeffs, 'wide', split_axis=2, concat_axis=3, tiled=True)  6.17 us
    all_to_all x1, waiting for transfers between devices, per_device(): lax.all_to_all(xsynth, 'wide', split_axis=3, concat_axis=2, tiled=True)  5.69 us
    pallas_call x1, Pallas kernels, modes_step(): pl.pallas_call(modes_kernel, in_specs=[vmem, vmem], out_specs=[vmem, vmem...  4.99 us
  transfers between devices with their start and end apart: 2, of which 2 were waited for; matrix products, arithmetic and copies ran while one was open for 2% of the time, Pallas kernels for 0%

profile of v16, /device:TPU:1, one launch (start us, length us, event | category | flops | bytes accessed | tf_op | source)
XLA Modules:
  0.0 123.7 jit_solution(2176874983391735482)
XLA Ops:
  0.7 0.8 multiply_convert_fusion.3.tz_ref
  1.5 36.5 %shard_map.67 = (bf16[16,2,64,512]{3,2,1,0:T(8,128)(2,1)}, f32[32,32]{1,0:T(8,128)}) custom-call(bf16[32,32,16,256]{3,2,1,0:T(8,128)(2,1)} %h_ref.3, bf16[32,32,16,256]{3,2,1,0:T(8,128)(2,1)} %g_ref.3, bf16[32,256]{1,0:T(8,128)(2,1)} %multiply_convert_fusion.3.tz_ref), custom_call_target="tpu_custom_call" | custom-call | tf_op jit(solution)/shard_map/pallas_call | solution.py:133
  38.0 6.2 %copy.29 = bf16[16,2,64,512]{2,0,3,1:T(8,128)(2,1)} copy(bf16[16,2,64,512]{3,2,1,0:T(8,128)(2,1)} %get-tuple-element.9) | data formatting | bytes 4194304 | tf_op jit(solution)/shard_map/reshape | solution.py:449
  44.2 3.6 %fusion.1 = bf16[2,64,32,32]{1,2,3,0:T(8,128)(2,1)S(1)} fusion(bf16[16,2,64,32,16]{2,0,4,3,1:T(8,128)(2,1)} %bitcast.48, s32[16,16]{0,1:T(8,128)S(1)} %multiply_add_fusion, s32[32]{0:T(128)S(1)} %add_select_fusion.5, pred[32]{0:T(512)(128)(4,1)S(1)} %iota_compare_fusion), kind=kOutput, calls=%fused_computation.2 | convolution fusion | flops 67379200 | bytes 2360480 | tf_op jit(solution)/shard_map/smcxl,nsl->mcnx/dot_general | solution.py:450
  47.9 0.2 copy.31
  48.1 1.1 reshape.89
  49.2 7.2 %all-to-all-start = ((bf16[8,2,8192]{2,1,0:T(2,128)(2,1)}), bf16[8,2,8192]{2,1,0:T(2,128)(2,1)S(1)}, u32[]{:S(2)}, u32[]{:S(2)}) async-start(bf16[8,2,8192]{2,1,0:T(2,128)(2,1)} %reshape.89), calls=%async_computation | async-start | bytes 524288 | tf_op jit(solution)/shard_map/all_to_all | solution.py:454
  56.4 0.1 iota.94
  56.5 1.2 multiply_convert_fusion.tyt_ref
  57.6 6.2 %all-to-all-done = bf16[8,2,8192]{2,1,0:T(2,128)(2,1)S(1)} async-done(((bf16[8,2,8192]{2,1,0:T(2,128)(2,1)}), bf16[8,2,8192]{2,1,0:T(2,128)(2,1)S(1)}, u32[]{:S(2)}, u32[]{:S(2)}) %all-to-all-start) | async-done | bytes 262176 | tf_op jit(solution)/shard_map/all_to_all | solution.py:454
  63.8 0.3 reshape.90
  64.2 1.0 fusion.35
  65.2 5.0 %shard_map.68 = (f32[256,1024]{1,0:T(8,128)}, bf16[256,32]{1,0:T(8,128)(2,1)}) custom-call(f32[256,64]{1,0:T(8,128)} %bitcast.55, bf16[256,1024]{1,0:T(8,128)(2,1)} %bitcast.56), custom_call_target="tpu_custom_call" | custom-call | tf_op jit(solution)/shard_map/pallas_call | solution.py:426
  70.2 0.9 copy.22
  71.1 0.4 convolution_convert_fusion
  71.5 0.3 copy.23
  71.8 1.2 reshape.91
  73.0 3.6 %all-to-all-start.1 = ((bf16[8,2,4096]{2,1,0:T(2,128)(2,1)}), bf16[8,2,4096]{2,1,0:T(2,128)(2,1)S(1)}, u32[]{:S(2)}, u32[]{:S(2)}) async-start(bf16[8,2,4096]{2,1,0:T(2,128)(2,1)} %reshape.91), calls=%async_computation.1 | async-start | bytes 262144 | tf_op jit(solution)/shard_map/all_to_all | solution.py:468
  76.6 0.8 multiply_convert_fusion.2.tz_ref
  77.4 5.7 %all-to-all-done.1 = bf16[8,2,4096]{2,1,0:T(2,128)(2,1)S(1)} async-done(((bf16[8,2,4096]{2,1,0:T(2,128)(2,1)}), bf16[8,2,4096]{2,1,0:T(2,128)(2,1)S(1)}, u32[]{:S(2)}, u32[]{:S(2)}) %all-to-all-start.1) | async-done | bytes 131104 | tf_op jit(solution)/shard_map/all_to_all | solution.py:468
  83.1 0.3 reshape.92
  83.3 1.7 %copy.24 = bf16[2,32,4,8,32]{4,2,3,1,0:T(4,128)(2,1)} copy(bf16[2,32,4,8,32]{1,2,0,4,3:T(4,128)(2,1)S(1)} %bitcast.52) | data formatting | bytes 262144 | tf_op jit(solution)/shard_map/all_to_all | solution.py:468
  85.1 30.3 %shard_map.69 = (bf16[32,32,16,256]{3,2,1,0:T(8,128)(2,1)}, f32[32,32]{1,0:T(8,128)}) custom-call(bf16[32,32,16,256]{3,2,1,0:T(8,128)(2,1)} %h_ref.3, bf16[32,32,16,256]{3,2,1,0:T(8,128)(2,1)} %g_ref.3, bf16[2,32,32,32]{3,2,1,0:T(8,128)(2,1)} %bitcast.49, bf16[256,32]{1,0:T(8,128)(2,1)} %multiply_convert_fusion.tyt_ref, ...), custom_call_target="tpu_custom_call" | custom-call | tf_op jit(solution)/shard_map/pallas_call | solution.py:340
  115.4 0.0 copy-start
  115.4 7.7 %copy.34 = bf16[32,32,16,256]{3,2,1,0:T(8,128)(2,1)} copy(bf16[32,32,16,256]{3,2,1,0:T(8,128)(2,1)} %get-tuple-element.18) | data formatting | bytes 16777216
  123.0 0.0 copy-done
  123.0 0.6 copy.35
  (7 shorter events, 0.1 us)
Async XLA Ops:
  49.2 14.6 %all-to-all-start = ((bf16[8,2,8192]{2,1,0:T(2,128)(2,1)}), bf16[8,2,8192]{2,1,0:T(2,128)(2,1)S(1)}, u32[]{:S(2)}, u32[]{:S(2)}) async-start(bf16[8,2,8192]{2,1,0:T(2,128)(2,1)} %reshape.89), calls=%async_computation | async-start | bytes 524288 | tf_op jit(solution)/shard_map/all_to_all | solution.py:454
  73.0 10.1 %all-to-all-start.1 = ((bf16[8,2,4096]{2,1,0:T(2,128)(2,1)}), bf16[8,2,4096]{2,1,0:T(2,128)(2,1)S(1)}, u32[]{:S(2)}, u32[]{:S(2)}) async-start(bf16[8,2,4096]{2,1,0:T(2,128)(2,1)} %reshape.91), calls=%async_computation.1 | async-start | bytes 262144 | tf_op jit(solution)/shard_map/all_to_all | solution.py:468
  115.4 7.7 %copy-start = (f32[32,32]{1,0:T(8,128)S(1)}, f32[32,32]{1,0:T(8,128)}, u32[]{:S(2)}) copy-start(f32[32,32]{1,0:T(8,128)} %get-tuple-element.20) | copy-start | bytes 12292

commit v17 on v15

--- a/solution.py
+++ b/solution.py
@@ -49,7 +49,7 @@
         )
         remote = []
         order = [k for pair in zip(range(1, count), range(count - 1, 0, -1)) for k in pair]
-        for k in sorted(set(order), key=order.index):
+        for k in list(reversed(sorted(set(order), key=order.index))):
             peer = lax.rem(me + k, count)
             remote.append(pltpu.make_async_remote_copy(
                 src_ref=slot_ref.at[slot, pl.ds(peer * mz_local, mz_local)],

time: 124 us -> 124 us (level)
  no operation moved by 1% of the time
where the time goes in v17:
time: 124 us
  Pallas kernels  72.1 us (58%)
  local copies, waits for them, and re-layouts  20.7 us (17%)
  waiting for transfers between devices  11.7 us (9%)
  starting transfers between devices  10.8 us (9%)
  matrix products  4.98 us (4%)
  other arithmetic  2.84 us (2%)
    pallas_call x1, Pallas kernels, analysis(): pl.pallas_call(functools.partial(analysis_kernel, axis, count), grid=(ste...  36.4 us
    pallas_call x1, Pallas kernels, synthesis(): pl.pallas_call(functools.partial(synthesis_kernel, axis, count, other, ot...  30.7 us
    unnamed x8, local copies, waits for them, and re-layouts  11.1 us
    all_to_all x1, starting transfers between devices, per_device(): lax.all_to_all(ycoeffs, 'wide', split_axis=2, concat_axis=3, tiled=True)  7.21 us
    reshape x1, local copies, waits for them, and re-layouts, per_device(): zc = zc.reshape(n_narrow, mz_local, 2 * channels, nx, ny)  6.22 us
    all_to_all x1, waiting for transfers between devices, per_device(): lax.all_to_all(ycoeffs, 'wide', split_axis=2, concat_axis=3, tiled=True)  6.04 us
    all_to_all x1, waiting for transfers between devices, per_device(): lax.all_to_all(xsynth, 'wide', split_axis=3, concat_axis=2, tiled=True)  5.69 us
    pallas_call x1, Pallas kernels, modes_step(): pl.pallas_call(modes_kernel, in_specs=[vmem, vmem], out_specs=[vmem, vmem...  4.99 us
  transfers between devices with their start and end apart: 2, of which 2 were waited for; matrix products, arithmetic and copies ran while one was open for 2% of the time, Pallas kernels for 0%

profile of v17, /device:TPU:1, one launch (start us, length us, event | category | flops | bytes accessed | tf_op | source)
XLA Modules:
  0.0 123.8 jit_solution(2223496489496180502)
XLA Ops:
  0.7 0.8 multiply_convert_fusion.3.tz_ref
  1.5 36.4 %shard_map.67 = (bf16[16,2,64,512]{3,2,1,0:T(8,128)(2,1)}, f32[32,32]{1,0:T(8,128)}) custom-call(bf16[32,32,16,256]{3,2,1,0:T(8,128)(2,1)} %h_ref.3, bf16[32,32,16,256]{3,2,1,0:T(8,128)(2,1)} %g_ref.3, bf16[32,256]{1,0:T(8,128)(2,1)} %multiply_convert_fusion.3.tz_ref), custom_call_target="tpu_custom_call" | custom-call | tf_op jit(solution)/shard_map/pallas_call | solution.py:133
  37.9 6.2 %copy.29 = bf16[16,2,64,512]{2,0,3,1:T(8,128)(2,1)} copy(bf16[16,2,64,512]{3,2,1,0:T(8,128)(2,1)} %get-tuple-element.9) | data formatting | bytes 4194304 | tf_op jit(solution)/shard_map/reshape | solution.py:448
  44.1 3.6 %fusion.1 = bf16[2,64,32,32]{1,2,3,0:T(8,128)(2,1)S(1)} fusion(bf16[16,2,64,32,16]{2,0,4,3,1:T(8,128)(2,1)} %bitcast.48, s32[16,16]{0,1:T(8,128)S(1)} %multiply_add_fusion, s32[32]{0:T(128)S(1)} %add_select_fusion.5, pred[32]{0:T(512)(128)(4,1)S(1)} %iota_compare_fusion), kind=kOutput, calls=%fused_computation.2 | convolution fusion | flops 67379200 | bytes 2360480 | tf_op jit(solution)/shard_map/smcxl,nsl->mcnx/dot_general | solution.py:449
  47.7 0.2 copy.31
  47.9 1.1 reshape.89
  49.0 7.2 %all-to-all-start = ((bf16[8,2,8192]{2,1,0:T(2,128)(2,1)}), bf16[8,2,8192]{2,1,0:T(2,128)(2,1)S(1)}, u32[]{:S(2)}, u32[]{:S(2)}) async-start(bf16[8,2,8192]{2,1,0:T(2,128)(2,1)} %reshape.89), calls=%async_computation | async-start | bytes 524288 | tf_op jit(solution)/shard_map/all_to_all | solution.py:453
  56.2 0.1 iota.94
  56.3 1.2 multiply_convert_fusion.tyt_ref
  57.5 6.0 %all-to-all-done = bf16[8,2,8192]{2,1,0:T(2,128)(2,1)S(1)} async-done(((bf16[8,2,8192]{2,1,0:T(2,128)(2,1)}), bf16[8,2,8192]{2,1,0:T(2,128)(2,1)S(1)}, u32[]{:S(2)}, u32[]{:S(2)}) %all-to-all-start) | async-done | bytes 262176 | tf_op jit(solution)/shard_map/all_to_all | solution.py:453
  63.5 0.3 reshape.90
  63.9 1.0 fusion.35
  64.9 5.0 %shard_map.68 = (f32[256,1024]{1,0:T(8,128)}, bf16[256,32]{1,0:T(8,128)(2,1)}) custom-call(f32[256,64]{1,0:T(8,128)} %bitcast.55, bf16[256,1024]{1,0:T(8,128)(2,1)} %bitcast.56), custom_call_target="tpu_custom_call" | custom-call | tf_op jit(solution)/shard_map/pallas_call | solution.py:425
  69.9 0.9 copy.22
  70.9 0.4 convolution_convert_fusion
  71.2 0.3 copy.23
  71.6 1.2 reshape.91
  72.7 3.6 %all-to-all-start.1 = ((bf16[8,2,4096]{2,1,0:T(2,128)(2,1)}), bf16[8,2,4096]{2,1,0:T(2,128)(2,1)S(1)}, u32[]{:S(2)}, u32[]{:S(2)}) async-start(bf16[8,2,4096]{2,1,0:T(2,128)(2,1)} %reshape.91), calls=%async_computation.1 | async-start | bytes 262144 | tf_op jit(solution)/shard_map/all_to_all | solution.py:467
  76.3 0.8 multiply_convert_fusion.2.tz_ref
  77.1 5.7 %all-to-all-done.1 = bf16[8,2,4096]{2,1,0:T(2,128)(2,1)S(1)} async-done(((bf16[8,2,4096]{2,1,0:T(2,128)(2,1)}), bf16[8,2,4096]{2,1,0:T(2,128)(2,1)S(1)}, u32[]{:S(2)}, u32[]{:S(2)}) %all-to-all-start.1) | async-done | bytes 131104 | tf_op jit(solution)/shard_map/all_to_all | solution.py:467
  82.8 0.3 reshape.92
  83.1 1.7 %copy.24 = bf16[2,32,4,8,32]{4,2,3,1,0:T(4,128)(2,1)} copy(bf16[2,32,4,8,32]{1,2,0,4,3:T(4,128)(2,1)S(1)} %bitcast.52) | data formatting | bytes 262144 | tf_op jit(solution)/shard_map/all_to_all | solution.py:467
  84.8 30.7 %shard_map.69 = (bf16[32,32,16,256]{3,2,1,0:T(8,128)(2,1)}, f32[32,32]{1,0:T(8,128)}) custom-call(bf16[32,32,16,256]{3,2,1,0:T(8,128)(2,1)} %h_ref.3, bf16[32,32,16,256]{3,2,1,0:T(8,128)(2,1)} %g_ref.3, bf16[2,32,32,32]{3,2,1,0:T(8,128)(2,1)} %bitcast.49, bf16[256,32]{1,0:T(8,128)(2,1)} %multiply_convert_fusion.tyt_ref, ...), custom_call_target="tpu_custom_call" | custom-call | tf_op jit(solution)/shard_map/pallas_call | solution.py:339
  115.6 0.0 copy-start
  115.6 7.7 %copy.34 = bf16[32,32,16,256]{3,2,1,0:T(8,128)(2,1)} copy(bf16[32,32,16,256]{3,2,1,0:T(8,128)(2,1)} %get-tuple-element.18) | data formatting | bytes 16777216
  123.2 0.0 copy-done
  123.2 0.6 copy.35
  (7 shorter events, 0.1 us)
Async XLA Ops:
  49.0 14.5 %all-to-all-start = ((bf16[8,2,8192]{2,1,0:T(2,128)(2,1)}), bf16[8,2,8192]{2,1,0:T(2,128)(2,1)S(1)}, u32[]{:S(2)}, u32[]{:S(2)}) async-start(bf16[8,2,8192]{2,1,0:T(2,128)(2,1)} %reshape.89), calls=%async_computation | async-start | bytes 524288 | tf_op jit(solution)/shard_map/all_to_all | solution.py:453
  72.7 10.1 %all-to-all-start.1 = ((bf16[8,2,4096]{2,1,0:T(2,128)(2,1)}), bf16[8,2,4096]{2,1,0:T(2,128)(2,1)S(1)}, u32[]{:S(2)}, u32[]{:S(2)}) async-start(bf16[8,2,4096]{2,1,0:T(2,128)(2,1)} %reshape.91), calls=%async_computation.1 | async-start | bytes 262144 | tf_op jit(solution)/shard_map/all_to_all | solution.py:467
  115.6 7.7 %copy-start = (f32[32,32]{1,0:T(8,128)S(1)}, f32[32,32]{1,0:T(8,128)}, u32[]{:S(2)}) copy-start(f32[32,32]{1,0:T(8,128)} %get-tuple-element.20) | copy-start | bytes 12292

commit v18 on v15

--- a/solution.py
+++ b/solution.py
@@ -2,6 +2,8 @@
 import math
 
 import jax
+import ml_dtypes
+import numpy as np
 import jax.numpy as jnp
 from jax import lax
 from jax.experimental import pallas as pl
@@ -15,14 +17,15 @@
 
 
 def basis_table(mode_count, length):
-    mode_index = jnp.arange(mode_count, dtype=jnp.int32)
+    mode_index = np.arange(mode_count, dtype=np.int32)
     halfway = mode_count // 2
-    frequency = jnp.where(mode_index < halfway, mode_index, mode_index - halfway + 1)
-    points = jnp.arange(length, dtype=jnp.int32)
+    frequency = np.where(mode_index < halfway, mode_index, mode_index - halfway + 1)
+    points = np.arange(length, dtype=np.int32)
     phases = frequency[:, None] * points[None, :] % length
-    angles = phases.astype(jnp.float32) * (2.0 * math.pi / length)
-    values_table = jnp.where((mode_index < halfway)[:, None], jnp.cos(angles), jnp.sin(angles))
-    return (values_table * (1.0 / math.sqrt(length))).astype(jnp.bfloat16)
+    angles = phases.astype(np.float32) * np.float32(2.0 * math.pi / length)
+    values_table = np.where((mode_index < halfway)[:, None], np.cos(angles), np.sin(angles))
+    values_table = values_table.astype(np.float32) * np.float32(1.0 / math.sqrt(length))
+    return jnp.asarray(values_table.astype(ml_dtypes.bfloat16))
 
 
 def _nt(a, b):

time: 124 us -> 119 us (0.960)
  blocking collectives: 0 us -> 23.8 us
  waiting for transfers between devices: 11.9 us -> 0 us
  starting transfers between devices: 10.8 us -> 0 us
  other arithmetic: 2.84 us -> 0 us
  local copies, waits for them, and re-layouts: 20.7 us -> 18 us
    all_to_all x0 -> x2, blocking collectives: none -> 23.8 us  [the longest x1 14.4 us: per_device(): lax.all_to_all(ycoeffs, 'wide', split_axis=2, concat_axis=3, tiled=True)]
    all_to_all x2 -> x0, waiting for transfers between devices: 11.9 us -> none  [the longest x1 6.17 us: per_device(): lax.all_to_all(ycoeffs, 'wide', split_axis=2, concat_axis=3, tiled=True)]
    all_to_all x2 -> x0, starting transfers between devices: 10.8 us -> none  [the longest x1 7.21 us: per_device(): lax.all_to_all(ycoeffs, 'wide', split_axis=2, concat_axis=3, tiled=True)]
    reshape x1 -> x0, local copies, waits for them, and re-layouts: 6.22 us -> none  [per_device(): zc = zc.reshape(n_narrow, mz_local, 2 * channels, nx, ny)]
    pallas_call x0 -> x1, local copies, waits for them, and re-layouts: none -> 4.79 us  [analysis(): pl.pallas_call(functools.partial(analysis_kernel, axis, count), grid=(ste...]
    convert_element_type x3 -> x0, other arithmetic: 2.81 us -> none  [basis_table(): return (values_table * (1.0 / math.sqrt(length))).astype(jnp.bfloat16)]
    unnamed x8 -> x12, local copies, waits for them, and re-layouts: 11.1 us -> 9.77 us
  transfers between devices with their start and end apart: 2 -> 0, of which waited for: 2 -> 0; matrix products, arithmetic and copies ran while one was open for 2% -> 0% of each run, Pallas kernels for 0% -> 0%
where the time goes in v18:
time: 119 us
  Pallas kernels  72.4 us (61%)
  blocking collectives  23.8 us (20%)
  local copies, waits for them, and re-layouts  18 us (15%)
  matrix products  4.06 us (3%)
    pallas_call x1, Pallas kernels, analysis(): pl.pallas_call(functools.partial(analysis_kernel, axis, count), grid=(ste...  36.6 us
    pallas_call x1, Pallas kernels, synthesis(): pl.pallas_call(functools.partial(synthesis_kernel, axis, count, other, ot...  30.8 us
    all_to_all x1, blocking collectives, per_device(): lax.all_to_all(ycoeffs, 'wide', split_axis=2, concat_axis=3, tiled=True)  14.4 us
    unnamed x12, local copies, waits for them, and re-layouts  9.77 us
    all_to_all x1, blocking collectives, per_device(): lax.all_to_all(xsynth, 'wide', split_axis=3, concat_axis=2, tiled=True)  9.33 us
    pallas_call x1, Pallas kernels, modes_step(): pl.pallas_call(modes_kernel, in_specs=[vmem, vmem], out_specs=[vmem, vmem...  4.99 us
    pallas_call x1, local copies, waits for them, and re-layouts, analysis(): pl.pallas_call(functools.partial(analysis_kernel, axis, count), grid=(ste...  4.79 us
    dot_general x1, matrix products, per_device(): jnp.einsum('smcxl,nsl->mcnx', zc, table_y.reshape(mode_count, n_narrow, n...  3.05 us

profile of v18, /device:TPU:1, one launch (start us, length us, event | category | flops | bytes accessed | tf_op | source)
XLA Modules:
  0.0 118.9 jit_solution(17686213106333956260)
XLA Ops:
  0.6 36.6 %shard_map.94 = (bf16[16,2,64,512]{3,2,1,0:T(8,128)(2,1)}, f32[32,32]{1,0:T(8,128)}) custom-call(bf16[32,32,16,256]{3,2,1,0:T(8,128)(2,1)} %h_ref.3, bf16[32,32,16,256]{3,2,1,0:T(8,128)(2,1)} %g_ref.3, bf16[32,256]{1,0:T(8,128)(2,1)} %constant.2.clone.tz_ref), custom_call_target="tpu_custom_call" | custom-call | tf_op jit(solution)/shard_map/pallas_call | solution.py:136
  37.2 0.0 copy-start
  37.3 4.8 %copy.20 = bf16[16,2,64,512]{2,3,1,0:T(8,128)(2,1)} copy(bf16[16,2,64,512]{3,2,1,0:T(8,128)(2,1)} %get-tuple-element.9) | data formatting | bytes 4194304 | tf_op jit(solution)/shard_map/pallas_call | solution.py:136
  42.0 0.0 copy-done
  42.0 0.0 copy-start.1
  42.0 3.0 %fusion.2 = bf16[2,64,32,32,1]{1,3,2,0,4:T(8,128)(2,1)S(1)} fusion(bf16[16,2,64,32,16]{2,4,3,1,0:T(8,128)(2,1)} %bitcast.43, bf16[32,16,16,1,1]{0,2,4,3,1:T(8,128)(2,1)S(1)} %copy-done), kind=kOutput, calls=%fused_computation.5 | convolution fusion | flops 67108864 | bytes 2375680 | tf_op jit(solution)/shard_map/smcxl,nsl->mcnx/dot_general | solution.py:452
  45.1 0.1 copy.37
  45.2 0.3 copy.38
  45.5 0.4 reshape.41
  45.9 14.4 %all_to_all.36 = bf16[8,2,8192]{2,1,0:T(2,128)(2,1)S(1)} all-to-all(bf16[8,2,8192]{2,1,0:T(2,128)(2,1)S(1)} %reshape.41), channel_id=1, replica_groups=mesh['wide'=8,'narrow'=16] {'wide'}, dimensions={0} | all-to-all | bytes 524288 | tf_op jit(solution)/shard_map/all_to_all | solution.py:456
  60.3 0.3 reshape.42
  60.7 0.0 copy-done.1
  60.7 0.9 fusion.3
  61.6 5.0 %shard_map.95 = (f32[256,1024]{1,0:T(8,128)}, bf16[256,32]{1,0:T(8,128)(2,1)}) custom-call(f32[256,64]{1,0:T(8,128)} %bitcast.52, bf16[256,1024]{1,0:T(8,128)(2,1)} %bitcast.51), custom_call_target="tpu_custom_call" | custom-call | tf_op jit(solution)/shard_map/pallas_call | solution.py:428
  66.6 0.9 copy.25
  67.5 0.2 convolution_convert_fusion
  67.7 0.3 copy.26
  68.0 0.5 reshape.43
  68.5 9.3 %all_to_all.37 = bf16[8,2,4096]{2,1,0:T(2,128)(2,1)S(1)} all-to-all(bf16[8,2,4096]{2,1,0:T(2,128)(2,1)S(1)} %reshape.43), channel_id=1, replica_groups=mesh['wide'=8,'narrow'=16] {'wide'}, dimensions={0} | all-to-all | bytes 262144 | tf_op jit(solution)/shard_map/all_to_all | solution.py:470
  77.9 0.3 reshape.44
  78.1 1.7 %copy.27 = bf16[2,32,4,8,32]{4,2,3,1,0:T(4,128)(2,1)} copy(bf16[2,32,4,8,32]{1,2,0,4,3:T(4,128)(2,1)S(1)} %bitcast.46) | data formatting | bytes 262144 | tf_op jit(solution)/shard_map/all_to_all | solution.py:470
  79.9 30.8 %shard_map.96 = (bf16[32,32,16,256]{3,2,1,0:T(8,128)(2,1)}, f32[32,32]{1,0:T(8,128)}) custom-call(bf16[32,32,16,256]{3,2,1,0:T(8,128)(2,1)} %h_ref.3, bf16[32,32,16,256]{3,2,1,0:T(8,128)(2,1)} %g_ref.3, bf16[2,32,32,32]{3,2,1,0:T(8,128)(2,1)} %bitcast.44, bf16[256,32]{1,0:T(8,128)(2,1)} %constant.5.tyt_ref, bf16[32,256]{1,0:T(8,128)(2,1)} %constant.8.tz_ref, ...), custom_call_target="tpu_custom_call" | custom-call | tf_op jit(solution)/shard_map/pallas_call | solution.py:342
  110.7 0.0 copy-start.2
  110.7 7.7 %copy.41 = bf16[32,32,16,256]{3,2,1,0:T(8,128)(2,1)} copy(bf16[32,32,16,256]{3,2,1,0:T(8,128)(2,1)} %get-tuple-element.18) | data formatting | bytes 16777216
  118.3 0.0 copy-done.2
  118.3 0.6 copy.42
  (1 shorter events, 0.0 us)
Async XLA Ops:
  37.2 4.8 %copy-start = (bf16[32,16,16,1,1]{0,2,4,3,1:T(8,128)(2,1)S(1)}, bf16[32,16,16,1,1]{0,2,4,3,1:T(8,128)(2,1)}, u32[]{:S(2)}) copy-start(bf16[32,16,16,1,1]{0,2,4,3,1:T(8,128)(2,1)} %constant.9) | copy-start | bytes 49156
  42.0 18.7 %copy-start.1 = (bf16[32,256,1,1]{1,0,3,2:T(8,128)(2,1)S(1)}, bf16[32,256,1,1]{1,0,3,2:T(8,128)(2,1)}, u32[]{:S(2)}) copy-start(bf16[32,256,1,1]{1,0,3,2:T(8,128)(2,1)} %constant.10) | copy-start | bytes 49156
  110.7 7.7 %copy-start.2 = (f32[32,32]{1,0:T(8,128)S(1)}, f32[32,32]{1,0:T(8,128)}, u32[]{:S(2)}) copy-start(f32[32,32]{1,0:T(8,128)} %get-tuple-element.20) | copy-start | bytes 12292
